TPU v7x, 512 devices: a whole 4x4x16 slice. The times are simulated.
512 devices in a mesh: gx: 64 (over z, x_lo, core), gy: 8 (over y, x_hi).
Axes of the slice: x: 4 (x_hi: 2, x_lo: 2; x = x_hi * 2 + x_lo), y: 4, z: 16, core: 2. Of those that a mesh axis runs over, the one named last changes fastest.
Arguments:
- positions: float32 [3, 262144], P(None, ('gx', 'gy')), may hold values from 0 to 1
- velocities: float32 [3, 262144], P(None, ('gx', 'gy')), may hold values from -4 to 4
- forces: float32 [3, 262144], P(None, ('gx', 'gy')), may hold values from -6 to 6
- neighbours: int32 [1, 32, 262144], P(None, None, ('gx', 'gy')), may hold values from -1 to 1151, as said below
- ghost_x: int32 [1, 2, 65536], P(None, None, ('gx', 'gy')), may hold values from 0 to 511, as said below
- ghost_y: int32 [1, 2, 98304], P(None, None, ('gx', 'gy')), may hold values from 0 to 767, as said below
- migrate_x: int32 [1, 2, 4096], P(None, None, ('gx', 'gy')), may hold values from 0 to 511, as said below
- migrate_y: int32 [1, 2, 4096], P(None, None, ('gx', 'gy')), may hold values from 0 to 511, as said below
- w_basis: float32 [64, 8], replicated, may hold values from -2 to 2
- b_basis: float32 [64], replicated, may hold values from -3 to 3
- w_embed: float32 [32, 64], replicated, may hold values from -0.75 to 0.75
- w_pair: float32 [64, 64], replicated, may hold values from -0.75 to 0.75
- w_mix: float32 [64, 32], replicated, may hold values from -1 to 1
- b_pair: float32 [64], replicated, may hold values from -3 to 3
- w_out: float32 [64], replicated, may hold values from -0.75 to 0.75
Outputs:
- positions_out: float32 [3, 262144], P(None, ('gx', 'gy'))
- velocities_out: float32 [3, 262144], P(None, ('gx', 'gy'))
- forces_out: float32 [3, 262144], P(None, ('gx', 'gy'))
Inputs may be any that keep to these rules, and one draw needn't show every extreme that they name: `neighbours`: entries index the step's extended columns of the bin (own slots, then 128 ghosts from the lower and 128 from the upper gx neighbour, then 192 from the lower and 192 from the upper gy neighbour); -1 marks an empty slot. In every bin the atoms with a non-empty list (live atoms) fill the first whole blocks of 128 slots, at least 3 blocks, and all 4 in some bin; other atoms have only -1 and no list names them. Every list names ghosts or live atoms only. `ghost_x`: for each step and each of the two rows, 128 distinct live slots of the bin. `ghost_y`: for each step and each of the two rows, 192 distinct columns of the bin's own live atoms and gx ghosts. `migrate_x`: for each step the 16 slots of a bin are distinct and live. `migrate_y`: for each step the 16 slots of a bin are distinct and live.
All inputs are finite; a program needn't handle non-finite values.
Results may differ from a plain program's by a relative error of at most 0.0003.
Values sent between devices are 32-bit elements; how exact they have to be, the bound alone decides.
No kernel may reach another device: no remote copies, remote signals or barrier semaphores. Data moves between devices by JAX's collectives and lax.ppermute only.
A program may use at most 64 MiB of HBM per device.

v0:
```python
import math

import jax
import jax.numpy as jnp
from jax import lax
from jax.sharding import PartitionSpec as P

NB = 8
NEI = 32
BLOCK = 128


TIME_STEP = 0.05
CENTRE_SPAN = 3.0
HIGHEST = lax.Precision.HIGHEST


def shifted(block, axis, distance):
    devices = range(lax.axis_size(axis))
    route = [((i - distance) % len(devices), i) for i in devices]
    return lax.ppermute(block, axis, route)


def matmul(left, right):
    return jnp.dot(left, right, precision=HIGHEST, preferred_element_type=jnp.float32)


def pair_latent(ext_pos, own_pos, nearby, w_basis, b_basis):
    present = nearby >= 0
    safe_index = jnp.where(present, nearby, 0)
    separation = ext_pos[:, safe_index] - own_pos[:, None, :]
    square = jnp.sum(separation * separation, axis=0)
    weight = jnp.where(present, 1.0 / (1.0 + square), 0.0)
    centres = jnp.arange(NB, dtype=jnp.float32) * (CENTRE_SPAN / (NB - 1))
    radial = jnp.exp(-((square[None] - centres[:, None, None]) ** 2))
    latent = jax.nn.silu(matmul(w_basis, radial.reshape(NB, -1)) + b_basis[:, None])
    return (latent * weight.reshape(1, -1), weight, safe_index)


def pair_env(ext_pos, own_pos, nearby, w_basis, b_basis):
    latent, weight, safe_index = pair_latent(ext_pos, own_pos, nearby, w_basis, b_basis)
    summed = latent.reshape(latent.shape[0], nearby.shape[0], nearby.shape[1]).sum(axis=1)
    return summed * (1.0 / math.sqrt(NEI))


def pair_energy(ext_pos, own_pos, nearby, embed_ext, embed_own, weights):
    w_basis, b_basis, w_pair, w_mix, b_pair, w_out = weights
    latent, weight, safe_index = pair_latent(ext_pos, own_pos, nearby, w_basis, b_basis)
    partner = embed_ext[:, safe_index]
    product = (partner * embed_own[:, None, :]).reshape(embed_own.shape[0], -1)
    hidden = jax.nn.silu(matmul(w_pair, latent) + matmul(w_mix, product) + b_pair[:, None])
    return jnp.sum(matmul(w_out, hidden) * weight.reshape(-1))


def cross_long(upward, downward):
    return (shifted(upward, "gx", 1), shifted(downward, "gx", -1))


def cross_narrow(upward, downward):
    return (shifted(upward, "gy", 1), shifted(downward, "gy", -1))


def migrate(bundle, slot_lists, offset, crossing):
    upward = bundle[:, slot_lists[0]] - offset
    downward = bundle[:, slot_lists[1]] + offset
    from_lower, from_upper = crossing(upward, downward)
    return bundle.at[:, slot_lists[1]].set(from_lower).at[:, slot_lists[0]].set(from_upper)


def extend(values, list_long, list_narrow, offset_long, offset_narrow):
    from_lower, from_upper = cross_long(
        values[:, list_long[0]] - offset_long, values[:, list_long[1]] + offset_long
    )
    partial_value = jnp.concatenate([values, from_lower, from_upper], axis=1)
    from_lower, from_upper = cross_narrow(
        partial_value[:, list_narrow[0]] - offset_narrow,
        partial_value[:, list_narrow[1]] + offset_narrow,
    )
    return jnp.concatenate([partial_value, from_lower, from_upper], axis=1)


def fold_back(cotangent, list_long, list_narrow, own_count):
    depth_long = list_long.shape[1]
    depth_narrow = list_narrow.shape[1]
    inner_end = own_count + 2 * depth_long
    lower_rows = cotangent[:, inner_end : inner_end + depth_narrow]
    upper_rows = cotangent[:, inner_end + depth_narrow :]
    sent_down, sent_up = cross_narrow(upper_rows, lower_rows)
    partial_value = (
        cotangent[:, :inner_end]
        .at[:, list_narrow[1]]
        .add(sent_down)
        .at[:, list_narrow[0]]
        .add(sent_up)
    )
    lower_rows = partial_value[:, own_count : own_count + depth_long]
    upper_rows = partial_value[:, own_count + depth_long :]
    sent_down, sent_up = cross_long(upper_rows, lower_rows)
    return (
        partial_value[:, :own_count]
        .at[:, list_long[1]]
        .add(sent_down)
        .at[:, list_long[0]]
        .add(sent_up)
    )


def force_field(coords, nearby, list_long, list_narrow, weights, block_count):
    w_basis, b_basis, w_embed, w_pair, w_mix, b_pair, w_out = weights
    pair_weights = (w_basis, b_basis, w_pair, w_mix, b_pair, w_out)
    own_count = coords.shape[1]
    zero_column = jnp.zeros((3, 1), jnp.float32)
    extended = extend(
        coords, list_long, list_narrow, zero_column.at[0, 0].set(1.0), zero_column.at[1, 0].set(1.0)
    )

    def env_turn(number, collected):
        first_row = number * BLOCK
        near_block = lax.dynamic_slice_in_dim(nearby, first_row, BLOCK, 1)
        own_block = lax.dynamic_slice_in_dim(extended, first_row, BLOCK, 1)
        env_block = pair_env(extended, own_block, near_block, w_basis, b_basis)
        return lax.dynamic_update_slice_in_dim(collected, env_block, first_row, 1)

    surround = lax.fori_loop(
        0, block_count, env_turn, jnp.zeros((w_basis.shape[0], own_count), jnp.float32)
    )
    embed_ext = matmul(w_embed, extend(surround, list_long, list_narrow, 0.0, 0.0))

    def energy_turn(number, running):
        first_row = number * BLOCK
        near_block = lax.dynamic_slice_in_dim(nearby, first_row, BLOCK, 1)

        def block_energy(ext_input, embed_input):
            own_input = lax.dynamic_slice_in_dim(ext_input, first_row, BLOCK, 1)
            embed_own = lax.dynamic_slice_in_dim(embed_input, first_row, BLOCK, 1)
            return pair_energy(
                ext_input, own_input, near_block, embed_input, embed_own, pair_weights
            )

        energy_value, pullback = jax.vjp(block_energy, extended, embed_ext)
        grad_pos, grad_embed = pullback(jnp.ones_like(energy_value))
        return (running[0] + grad_pos, running[1] + grad_embed)

    grad_ext, grad_embed = lax.fori_loop(
        0, block_count, energy_turn, (jnp.zeros_like(extended), jnp.zeros_like(embed_ext))
    )
    grad_env = fold_back(matmul(w_embed.T, grad_embed), list_long, list_narrow, own_count)

    def env_back_turn(number, running):
        first_row = number * BLOCK
        near_block = lax.dynamic_slice_in_dim(nearby, first_row, BLOCK, 1)
        cot_block = lax.dynamic_slice_in_dim(grad_env, first_row, BLOCK, 1)

        def block_env(ext_input):
            own_input = lax.dynamic_slice_in_dim(ext_input, first_row, BLOCK, 1)
            return pair_env(ext_input, own_input, near_block, w_basis, b_basis)

        env_value, pullback = jax.vjp(block_env, extended)
        return running + pullback(cot_block)[0]

    grad_ext = lax.fori_loop(0, block_count, env_back_turn, grad_ext)
    return -fold_back(grad_ext, list_long, list_narrow, own_count)


def on_device(
    positions,
    velocities,
    forces,
    neighbours,
    ghost_x,
    ghost_y,
    migrate_x,
    migrate_y,
    w_basis,
    b_basis,
    w_embed,
    w_pair,
    w_mix,
    b_pair,
    w_out,
):
    weights = (w_basis, b_basis, w_embed, w_pair, w_mix, b_pair, w_out)
    coords = positions
    speeds = velocities
    pushes = forces
    total_blocks = positions.shape[1] // BLOCK
    bundle_shift = jnp.zeros((6, 1), jnp.float32)
    speeds = speeds + 0.5 * TIME_STEP * pushes
    coords = coords + TIME_STEP * speeds
    bundle = jnp.concatenate([coords, speeds], axis=0)
    bundle = migrate(bundle, migrate_x[0], bundle_shift.at[0, 0].set(1.0), cross_long)
    bundle = migrate(bundle, migrate_y[0], bundle_shift.at[1, 0].set(1.0), cross_narrow)
    coords = bundle[:3]
    speeds = bundle[3:]
    nearby = neighbours[0]
    pushes = force_field(coords, nearby, ghost_x[0], ghost_y[0], weights, total_blocks)
    speeds = speeds + 0.5 * TIME_STEP * pushes
    return (coords, speeds, pushes)


def solution(mesh):
    placed = (
        P(None, ("gx", "gy")),
        P(None, ("gx", "gy")),
        P(None, ("gx", "gy")),
        P(None, None, ("gx", "gy")),
        P(None, None, ("gx", "gy")),
        P(None, None, ("gx", "gy")),
        P(None, None, ("gx", "gy")),
        P(None, None, ("gx", "gy")),
        P(),
        P(),
        P(),
        P(),
        P(),
        P(),
        P(),
    )
    return jax.shard_map(
        on_device,
        mesh=mesh,
        in_specs=placed,
        out_specs=(P(None, ("gx", "gy")), P(None, ("gx", "gy")), P(None, ("gx", "gy"))),
        check_vma=False,
    )
```

profile of v0, /device:TPU:1, one launch (start us, length us, event | category | flops | bytes accessed | tf_op | source)
XLA Modules:
  0.0 762.7 jit_solution(1294008661717437517)
XLA Ops:
  3.6 4.5 collective-permute-start
  9.3 6.2 collective-permute-start.1
  23.7 7.0 collective-permute-start.3
  36.4 8.3 %collective-permute-start.5 = (f32[3,128]{0,1:T(8,128)S(1)}, f32[3,128]{0,1:T(8,128)S(1)}, u32[]{:S(2)}, u32[]{:S(2)}) collective-permute-start(f32[3,128]{0,1:T(8,128)S(1)} %add_bitcast_fusion.2), channel_id=1, source_target_pairs={{8,0},{16,8},{24,16},{32,24},{40,32},{48,40},{56,48},{64,56},{72,6... | collective-permute-start | bytes 4616 | tf_op jit(solution)/shard_map/ppermute | solution.py:21
  46.3 4.4 collective-permute-start.6
  51.4 4.5 collective-permute-start.7
  59.0 52.3 %while.46 = (s32[]{:T(128)}, f32[64,512]{1,0:T(8,128)S(1)}, s32[32,512]{1,0:T(8,128)S(1)}, f32[3,1152]{0,1:T(8,128)S(1)}, f32[64,8]{0,1:T(8,128)S(1)}, /*index=5...) while((s32[]{:T(128)}, f32[64,512]{1,0:T(8,128)S(1)}, ...), condition=%wide.region_7.0_spmd, body=%wide.region_4.7_spmd.sunk | while | flops 27172880 | bytes 4594700 | solution.py:124
  59.0 10.8 %gather_fusion = f32[4096,3]{1,0:T(8,128)S(1)} fusion(f32[3,1152]{0,1:T(8,128)S(1)} %get-tuple-element.947, s32[4096]{0:T(1024)S(1)} %fusion.164), kind=kCustom, calls=%fused_computation.clone.1 | custom fusion | bytes 114688 | tf_op jit(solution)/shard_map/while/body/eval_jaxpr/gather | solution.py:31
  72.1 10.8 %gather_fusion = f32[4096,3]{1,0:T(8,128)S(1)} fusion(f32[3,1152]{0,1:T(8,128)S(1)} %get-tuple-element.947, s32[4096]{0:T(1024)S(1)} %fusion.164), kind=kCustom, calls=%fused_computation.clone.1 | custom fusion | bytes 114688 | tf_op jit(solution)/shard_map/while/body/eval_jaxpr/gather | solution.py:31
  85.2 10.8 %gather_fusion = f32[4096,3]{1,0:T(8,128)S(1)} fusion(f32[3,1152]{0,1:T(8,128)S(1)} %get-tuple-element.947, s32[4096]{0:T(1024)S(1)} %fusion.164), kind=kCustom, calls=%fused_computation.clone.1 | custom fusion | bytes 114688 | tf_op jit(solution)/shard_map/while/body/eval_jaxpr/gather | solution.py:31
  98.3 10.8 %gather_fusion = f32[4096,3]{1,0:T(8,128)S(1)} fusion(f32[3,1152]{0,1:T(8,128)S(1)} %get-tuple-element.947, s32[4096]{0:T(1024)S(1)} %fusion.164), kind=kCustom, calls=%fused_computation.clone.1 | custom fusion | bytes 114688 | tf_op jit(solution)/shard_map/while/body/eval_jaxpr/gather | solution.py:31
  114.7 8.1 %collective-permute-start.9 = (f32[64,128]{0,1:T(8,128)S(1)}, f32[64,128]{0,1:T(8,128)S(1)}, u32[]{:S(2)}, u32[]{:S(2)}) collective-permute-start(f32[64,128]{0,1:T(8,128)S(1)} %bitcast.356), channel_id=1, source_target_pairs={{8,0},{16,8},{24,16},{32,24},{40,32},{48,40},{56,48},{64,56},{72,6... | collective-permute-start | bytes 98312 | tf_op jit(solution)/shard_map/ppermute | solution.py:21
  125.1 4.3 collective-permute-start.10
  129.5 4.6 collective-permute-start.11
  137.1 375.9 %while.48 = (s32[]{:T(128)}, f32[3,1152]{0,1:T(8,128)}, f32[32,1152]{0,1:T(8,128)}, s32[32,512]{1,0:T(8,128)S(1)}, f32[3,1152]{0,1:T(8,128)S(1)}, /*index=5*/f32...) while((s32[]{:T(128)}, f32[3,1152]{0,1:T(8,128)}, ...), condition=%wide.region_16.17_spmd.clone, body=%wide.region_8.16_spmd.clone.sunk | while | flops 671292544 | bytes 36430220 | solution.py:144
  137.4 10.8 %gather_fusion.2 = f32[4096,3]{1,0:T(8,128)S(1)} fusion(f32[3,1152]{0,1:T(8,128)S(1)} %get-tuple-element.995, s32[4096]{0:T(1024)S(1)} %get-tuple-element.917), kind=kCustom, calls=%fused_computation.1.clone.clone.1 | custom fusion | bytes 114688 | tf_op jit(solution)/shard_map/while/body/eval_jaxpr/jvp()/gather | solution.py:31
  152.2 14.1 %gather_fusion.3 = f32[4096,32]{1,0:T(8,128)} fusion(f32[32,1152]{0,1:T(8,128)S(1)} %get-tuple-element.1000, s32[4096]{0:T(1024)S(1)} %get-tuple-element.917), kind=kCustom, calls=%fused_computation.2.clone.clone.1 | custom fusion | bytes 1064960 | tf_op jit(solution)/shard_map/while/body/eval_jaxpr/jvp()/gather | solution.py:49
  177.6 22.9 %scatter_custom_fusion.40 = f32[3,1152]{0,1:T(8,128)S(1)} fusion(s32[4096]{0:T(1024)S(1)} %get-tuple-element.915, f32[4096,3]{1,0:T(8,128)} %bitcast.337, f32[]{:T(128)} %constant.346.clone.1..sunk.1), kind=kCustom, calls=%fused_computation.141.clone.1 | custom fusion | flops 12288 | bytes 14336 | tf_op jit(solution)/shard_map/while/body/eval_jaxpr/transpose(jvp())/scatter-add | solution.py:31
  207.3 22.8 %scatter_custom_fusion.41 = f32[32,1152]{0,1:T(8,128)S(1)} fusion(s32[4096]{0:T(1024)S(1)} %get-tuple-element.915, f32[4096,32]{1,0:T(8,128)} %bitcast.341, f32[]{:T(128)} %constant.346.clone.1..sunk.1), kind=kCustom, calls=%fused_computation.139.clone.1 | custom fusion | flops 131072 | bytes 147968 | tf_op jit(solution)/shard_map/while/body/eval_jaxpr/transpose(jvp())/scatter-add | solution.py:49
  231.3 10.8 %gather_fusion.2 = f32[4096,3]{1,0:T(8,128)S(1)} fusion(f32[3,1152]{0,1:T(8,128)S(1)} %get-tuple-element.995, s32[4096]{0:T(1024)S(1)} %get-tuple-element.917), kind=kCustom, calls=%fused_computation.1.clone.clone.1 | custom fusion | bytes 114688 | tf_op jit(solution)/shard_map/while/body/eval_jaxpr/jvp()/gather | solution.py:31
  246.1 14.1 %gather_fusion.3 = f32[4096,32]{1,0:T(8,128)} fusion(f32[32,1152]{0,1:T(8,128)S(1)} %get-tuple-element.1000, s32[4096]{0:T(1024)S(1)} %get-tuple-element.917), kind=kCustom, calls=%fused_computation.2.clone.clone.1 | custom fusion | bytes 1064960 | tf_op jit(solution)/shard_map/while/body/eval_jaxpr/jvp()/gather | solution.py:49
  271.5 22.9 %scatter_custom_fusion.40 = f32[3,1152]{0,1:T(8,128)S(1)} fusion(s32[4096]{0:T(1024)S(1)} %get-tuple-element.915, f32[4096,3]{1,0:T(8,128)} %bitcast.337, f32[]{:T(128)} %constant.346.clone.1..sunk.1), kind=kCustom, calls=%fused_computation.141.clone.1 | custom fusion | flops 12288 | bytes 14336 | tf_op jit(solution)/shard_map/while/body/eval_jaxpr/transpose(jvp())/scatter-add | solution.py:31
  301.2 22.8 %scatter_custom_fusion.41 = f32[32,1152]{0,1:T(8,128)S(1)} fusion(s32[4096]{0:T(1024)S(1)} %get-tuple-element.915, f32[4096,32]{1,0:T(8,128)} %bitcast.341, f32[]{:T(128)} %constant.346.clone.1..sunk.1), kind=kCustom, calls=%fused_computation.139.clone.1 | custom fusion | flops 131072 | bytes 147968 | tf_op jit(solution)/shard_map/while/body/eval_jaxpr/transpose(jvp())/scatter-add | solution.py:49
  325.2 10.8 %gather_fusion.2 = f32[4096,3]{1,0:T(8,128)S(1)} fusion(f32[3,1152]{0,1:T(8,128)S(1)} %get-tuple-element.995, s32[4096]{0:T(1024)S(1)} %get-tuple-element.917), kind=kCustom, calls=%fused_computation.1.clone.clone.1 | custom fusion | bytes 114688 | tf_op jit(solution)/shard_map/while/body/eval_jaxpr/jvp()/gather | solution.py:31
  340.0 14.1 %gather_fusion.3 = f32[4096,32]{1,0:T(8,128)} fusion(f32[32,1152]{0,1:T(8,128)S(1)} %get-tuple-element.1000, s32[4096]{0:T(1024)S(1)} %get-tuple-element.917), kind=kCustom, calls=%fused_computation.2.clone.clone.1 | custom fusion | bytes 1064960 | tf_op jit(solution)/shard_map/while/body/eval_jaxpr/jvp()/gather | solution.py:49
  356.6 2.6 fusion.190
  365.4 22.9 %scatter_custom_fusion.40 = f32[3,1152]{0,1:T(8,128)S(1)} fusion(s32[4096]{0:T(1024)S(1)} %get-tuple-element.915, f32[4096,3]{1,0:T(8,128)} %bitcast.337, f32[]{:T(128)} %constant.346.clone.1..sunk.1), kind=kCustom, calls=%fused_computation.141.clone.1 | custom fusion | flops 12288 | bytes 14336 | tf_op jit(solution)/shard_map/while/body/eval_jaxpr/transpose(jvp())/scatter-add | solution.py:31
  395.1 22.8 %scatter_custom_fusion.41 = f32[32,1152]{0,1:T(8,128)S(1)} fusion(s32[4096]{0:T(1024)S(1)} %get-tuple-element.915, f32[4096,32]{1,0:T(8,128)} %bitcast.341, f32[]{:T(128)} %constant.346.clone.1..sunk.1), kind=kCustom, calls=%fused_computation.139.clone.1 | custom fusion | flops 131072 | bytes 147968 | tf_op jit(solution)/shard_map/while/body/eval_jaxpr/transpose(jvp())/scatter-add | solution.py:49
  419.1 10.8 %gather_fusion.2 = f32[4096,3]{1,0:T(8,128)S(1)} fusion(f32[3,1152]{0,1:T(8,128)S(1)} %get-tuple-element.995, s32[4096]{0:T(1024)S(1)} %get-tuple-element.917), kind=kCustom, calls=%fused_computation.1.clone.clone.1 | custom fusion | bytes 114688 | tf_op jit(solution)/shard_map/while/body/eval_jaxpr/jvp()/gather | solution.py:31
  433.9 14.1 %gather_fusion.3 = f32[4096,32]{1,0:T(8,128)} fusion(f32[32,1152]{0,1:T(8,128)S(1)} %get-tuple-element.1000, s32[4096]{0:T(1024)S(1)} %get-tuple-element.917), kind=kCustom, calls=%fused_computation.2.clone.clone.1 | custom fusion | bytes 1064960 | tf_op jit(solution)/shard_map/while/body/eval_jaxpr/jvp()/gather | solution.py:49
  459.3 22.9 %scatter_custom_fusion.40 = f32[3,1152]{0,1:T(8,128)S(1)} fusion(s32[4096]{0:T(1024)S(1)} %get-tuple-element.915, f32[4096,3]{1,0:T(8,128)} %bitcast.337, f32[]{:T(128)} %constant.346.clone.1..sunk.1), kind=kCustom, calls=%fused_computation.141.clone.1 | custom fusion | flops 12288 | bytes 14336 | tf_op jit(solution)/shard_map/while/body/eval_jaxpr/transpose(jvp())/scatter-add | solution.py:31
  489.0 22.8 %scatter_custom_fusion.41 = f32[32,1152]{0,1:T(8,128)S(1)} fusion(s32[4096]{0:T(1024)S(1)} %get-tuple-element.915, f32[4096,32]{1,0:T(8,128)} %bitcast.341, f32[]{:T(128)} %constant.346.clone.1..sunk.1), kind=kCustom, calls=%fused_computation.139.clone.1 | custom fusion | flops 131072 | bytes 147968 | tf_op jit(solution)/shard_map/while/body/eval_jaxpr/transpose(jvp())/scatter-add | solution.py:49
  514.9 17.3 %collective-permute-start.12 = (f32[64,192]{1,0:T(8,128)S(1)}, f32[64,192]{1,0:T(8,128)S(1)}, u32[]{:S(2)}, u32[]{:S(2)}) collective-permute-start(f32[64,192]{1,0:T(8,128)S(1)} %get-tuple-element.728), channel_id=1, source_target_pairs={{7,0},{0,1},{1,2},{2,3},{3,4},{4,5},{5,6},{6,7},{15,8},{8,9},{9,10... | collective-permute-start | bytes 147464 | tf_op jit(solution)/shard_map/ppermute | solution.py:21
  534.5 4.3 collective-permute-done.13
  544.3 8.7 %collective-permute-start.15 = (f32[64,128]{0,1:T(8,128)S(1)}, f32[64,128]{0,1:T(8,128)S(1)}, u32[]{:S(2)}, u32[]{:S(2)}) collective-permute-start(f32[64,128]{0,1:T(8,128)S(1)} %get-tuple-element.725), channel_id=1, source_target_pairs={{8,0},{16,8},{24,16},{32,24},{40,32},{48,40},{56,48},{64,56},{72,6... | collective-permute-start | bytes 98312 | tf_op jit(solution)/shard_map/ppermute | solution.py:21
  556.6 173.8 %while.47 = (s32[]{:T(128)}, f32[3,1152]{0,1:T(8,128)S(1)}, s32[32,512]{1,0:T(8,128)S(1)}, f32[3,1152]{0,1:T(8,128)S(1)}, f32[64,512]{1,0:T(8,128)}, /*index=5*/...) while((s32[]{:T(128)}, f32[3,1152]{0,1:T(8,128)S(1)}, ...), condition=%wide.region_27.28_spmd, body=%wide.region_21.27_spmd.sunk | while | flops 55312144 | bytes 10386012 | solution.py:161
  558.5 10.8 %gather_fusion.1 = f32[4096,3]{1,0:T(8,128)S(1)} fusion(f32[3,1152]{0,1:T(8,128)S(1)} %get-tuple-element.1038, s32[4096]{0:T(1024)S(1)} %get-tuple-element.900), kind=kCustom, calls=%fused_computation.3.clone.1 | custom fusion | bytes 114688 | tf_op jit(solution)/shard_map/while/body/eval_jaxpr/jvp()/gather | solution.py:31
  575.3 22.8 %scatter_custom_fusion.37 = f32[3,1152]{0,1:T(8,128)S(1)} fusion(s32[4096]{0:T(1024)S(1)} %get-tuple-element.898, f32[4096,3]{1,0:T(8,128)} %bitcast.336, f32[]{:T(128)} %constant.346.clone.1..sunk), kind=kCustom, calls=%fused_computation.72.clone.1 | custom fusion | flops 12288 | bytes 14336 | tf_op jit(solution)/shard_map/while/body/eval_jaxpr/transpose(jvp())/scatter-add | solution.py:31
  601.9 10.8 %gather_fusion.1 = f32[4096,3]{1,0:T(8,128)S(1)} fusion(f32[3,1152]{0,1:T(8,128)S(1)} %get-tuple-element.1038, s32[4096]{0:T(1024)S(1)} %get-tuple-element.900), kind=kCustom, calls=%fused_computation.3.clone.1 | custom fusion | bytes 114688 | tf_op jit(solution)/shard_map/while/body/eval_jaxpr/jvp()/gather | solution.py:31
  618.8 22.8 %scatter_custom_fusion.37 = f32[3,1152]{0,1:T(8,128)S(1)} fusion(s32[4096]{0:T(1024)S(1)} %get-tuple-element.898, f32[4096,3]{1,0:T(8,128)} %bitcast.336, f32[]{:T(128)} %constant.346.clone.1..sunk), kind=kCustom, calls=%fused_computation.72.clone.1 | custom fusion | flops 12288 | bytes 14336 | tf_op jit(solution)/shard_map/while/body/eval_jaxpr/transpose(jvp())/scatter-add | solution.py:31
  645.4 10.8 %gather_fusion.1 = f32[4096,3]{1,0:T(8,128)S(1)} fusion(f32[3,1152]{0,1:T(8,128)S(1)} %get-tuple-element.1038, s32[4096]{0:T(1024)S(1)} %get-tuple-element.900), kind=kCustom, calls=%fused_computation.3.clone.1 | custom fusion | bytes 114688 | tf_op jit(solution)/shard_map/while/body/eval_jaxpr/jvp()/gather | solution.py:31
  662.2 22.8 %scatter_custom_fusion.37 = f32[3,1152]{0,1:T(8,128)S(1)} fusion(s32[4096]{0:T(1024)S(1)} %get-tuple-element.898, f32[4096,3]{1,0:T(8,128)} %bitcast.336, f32[]{:T(128)} %constant.346.clone.1..sunk), kind=kCustom, calls=%fused_computation.72.clone.1 | custom fusion | flops 12288 | bytes 14336 | tf_op jit(solution)/shard_map/while/body/eval_jaxpr/transpose(jvp())/scatter-add | solution.py:31
  688.8 10.8 %gather_fusion.1 = f32[4096,3]{1,0:T(8,128)S(1)} fusion(f32[3,1152]{0,1:T(8,128)S(1)} %get-tuple-element.1038, s32[4096]{0:T(1024)S(1)} %get-tuple-element.900), kind=kCustom, calls=%fused_computation.3.clone.1 | custom fusion | bytes 114688 | tf_op jit(solution)/shard_map/while/body/eval_jaxpr/jvp()/gather | solution.py:31
  705.6 22.8 %scatter_custom_fusion.37 = f32[3,1152]{0,1:T(8,128)S(1)} fusion(s32[4096]{0:T(1024)S(1)} %get-tuple-element.898, f32[4096,3]{1,0:T(8,128)} %bitcast.336, f32[]{:T(128)} %constant.346.clone.1..sunk), kind=kCustom, calls=%fused_computation.72.clone.1 | custom fusion | flops 12288 | bytes 14336 | tf_op jit(solution)/shard_map/while/body/eval_jaxpr/transpose(jvp())/scatter-add | solution.py:31
  730.4 6.3 collective-permute-start.16
  736.7 3.4 collective-permute-start.17
  742.0 3.7 collective-permute-done.17
  749.7 9.4 %collective-permute-start.19 = (f32[3,128]{0,1:T(8,128)S(1)}, f32[3,128]{0,1:T(8,128)S(1)}, u32[]{:S(2)}, u32[]{:S(2)}) collective-permute-start(f32[3,128]{0,1:T(8,128)S(1)} %get-tuple-element.723), channel_id=1, source_target_pairs={{8,0},{16,8},{24,16},{32,24},{40,32},{48,40},{56,48},{64,56},{72,6... | collective-permute-start | bytes 4616 | tf_op jit(solution)/shard_map/ppermute | solution.py:21
  (420 shorter events, 192.0 us)
Async XLA Ops:
  0.6 135.9 %copy-start = (f32[32,64]{1,0:T(8,128)S(1)}, f32[32,64]{1,0:T(8,128)}, u32[]{:S(2)}) copy-start(f32[32,64]{1,0:T(8,128)} %param.39) | copy-start | bytes 24580
  0.6 33.1 %copy-start.22 = (f32[3]{0:T(128)S(1)}, f32[3]{0:T(128)}, u32[]{:S(2)}) copy-start(f32[3]{0:T(128)} %constant.347.clone.1) | copy-start | bytes 40
  0.7 35.7 %copy-start.21 = (f32[3]{0:T(128)S(1)}, f32[3]{0:T(128)}, u32[]{:S(2)}) copy-start(f32[3]{0:T(128)} %constant.348.clone.1) | copy-start | bytes 40
  0.7 45.6 %copy-start.20 = (f32[3]{0:T(128)S(1)}, f32[3]{0:T(128)}, u32[]{:S(2)}) copy-start(f32[3]{0:T(128)} %constant.350.clone.1) | copy-start | bytes 40
  0.7 50.7 %copy-start.19 = (f32[3]{0:T(128)S(1)}, f32[3]{0:T(128)}, u32[]{:S(2)}) copy-start(f32[3]{0:T(128)} %constant.351.clone.1) | copy-start | bytes 40
  3.6 14.2 %collective-permute-start = (f32[6,8]{0,1:T(8,128)S(1)}, f32[6,8]{0,1:T(8,128)S(1)}, u32[]{:S(2)}, u32[]{:S(2)}) collective-permute-start(f32[6,8]{0,1:T(8,128)S(1)} %add_bitcast_fusion.7), channel_id=1, source_target_pairs={{504,0},{0,8},{8,16},{16,24},{24,32},{32,40},{40,48},{48,56},{56,6... | collective-permute-start | bytes 584 | tf_op jit(solution)/shard_map/ppermute | solution.py:21
  9.3 9.3 %collective-permute-start.1 = (f32[6,8]{0,1:T(8,128)S(1)}, f32[6,8]{0,1:T(8,128)S(1)}, u32[]{:S(2)}, u32[]{:S(2)}) collective-permute-start(f32[6,8]{0,1:T(8,128)S(1)} %add_bitcast_fusion.6), channel_id=1, source_target_pairs={{8,0},{16,8},{24,16},{32,24},{40,32},{48,40},{56,48},{64,56},{72,6... | collective-permute-start | bytes 584 | tf_op jit(solution)/shard_map/ppermute | solution.py:21
  21.2 9.6 %collective-permute-start.2 = (f32[6,8]{0,1:T(8,128)S(1)}, f32[6,8]{0,1:T(8,128)S(1)}, u32[]{:S(2)}, u32[]{:S(2)}) collective-permute-start(f32[6,8]{0,1:T(8,128)S(1)} %add_bitcast_fusion.5), channel_id=1, source_target_pairs={{7,0},{0,1},{1,2},{2,3},{3,4},{4,5},{5,6},{6,7},{15,8},{8,9},{9,10... | collective-permute-start | bytes 584 | tf_op jit(solution)/shard_map/ppermute | solution.py:21
  23.7 7.8 %collective-permute-start.3 = (f32[6,8]{0,1:T(8,128)S(1)}, f32[6,8]{0,1:T(8,128)S(1)}, u32[]{:S(2)}, u32[]{:S(2)}) collective-permute-start(f32[6,8]{0,1:T(8,128)S(1)} %add_bitcast_fusion.4), channel_id=1, source_target_pairs={{1,0},{2,1},{3,2},{4,3},{5,4},{6,5},{7,6},{0,7},{9,8},{10,9},{11,1... | collective-permute-start | bytes 584 | tf_op jit(solution)/shard_map/ppermute | solution.py:21
  31.5 27.5 %copy-start.12 = (s32[1,32,512]{2,1,0:T(8,128)S(1)}, s32[1,32,512]{2,1,0:T(8,128)}, u32[]{:S(2)}) copy-start(s32[1,32,512]{2,1,0:T(8,128)} %param.32) | copy-start | bytes 196612
  31.5 27.5 %copy-start.15 = (f32[64,8]{0,1:T(8,128)S(1)}, f32[64,8]{0,1:T(8,128)}, u32[]{:S(2)}) copy-start(f32[64,8]{0,1:T(8,128)} %param.37) | copy-start | bytes 6148
  31.5 27.5 %copy-start.17 = (f32[64]{0:T(128)S(1)}, f32[64]{0:T(128)}, u32[]{:S(2)}) copy-start(f32[64]{0:T(128)} %param.38) | copy-start | bytes 772
  33.8 10.9 %collective-permute-start.4 = (f32[3,128]{0,1:T(8,128)S(1)}, f32[3,128]{0,1:T(8,128)S(1)}, u32[]{:S(2)}, u32[]{:S(2)}) collective-permute-start(f32[3,128]{0,1:T(8,128)S(1)} %add_bitcast_fusion.3), channel_id=1, source_target_pairs={{504,0},{0,8},{8,16},{16,24},{24,32},{32,40},{40,48},{48,56},{56,6... | collective-permute-start | bytes 4616 | tf_op jit(solution)/shard_map/ppermute | solution.py:21
  36.4 9.2 %collective-permute-start.5 = (f32[3,128]{0,1:T(8,128)S(1)}, f32[3,128]{0,1:T(8,128)S(1)}, u32[]{:S(2)}, u32[]{:S(2)}) collective-permute-start(f32[3,128]{0,1:T(8,128)S(1)} %add_bitcast_fusion.2), channel_id=1, source_target_pairs={{8,0},{16,8},{24,16},{32,24},{40,32},{48,40},{56,48},{64,56},{72,6... | collective-permute-start | bytes 4616 | tf_op jit(solution)/shard_map/ppermute | solution.py:21
  46.3 9.9 %collective-permute-start.6 = (f32[3,192]{0,1:T(8,128)S(1)}, f32[3,192]{0,1:T(8,128)S(1)}, u32[]{:S(2)}, u32[]{:S(2)}) collective-permute-start(f32[3,192]{0,1:T(8,128)S(1)} %add_bitcast_fusion.1), channel_id=1, source_target_pairs={{7,0},{0,1},{1,2},{2,3},{3,4},{4,5},{5,6},{6,7},{15,8},{8,9},{9,10... | collective-permute-start | bytes 6920 | tf_op jit(solution)/shard_map/ppermute | solution.py:21
  51.4 7.1 collective-permute-start.7
  112.8 10.1 %collective-permute-start.8 = (f32[64,128]{0,1:T(8,128)S(1)}, f32[64,128]{0,1:T(8,128)S(1)}, u32[]{:S(2)}, u32[]{:S(2)}) collective-permute-start(f32[64,128]{0,1:T(8,128)S(1)} %bitcast.357), channel_id=1, source_target_pairs={{504,0},{0,8},{8,16},{16,24},{24,32},{32,40},{40,48},{48,56},{56,6... | collective-permute-start | bytes 98312 | tf_op jit(solution)/shard_map/ppermute | solution.py:21
  114.7 22.4 %copy-start.14 = (f32[64,32]{0,1:T(8,128)S(1)}, f32[64,32]{0,1:T(8,128)}, u32[]{:S(2)}) copy-start(f32[64,32]{0,1:T(8,128)} %param.41) | copy-start | bytes 24580
  114.7 22.4 %copy-start.18 = (f32[64]{0:T(128)S(1)}, f32[64]{0:T(128)}, u32[]{:S(2)}) copy-start(f32[64]{0:T(128)} %param.42) | copy-start | bytes 772
  114.7 22.4 %copy-start.24 = (f32[64]{0:T(128)S(1)}, f32[64]{0:T(128)}, u32[]{:S(2)}) copy-start(f32[64]{0:T(128)} %param.43) | copy-start | bytes 772
  114.7 9.0 %collective-permute-start.9 = (f32[64,128]{0,1:T(8,128)S(1)}, f32[64,128]{0,1:T(8,128)S(1)}, u32[]{:S(2)}, u32[]{:S(2)}) collective-permute-start(f32[64,128]{0,1:T(8,128)S(1)} %bitcast.356), channel_id=1, source_target_pairs={{8,0},{16,8},{24,16},{32,24},{40,32},{48,40},{56,48},{64,56},{72,6... | collective-permute-start | bytes 98312 | tf_op jit(solution)/shard_map/ppermute | solution.py:21
  125.1 9.1 %collective-permute-start.10 = (f32[64,192]{0,1:T(8,128)S(1)}, f32[64,192]{0,1:T(8,128)S(1)}, u32[]{:S(2)}, u32[]{:S(2)}) collective-permute-start(f32[64,192]{0,1:T(8,128)S(1)} %bitcast.355), channel_id=1, source_target_pairs={{7,0},{0,1},{1,2},{2,3},{3,4},{4,5},{5,6},{6,7},{15,8},{8,9},{9,10... | collective-permute-start | bytes 147464 | tf_op jit(solution)/shard_map/ppermute | solution.py:21
  129.5 6.9 collective-permute-start.11
  137.3 14.9 %copy-start.1 = (f32[3,1152]{0,1:T(8,128)}, f32[3,1152]{0,1:T(8,128)S(1)}, u32[]{:S(2)}) copy-start(f32[3,1152]{0,1:T(8,128)S(1)} %get-tuple-element.995) | copy-start | bytes 41476 | tf_op jit(solution)/shard_map/while
  177.6 24.6 %copy-start.3 = (f32[3,1152]{0,1:T(8,128)S(1)}, f32[3,1152]{0,1:T(8,128)}, u32[]{:S(2)}) copy-start(f32[3,1152]{0,1:T(8,128)} %get-tuple-element.974) | copy-start | bytes 41476 | tf_op jit(solution)/shard_map/while
  205.3 24.9 %copy-start.10 = (f32[32,1152]{0,1:T(8,128)S(1)}, f32[32,1152]{0,1:T(8,128)}, u32[]{:S(2)}) copy-start(f32[32,1152]{0,1:T(8,128)} %get-tuple-element.975) | copy-start | bytes 442372 | tf_op jit(solution)/shard_map/while
  205.3 26.0 %copy-start.2 = (f32[3,1152]{0,1:T(8,128)S(1)}, f32[3,1152]{0,1:T(8,128)}, u32[]{:S(2)}) copy-start(f32[3,1152]{0,1:T(8,128)} %copy-done.1) | copy-start | bytes 41476 | tf_op jit(solution)/shard_map/while
  231.2 14.9 %copy-start.1 = (f32[3,1152]{0,1:T(8,128)}, f32[3,1152]{0,1:T(8,128)S(1)}, u32[]{:S(2)}) copy-start(f32[3,1152]{0,1:T(8,128)S(1)} %get-tuple-element.995) | copy-start | bytes 41476 | tf_op jit(solution)/shard_map/while
  271.5 24.6 %copy-start.3 = (f32[3,1152]{0,1:T(8,128)S(1)}, f32[3,1152]{0,1:T(8,128)}, u32[]{:S(2)}) copy-start(f32[3,1152]{0,1:T(8,128)} %get-tuple-element.974) | copy-start | bytes 41476 | tf_op jit(solution)/shard_map/while
  299.2 24.9 %copy-start.10 = (f32[32,1152]{0,1:T(8,128)S(1)}, f32[32,1152]{0,1:T(8,128)}, u32[]{:S(2)}) copy-start(f32[32,1152]{0,1:T(8,128)} %get-tuple-element.975) | copy-start | bytes 442372 | tf_op jit(solution)/shard_map/while
  299.2 26.0 %copy-start.2 = (f32[3,1152]{0,1:T(8,128)S(1)}, f32[3,1152]{0,1:T(8,128)}, u32[]{:S(2)}) copy-start(f32[3,1152]{0,1:T(8,128)} %copy-done.1) | copy-start | bytes 41476 | tf_op jit(solution)/shard_map/while
  325.1 14.9 %copy-start.1 = (f32[3,1152]{0,1:T(8,128)}, f32[3,1152]{0,1:T(8,128)S(1)}, u32[]{:S(2)}) copy-start(f32[3,1152]{0,1:T(8,128)S(1)} %get-tuple-element.995) | copy-start | bytes 41476 | tf_op jit(solution)/shard_map/while
  365.4 24.6 %copy-start.3 = (f32[3,1152]{0,1:T(8,128)S(1)}, f32[3,1152]{0,1:T(8,128)}, u32[]{:S(2)}) copy-start(f32[3,1152]{0,1:T(8,128)} %get-tuple-element.974) | copy-start | bytes 41476 | tf_op jit(solution)/shard_map/while
  393.1 24.9 %copy-start.10 = (f32[32,1152]{0,1:T(8,128)S(1)}, f32[32,1152]{0,1:T(8,128)}, u32[]{:S(2)}) copy-start(f32[32,1152]{0,1:T(8,128)} %get-tuple-element.975) | copy-start | bytes 442372 | tf_op jit(solution)/shard_map/while
  393.1 26.0 %copy-start.2 = (f32[3,1152]{0,1:T(8,128)S(1)}, f32[3,1152]{0,1:T(8,128)}, u32[]{:S(2)}) copy-start(f32[3,1152]{0,1:T(8,128)} %copy-done.1) | copy-start | bytes 41476 | tf_op jit(solution)/shard_map/while
  459.3 24.6 %copy-start.3 = (f32[3,1152]{0,1:T(8,128)S(1)}, f32[3,1152]{0,1:T(8,128)}, u32[]{:S(2)}) copy-start(f32[3,1152]{0,1:T(8,128)} %get-tuple-element.974) | copy-start | bytes 41476 | tf_op jit(solution)/shard_map/while
  487.0 24.9 %copy-start.10 = (f32[32,1152]{0,1:T(8,128)S(1)}, f32[32,1152]{0,1:T(8,128)}, u32[]{:S(2)}) copy-start(f32[32,1152]{0,1:T(8,128)} %get-tuple-element.975) | copy-start | bytes 442372 | tf_op jit(solution)/shard_map/while
  487.0 26.0 %copy-start.2 = (f32[3,1152]{0,1:T(8,128)S(1)}, f32[3,1152]{0,1:T(8,128)}, u32[]{:S(2)}) copy-start(f32[3,1152]{0,1:T(8,128)} %copy-done.1) | copy-start | bytes 41476 | tf_op jit(solution)/shard_map/while
  514.9 19.4 %collective-permute-start.12 = (f32[64,192]{1,0:T(8,128)S(1)}, f32[64,192]{1,0:T(8,128)S(1)}, u32[]{:S(2)}, u32[]{:S(2)}) collective-permute-start(f32[64,192]{1,0:T(8,128)S(1)} %get-tuple-element.728), channel_id=1, source_target_pairs={{7,0},{0,1},{1,2},{2,3},{3,4},{4,5},{5,6},{6,7},{15,8},{8,9},{9,10... | collective-permute-start | bytes 147464 | tf_op jit(solution)/shard_map/ppermute | solution.py:21
  532.3 6.5 collective-permute-start.13
  538.8 17.8 %copy-start.5 = (f32[3,1152]{0,1:T(8,128)S(1)}, f32[3,1152]{0,1:T(8,128)}, u32[]{:S(2)}) copy-start(f32[3,1152]{0,1:T(8,128)} %get-tuple-element.1010) | copy-start | bytes 41476
  542.4 10.6 %collective-permute-start.14 = (f32[64,128]{0,1:T(8,128)S(1)}, f32[64,128]{0,1:T(8,128)S(1)}, u32[]{:S(2)}, u32[]{:S(2)}) collective-permute-start(f32[64,128]{0,1:T(8,128)S(1)} %get-tuple-element.726), channel_id=1, source_target_pairs={{504,0},{0,8},{8,16},{16,24},{24,32},{32,40},{40,48},{48,56},{56,6... | collective-permute-start | bytes 98312 | tf_op jit(solution)/shard_map/ppermute | solution.py:21
  544.3 10.1 %collective-permute-start.15 = (f32[64,128]{0,1:T(8,128)S(1)}, f32[64,128]{0,1:T(8,128)S(1)}, u32[]{:S(2)}, u32[]{:S(2)}) collective-permute-start(f32[64,128]{0,1:T(8,128)S(1)} %get-tuple-element.725), channel_id=1, source_target_pairs={{8,0},{16,8},{24,16},{32,24},{40,32},{48,40},{56,48},{64,56},{72,6... | collective-permute-start | bytes 98312 | tf_op jit(solution)/shard_map/ppermute | solution.py:21
  730.4 28.7 %copy-start.13 = (f32[3,512]{0,1:T(8,128)S(1)}, f32[3,512]{0,1:T(8,128)}, u32[]{:S(2)}) copy-start(f32[3,512]{0,1:T(8,128)} %get-tuple-element.729) | copy-start | bytes 18436
  730.4 9.9 %collective-permute-start.16 = (f32[3,192]{0,1:T(8,128)S(1)}, f32[3,192]{0,1:T(8,128)S(1)}, u32[]{:S(2)}, u32[]{:S(2)}) collective-permute-start(f32[3,192]{0,1:T(8,128)S(1)} %get-tuple-element.722), channel_id=1, source_target_pairs={{7,0},{0,1},{1,2},{2,3},{3,4},{4,5},{5,6},{6,7},{15,8},{8,9},{9,10... | collective-permute-start | bytes 6920 | tf_op jit(solution)/shard_map/ppermute | solution.py:21
  736.7 8.9 %collective-permute-start.17 = (f32[3,192]{0,1:T(8,128)S(1)}, f32[3,192]{0,1:T(8,128)S(1)}, u32[]{:S(2)}, u32[]{:S(2)}) collective-permute-start(f32[3,192]{0,1:T(8,128)S(1)} %get-tuple-element.721), channel_id=1, source_target_pairs={{1,0},{2,1},{3,2},{4,3},{5,4},{6,5},{7,6},{0,7},{9,8},{10,9},{11,1... | collective-permute-start | bytes 6920 | tf_op jit(solution)/shard_map/ppermute | solution.py:21
  747.7 11.5 %collective-permute-start.18 = (f32[3,128]{0,1:T(8,128)S(1)}, f32[3,128]{0,1:T(8,128)S(1)}, u32[]{:S(2)}, u32[]{:S(2)}) collective-permute-start(f32[3,128]{0,1:T(8,128)S(1)} %get-tuple-element.724), channel_id=1, source_target_pairs={{504,0},{0,8},{8,16},{16,24},{24,32},{32,40},{40,48},{48,56},{56,6... | collective-permute-start | bytes 4616 | tf_op jit(solution)/shard_map/ppermute | solution.py:21
  749.7 10.9 %collective-permute-start.19 = (f32[3,128]{0,1:T(8,128)S(1)}, f32[3,128]{0,1:T(8,128)S(1)}, u32[]{:S(2)}, u32[]{:S(2)}) collective-permute-start(f32[3,128]{0,1:T(8,128)S(1)} %get-tuple-element.723), channel_id=1, source_target_pairs={{8,0},{16,8},{24,16},{32,24},{40,32},{48,40},{56,48},{64,56},{72,6... | collective-permute-start | bytes 4616 | tf_op jit(solution)/shard_map/ppermute | solution.py:21
  (30 other events, 78.1 us)
where the time goes:
time: 768 us; the launch traced here: 763 us
  other arithmetic  336 us (44%)
  local copies, waits for them, and re-layouts  230 us (30%)
  starting transfers between devices  109 us (14%)
  matrix products  71.4 us (9%)
  waiting for transfers between devices  13.9 us (2%)
    scatter-add x8, other arithmetic, pair_latent(): separation = ext_pos[:, safe_index] - own_pos[:, None, :]  183 us
    gather x12, local copies, waits for them, and re-layouts, pair_latent(): separation = ext_pos[:, safe_index] - own_pos[:, None, :]  129 us
    ppermute x20, starting transfers between devices, shifted(): return lax.ppermute(block, axis, route)  109 us
    scatter-add x4, other arithmetic, pair_energy(): partner = embed_ext[:, safe_index]  91.2 us
    dot_general x42, matrix products, matmul(): jnp.dot(left, right, precision=HIGHEST, preferred_element_type=jnp.float32)  71.4 us
    gather x8, local copies, waits for them, and re-layouts, pair_energy(): partner = embed_ext[:, safe_index]  65.5 us
  transfers between devices with their start and end apart: 20, of which 6 were waited for; matrix products, arithmetic and copies ran while one was open for 2% of the time, Pallas kernels for 0%

commit v1 on v0

v1 whole, which is shorter than its diff:
```python
import math

import jax
import jax.numpy as jnp
from jax import lax
from jax.experimental import pallas as pl
from jax.experimental.pallas import tpu as pltpu
from jax.sharding import PartitionSpec as P

F32 = jnp.float32
BF16 = jnp.bfloat16
I32 = jnp.int32

TIME_STEP = 0.05
CENTRE_SPAN = 3.0
HIGHEST = lax.Precision.HIGHEST

NB = 8
NEI = 32
H = 64
EMB = 32
OWN = 512
GX = 128
GY = 192
MIG = 8
LANES = 128
INNER = OWN + 2 * GX
EXT = INNER + 2 * GY
GROUPS = EXT // LANES
HALF = 256
LEVELS = -(-EXT // HALF)
BIG = 48 * 1024 * 1024


def half_split(value):
    high = value.astype(BF16)
    low = (value - high.astype(F32)).astype(BF16)
    return high, low


def third_split(value):
    high = value.astype(BF16)
    rest = value - high.astype(F32)
    middle = rest.astype(BF16)
    low = (rest - middle.astype(F32)).astype(BF16)
    return high, middle, low


def lane_take(table, index):
    return jnp.take_along_axis(table, index, axis=1, mode="promise_in_bounds")


def take_lanes(read, rows, groups, index_row):
    low = jnp.broadcast_to(index_row & (LANES - 1), (8, LANES))
    high = jnp.broadcast_to(index_row >> 7, (8, LANES))
    pieces = []
    for r in range(rows // 8):
        taken = jnp.zeros((8, LANES), F32)
        for g in range(groups):
            taken = jnp.where(high == g, lane_take(read(r, g), low), taken)
        pieces.append(taken)
    return jnp.concatenate(pieces, axis=0) if len(pieces) > 1 else pieces[0]


def tile_reader(ref):
    return lambda r, g: ref[8 * r : 8 * r + 8, LANES * g : LANES * (g + 1)]


def spread(values, lists, width):
    count = values.shape[1]
    hot = jnp.where(lax.broadcasted_iota(I32, (width, count), 0) == lists, 1.0, 0.0).astype(BF16)
    total = None
    for part in third_split(values):
        piece = lax.dot_general(part, hot, (((1,), (1,)), ((), ())), preferred_element_type=F32)
        total = piece if total is None else total + piece
    return total


def by_parity(parity, even, odd):
    return jnp.where(parity == 0, even, odd)


def unit_row(rows, row, amount):
    return jnp.where(lax.broadcasted_iota(I32, (rows, 1), 0) == row, amount, 0.0)


def place(bundle, slots, message):
    lane = lax.broadcasted_iota(I32, bundle.shape, 1)
    for k in range(MIG):
        bundle = jnp.where(lane == slots[:, k : k + 1], message[:, k : k + 1], bundle)
    return bundle


def take_migrants(scratch, lists, row, first, second):
    pair = []
    for chosen, shift in (first, second):
        pair.append(take_lanes(tile_reader(scratch), 8, OWN // LANES, chosen) + unit_row(8, row, shift))
    return pair


def prepare_kernel(
    par, basis_t, pair, mix_t, w_embed, b_basis, b_pair, w_out, basis, ahead, back, w_back, columns
):
    high, low = half_split(basis_t[...])
    high, low = high.astype(F32), low.astype(F32)
    parts = [part.astype(F32) for part in third_split(b_basis[...])]
    parts = jnp.concatenate(parts + [jnp.zeros((NB - 3, H), F32)], axis=0)
    basis[...] = jnp.concatenate([high, high, low, parts], axis=0).T.astype(BF16)
    rows = jnp.concatenate([b_pair[...], w_out[...], jnp.zeros((NB - 2, H), F32)], axis=0)
    columns[...] = rows.T
    w_back[...] = w_embed[...].T
    layer_t = jnp.concatenate([pair[...].T, mix_t[...]], axis=0)
    high, low = half_split(layer_t)
    high, low = high.astype(F32), low.astype(F32)
    nothing = jnp.zeros((H + EMB, H), F32)
    back[...] = jnp.concatenate(
        [jnp.concatenate([high, high], axis=1), jnp.concatenate([low, nothing], axis=1)], axis=0
    ).astype(BF16)
    ahead[0:H, :] = jnp.concatenate([high, high], axis=0).T.astype(BF16)
    ahead[H : 2 * H, :] = jnp.concatenate([low, nothing], axis=0).T.astype(BF16)


def start_kernel(par, pos, vel, frc, mx, bundle_out, one, two):
    speeds = vel[...] + (0.5 * TIME_STEP) * frc[...]
    coords = pos[...] + TIME_STEP * speeds
    bundle_out[0:3, :] = coords
    bundle_out[3:6, :] = speeds
    bundle_out[6:8, :] = jnp.zeros((2, OWN), F32)
    p = par[0]
    first = (by_parity(p, mx[0:1, :], mx[1:2, :]), by_parity(p, -1.0, 1.0))
    second = (by_parity(p, mx[1:2, :], mx[0:1, :]), by_parity(p, 1.0, -1.0))
    one[...], two[...] = take_migrants(bundle_out, mx, 0, first, second)


def arrive(bundle, par, p_index, lists, one, two):
    p = par[p_index]
    from_lower = by_parity(p, two[...], one[...])
    from_upper = by_parity(p, one[...], two[...])
    bundle = place(bundle, lists[1:2, :], from_lower)
    return place(bundle, lists[0:1, :], from_upper)


def cross_kernel(par, bundle, one_in, two_in, mx, my, bundle_out, one, two):
    bundle_out[...] = arrive(bundle[...], par, 0, mx, one_in, two_in)
    p = par[1]
    first = (by_parity(p, my[0:1, :], my[1:2, :]), by_parity(p, -1.0, 1.0))
    second = (by_parity(p, my[1:2, :], my[0:1, :]), by_parity(p, 1.0, -1.0))
    one[...], two[...] = take_migrants(bundle_out, my, 1, first, second)


def settle_kernel(par, bundle, one_in, two_in, my, gx, bundle_out, one, two):
    bundle_out[...] = arrive(bundle[...], par, 1, my, one_in, two_in)
    p = par[0]
    first = (by_parity(p, gx[0:1, :], gx[1:2, :]), by_parity(p, -1.0, 1.0))
    second = (by_parity(p, gx[1:2, :], gx[0:1, :]), by_parity(p, 1.0, -1.0))
    one[...], two[...] = take_migrants(bundle_out, gx, 0, first, second)


def narrow_messages(par, table, rows, gy, row, one, two):
    p = par[1]
    for out, chosen, shift in (
        (one, by_parity(p, gy[0:1, :], gy[1:2, :]), by_parity(p, -1.0, 1.0)),
        (two, by_parity(p, gy[1:2, :], gy[0:1, :]), by_parity(p, 1.0, -1.0)),
    ):
        for c in range(2):
            taken = take_lanes(tile_reader(table), rows, INNER // LANES, chosen[:, LANES * c : LANES * (c + 1)])
            if row is not None:
                taken = taken + unit_row(rows, row, shift)
            out[:, LANES * c : LANES * (c + 1)] = taken


def inner_table(par, own, one, two, table):
    p = par[0]
    table[:, 0:OWN] = own
    table[:, OWN : OWN + GX] = by_parity(p, two[...], one[...])
    table[:, OWN + GX : INNER] = by_parity(p, one[...], two[...])


def outer_table(par, one, two, table):
    p = par[1]
    table[:, INNER : INNER + GY] = by_parity(p, two[:, 0:GY], one[:, 0:GY])
    table[:, INNER + GY : EXT] = by_parity(p, one[:, 0:GY], two[:, 0:GY])


def ghost_kernel(shift_row, par, own, one_in, two_in, gy, one, two, table):
    inner_table(par, own[...], one_in, two_in, table)
    narrow_messages(par, table, own.shape[0], gy, shift_row, one, two)


def env_kernel(
    par, own, gx1, gx2, gy1, gy2, nbr, basis, w_embed, gx,
    embed, one, two, lat_high, lat_low, slope, geo, table, square,
):
    inner_table(par, own[...], gx1, gx2, table)
    outer_table(par, gy1, gy2, table)
    for b in range(OWN // LANES):
        lanes = slice(LANES * b, LANES * (b + 1))
        for q in range(NEI // 8):
            rows = slice(8 * q, 8 * q + 8)
            index = nbr[rows, lanes]
            low = index & (LANES - 1)
            high = index >> 7
            total = jnp.zeros((8, LANES), F32)
            for c in range(3):
                taken = jnp.zeros((8, LANES), F32)
                for g in range(GROUPS):
                    tile = jnp.broadcast_to(table[c : c + 1, LANES * g : LANES * (g + 1)], (8, LANES))
                    taken = jnp.where(high == g, lane_take(tile, low), taken)
                apart = taken - own[c : c + 1, lanes]
                geo[c, rows, lanes] = apart
                total = total + apart * apart
            square[rows, lanes] = total
            geo[3, rows, lanes] = jnp.where(index >= 0, 1.0 / (1.0 + total), 0.0)

    centre = lax.broadcasted_iota(I32, (NB, 1), 0).astype(F32) * (CENTRE_SPAN / (NB - 1))
    ones = jnp.ones((NB, HALF), F32)
    left = basis[...]
    for half in range(OWN // HALF):
        lanes = slice(HALF * half, HALF * (half + 1))

        def turn(n, gathered):
            offset = square[pl.ds(n, 1), lanes] - centre
            weight = geo[3, pl.ds(n, 1), lanes]
            radial = jnp.exp(-(offset * offset))
            falling = -2.0 * offset * radial
            radial_high = radial.astype(BF16).astype(F32)
            falling_high = falling.astype(BF16).astype(F32)
            right = jnp.concatenate(
                [
                    jnp.concatenate([radial_high, radial - radial_high, radial_high, ones], axis=0),
                    jnp.concatenate([falling_high, falling - falling_high, falling_high, 0.0 * ones], axis=0),
                ],
                axis=1,
            ).astype(BF16)
            both = lax.dot_general(left, right, (((1,), (0,)), ((), ())), preferred_element_type=F32)
            value = both[:, :HALF]
            rate = both[:, HALF:]
            gate = 0.5 * jnp.tanh(0.5 * value) + 0.5
            raw = value * gate
            latent = raw * weight
            slope[n, :, lanes] = weight * ((gate + raw * (1.0 - gate)) * rate - latent)
            high, low = half_split(latent)
            lat_high[n, :, lanes] = high
            lat_low[n, :, lanes] = low
            return gathered + latent

        gathered = lax.fori_loop(0, NEI, turn, jnp.zeros((H, HALF), F32))
        environ = gathered * (1.0 / math.sqrt(NEI))
        embed[:, lanes] = jnp.dot(w_embed[...], environ, precision=HIGHEST, preferred_element_type=F32)
    p = par[0]
    reader = tile_reader(embed)
    one[...] = take_lanes(reader, EMB, OWN // LANES, by_parity(p, gx[0:1, :], gx[1:2, :]))
    two[...] = take_lanes(reader, EMB, OWN // LANES, by_parity(p, gx[1:2, :], gx[0:1, :]))


def hot_rows(low_row, count):
    level = lax.broadcasted_iota(I32, (HALF, count), 0)
    return jnp.where(level == low_row, 1.0, 0.0).astype(BF16)


def level_rows(value, high_row):
    pieces = []
    for k in range(LEVELS):
        mask = jnp.where(high_row == k, 1.0, 0.0).astype(BF16)
        pieces.append(value * mask)
    return jnp.concatenate(pieces, axis=0)


def pair_kernel(
    par, own, gx1, gx2, gy1, gy2, nbr, lat_high, lat_low, slope, geo, ahead, back, columns,
    rise, inner, one, two, table, spread_sum, own_sum, joined,
):
    inner_table(par, own[...], gx1, gx2, table)
    outer_table(par, gy1, gy2, table)
    spread_sum[...] = jnp.zeros(spread_sum.shape, F32)
    own_sum[...] = jnp.zeros(own_sum.shape, F32)
    left = ahead[...]
    right_back = back[...]
    bias = columns[:, 0:1]
    readout = columns[:, 1:2]

    def turn(n, carry):
        for half in range(OWN // HALF):
            lanes = slice(HALF * half, HALF * (half + 1))
            index = nbr[pl.ds(n, 1), lanes]
            weight = geo[3, pl.ds(n, 1), lanes]
            partner = jnp.concatenate(
                [
                    take_lanes(tile_reader(table), EMB, GROUPS, index[:, LANES * c : LANES * (c + 1)])
                    for c in range(HALF // LANES)
                ],
                axis=1,
            )
            embed_own = own[:, lanes]
            product_high, product_low = half_split(partner * embed_own)
            right = jnp.concatenate(
                [lat_high[n, :, lanes], product_high, lat_low[n, :, lanes], product_low], axis=0
            )
            sums = lax.dot_general(left, right, (((1,), (0,)), ((), ())), preferred_element_type=F32)
            value = sums[:H] + sums[H:] + bias
            gate = 0.5 * jnp.tanh(0.5 * value) + 0.5
            hidden = value * gate
            dvalue = (gate + hidden * (1.0 - gate)) * (readout * weight)
            dhigh, dlow = half_split(dvalue)
            sums = lax.dot_general(
                right_back, jnp.concatenate([dhigh, dlow], axis=0), (((1,), (0,)), ((), ())),
                preferred_element_type=F32,
            )
            total = sums[: H + EMB] + sums[H + EMB :]
            dlatent = total[:H]
            dproduct = total[H:]
            dsum = dlatent * slope[n, :, lanes] - (weight * weight) * (hidden * readout)
            rise[pl.ds(n, 1), lanes] = jnp.sum(dsum, axis=0, keepdims=True)
            own_sum[:, lanes] = own_sum[:, lanes] + dproduct * partner
            high, low = half_split(dproduct * embed_own)
            joined[:, lanes] = jnp.concatenate([high, low], axis=0)
        index = nbr[pl.ds(n, 1), :]
        spread_sum[...] += lax.dot_general(
            level_rows(joined[...], index >> 8), hot_rows(index & (HALF - 1), OWN),
            (((1,), (1,)), ((), ())), preferred_element_type=F32,
        )
        return carry

    lax.fori_loop(0, NEI, turn, 0)
    for k in range(LEVELS):
        base = 2 * EMB * k
        width = min(HALF, EXT - HALF * k)
        table[:, HALF * k : HALF * k + width] = (
            spread_sum[base : base + EMB, :width] + spread_sum[base + EMB : base + 2 * EMB, :width]
        )
    inner[:, 0:OWN] = table[:, 0:OWN] + own_sum[...]
    inner[:, OWN:INNER] = table[:, OWN:INNER]
    outer_messages(par, table, one, two)


def outer_messages(par, table, one, two):
    p = par[1]
    down = table[:, INNER : INNER + GY]
    up = table[:, INNER + GY : EXT]
    one[...] = by_parity(p, up, down)
    two[...] = by_parity(p, down, up)


def fold_narrow(par, inner, one, two, gy):
    p = par[1]
    from_upper = by_parity(p, one[...], two[...])
    from_lower = by_parity(p, two[...], one[...])
    return (
        inner[...]
        + spread(from_upper, gy[0:1, 0:GY], INNER)
        + spread(from_lower, gy[1:2, 0:GY], INNER)
    )


def fold_long(par, own, one, two, gx):
    p = par[0]
    from_upper = by_parity(p, one[...], two[...])
    from_lower = by_parity(p, two[...], one[...])
    return own[...] + spread(from_upper, gx[0:1, :], OWN) + spread(from_lower, gx[1:2, :], OWN)


def fold_kernel(par, inner, one_in, two_in, gy, own, one, two):
    total = fold_narrow(par, inner, one_in, two_in, gy)
    own[...] = total[:, 0:OWN]
    down = total[:, OWN : OWN + GX]
    up = total[:, OWN + GX : INNER]
    p = par[0]
    one[...] = by_parity(p, up, down)
    two[...] = by_parity(p, down, up)


def force_kernel(
    par, own_in, gx1, gx2, gx, w_back, slope, rise, geo, nbr, inner, one, two, table, spread_sum, pushes, grown,
):
    grad = fold_long(par, own_in, gx1, gx2, gx)
    grown[...] = jnp.dot(w_back[...], grad, precision=HIGHEST, preferred_element_type=F32) * (1.0 / math.sqrt(NEI))
    spread_sum[...] = jnp.zeros(spread_sum.shape, F32)

    def turn(n, carry):
        rate = jnp.sum(slope[n] * grown[...], axis=0, keepdims=True) + rise[pl.ds(n, 1), :]
        twice = 2.0 * rate
        push = [geo[c, pl.ds(n, 1), :] * twice for c in range(3)]
        highs = [v.astype(BF16).astype(F32) for v in push]
        rows = highs + [v - h for v, h in zip(push, highs)]
        empty = jnp.zeros((2, OWN), F32)
        value = jnp.concatenate(rows + [empty], axis=0)
        pushes[...] += value
        index = nbr[pl.ds(n, 1), :]
        high_row = index >> 8
        lifted = jnp.concatenate(
            [jnp.where(high_row == k, value, 0.0) for k in range(LEVELS)], axis=0
        ).astype(BF16)
        spread_sum[...] += lax.dot_general(
            lifted, hot_rows(index & (HALF - 1), OWN), (((1,), (1,)), ((), ())), preferred_element_type=F32
        )
        return carry

    pushes[...] = jnp.zeros(pushes.shape, F32)
    lax.fori_loop(0, NEI, turn, 0)
    table[...] = jnp.zeros(table.shape, F32)
    for k in range(LEVELS):
        width = min(HALF, EXT - HALF * k)
        table[0:3, HALF * k : HALF * k + width] = (
            spread_sum[8 * k : 8 * k + 3, :width] + spread_sum[8 * k + 3 : 8 * k + 6, :width]
        )
    table[0:3, 0:OWN] = table[0:3, 0:OWN] - pushes[0:3, :] - pushes[3:6, :]
    inner[...] = table[:, 0:INNER]
    outer_messages(par, table, one, two)


def final_kernel(par, own, one, two, gx, bundle, pos_out, vel_out, frc_out):
    forces = -fold_long(par, own, one, two, gx)[0:3, :]
    pos_out[...] = bundle[0:3, :]
    vel_out[...] = bundle[3:6, :] + (0.5 * TIME_STEP) * forces
    frc_out[...] = forces


def call(kernel, name, shapes, scratch, par, *operands):
    return pl.pallas_call(
        kernel,
        name=name,
        out_shape=[jax.ShapeDtypeStruct(shape, kind) for shape, kind in shapes],
        in_specs=[pl.BlockSpec(memory_space=pltpu.SMEM)]
        + [pl.BlockSpec(memory_space=pltpu.VMEM)] * len(operands),
        out_specs=[pl.BlockSpec(memory_space=pltpu.VMEM)] * len(shapes),
        scratch_shapes=[pltpu.VMEM(shape, kind) for shape, kind in scratch],
        compiler_params=pltpu.CompilerParams(vmem_limit_bytes=BIG),
    )(par, *operands)


def swap(axis, first):
    count = lax.axis_size(axis)
    offset = 0 if first else 1
    route = []
    for i in range(count):
        route.append((i, (((i + offset) ^ 1) - offset) % count))
    return route


def exchange(axis, one, two):
    return (
        lax.ppermute(one, axis, swap(axis, True)),
        lax.ppermute(two, axis, swap(axis, False)),
    )


def on_device(
    positions, velocities, forces, neighbours, ghost_x, ghost_y, migrate_x, migrate_y,
    w_basis, b_basis, w_embed, w_pair, w_mix, b_pair, w_out,
):
    par = jnp.stack([lax.axis_index("gx") % 2, lax.axis_index("gy") % 2]).astype(I32)
    near = neighbours[0]
    gx = ghost_x[0]
    gy = jnp.pad(ghost_y[0], ((0, 0), (0, HALF - GY)))
    mx = jnp.pad(migrate_x[0], ((0, 0), (0, LANES - MIG)))
    my = jnp.pad(migrate_y[0], ((0, 0), (0, LANES - MIG)))

    basis, ahead, back, w_back, columns = call(
        prepare_kernel,
        "prepare",
        [
            ((H, 4 * NB), BF16), ((2 * H, 2 * (H + EMB)), BF16), ((2 * (H + EMB), 2 * H), BF16),
            ((H, EMB), F32), ((H, NB), F32),
        ],
        [],
        par, w_basis.T, w_pair, w_mix.T, w_embed,
        b_basis.reshape(1, H), b_pair.reshape(1, H), w_out.reshape(1, H),
    )

    tile = ((8, LANES), F32)
    wide = ((8, OWN), F32)
    bundle, one, two = call(start_kernel, "start", [wide, tile, tile], [], par, positions, velocities, forces, mx)
    one, two = exchange("gx", one, two)
    bundle, one, two = call(cross_kernel, "cross", [wide, tile, tile], [], par, bundle, one, two, mx, my)
    one, two = exchange("gy", one, two)
    bundle, one, two = call(settle_kernel, "settle", [wide, tile, tile], [], par, bundle, one, two, my, gx)
    px = exchange("gx", one, two)
    message = ((8, HALF), F32)
    one, two = call(
        lambda *refs: ghost_kernel(1, *refs), "ghost", [message, message], [((8, INNER), F32)], par, bundle, *px, gy
    )
    py = exchange("gy", one, two)

    embed, one, two, lat_high, lat_low, slope, geo = call(
        env_kernel,
        "env",
        [
            ((EMB, OWN), F32), ((EMB, GX), F32), ((EMB, GX), F32),
            ((NEI, H, OWN), BF16), ((NEI, H, OWN), BF16), ((NEI, H, OWN), F32), ((4, NEI, OWN), F32),
        ],
        [((8, EXT), F32), ((NEI, OWN), F32)],
        par, bundle, *px, *py, near, basis, w_embed, gx,
    )
    ex = exchange("gx", one, two)
    message = ((EMB, HALF), F32)
    one, two = call(
        lambda *refs: ghost_kernel(None, *refs), "ghost_embed", [message, message], [((EMB, INNER), F32)],
        par, embed, *ex, gy,
    )
    ey = exchange("gy", one, two)
    message = ((EMB, GY), F32)
    rise, inner, one, two = call(
        pair_kernel,
        "pair",
        [((NEI, OWN), F32), ((EMB, INNER), F32), message, message],
        [
            ((EMB, EXT), F32), ((LEVELS * 2 * EMB, HALF), F32), ((EMB, OWN), F32), ((2 * EMB, OWN), BF16),
        ],
        par, embed, *ex, *ey, near, lat_high, lat_low, slope, geo, ahead, back, columns,
    )
    one, two = exchange("gy", one, two)
    message = ((EMB, GX), F32)
    own, one, two = call(
        fold_kernel, "fold_embed", [((EMB, OWN), F32), message, message], [], par, inner, one, two, gy
    )
    one, two = exchange("gx", one, two)
    message = ((8, GY), F32)
    inner, one, two = call(
        force_kernel,
        "force",
        [((8, INNER), F32), message, message],
        [((8, EXT), F32), ((8 * LEVELS, HALF), F32), ((8, OWN), F32), ((H, OWN), F32)],
        par, own, one, two, gx, w_back, slope, rise, geo, near,
    )
    one, two = exchange("gy", one, two)
    own, one, two = call(fold_kernel, "fold_force", [wide, tile, tile], [], par, inner, one, two, gy)
    one, two = exchange("gx", one, two)
    flat = ((3, OWN), F32)
    return tuple(call(final_kernel, "final", [flat, flat, flat], [], par, own, one, two, gx, bundle))


def solution(mesh):
    both = ("gx", "gy")
    flat = P(None, both)
    stacked = P(None, None, both)
    return jax.shard_map(
        on_device,
        mesh=mesh,
        in_specs=(flat,) * 3 + (stacked,) * 5 + (P(),) * 7,
        out_specs=(flat,) * 3,
        check_vma=False,
    )
```

time: 768 us -> 188 us (0.24)
  other arithmetic: 336 us -> 0.07 us
  local copies, waits for them, and re-layouts: 230 us -> 12.7 us
  matrix products: 71.4 us -> 0 us
  Pallas kernels: 0 us -> 64.9 us
  starting transfers between devices: 109 us -> 77.1 us
  waiting for transfers between devices: 13.9 us -> 31 us
    scatter-add x20 -> x0, other arithmetic: 287 us -> none  [the longest x8 183 us: pair_latent(): separation = ext_pos[:, safe_index] - own_pos[:, None, :]]
    gather x32 -> x0, local copies, waits for them, and re-layouts: 202 us -> none  [the longest x12 129 us: pair_latent(): separation = ext_pos[:, safe_index] - own_pos[:, None, :]]
    dot_general x42 -> x0, matrix products: 71.4 us -> none  [matmul(): jnp.dot(left, right, precision=HIGHEST, preferred_element_type=jnp.float32)]
    pallas_call x0 -> x12, Pallas kernels: none -> 64.9 us  [call(): pl.pallas_call(kernel, name=name, out_shape=[jax.ShapeDtypeStruct(shape,...]
    ppermute x20, starting transfers between devices: 109 us -> 77.1 us  [the longest x10 46 us: exchange(): lax.ppermute(one, axis, swap(axis, True))]
    reduce_sum x28 -> x0, other arithmetic: 22.4 us -> none  [the longest x8 14 us: pair_latent(): separation = ext_pos[:, safe_index] - own_pos[:, None, :]]
    ppermute x20, waiting for transfers between devices: 13.9 us -> 31 us  [the longest x10 29 us: exchange(): lax.ppermute(two, axis, swap(axis, False))]
    add_any x28 -> x0, other arithmetic: 13.9 us -> none  [the longest x8 13.6 us: pair_latent(): square = jnp.sum(separation * separation, axis=0)]
  transfers between devices with their start and end apart: 20 -> 20, of which waited for: 6 -> 10; matrix products, arithmetic and copies ran while one was open for 2% -> 1% of each run, Pallas kernels for 0% -> 0%
where the time goes in v1:
time: 188 us; the launch traced here: 187 us
  starting transfers between devices  77.1 us (41%)
  Pallas kernels  64.9 us (35%)
  waiting for transfers between devices  31 us (16%)
  local copies, waits for them, and re-layouts  12.7 us (7%)
    pallas_call x12, Pallas kernels, call(): pl.pallas_call(kernel, name=name, out_shape=[jax.ShapeDtypeStruct(shape,...  64.9 us
    ppermute x10, starting transfers between devices, exchange(): lax.ppermute(one, axis, swap(axis, True))  46 us
    ppermute x10, starting transfers between devices, exchange(): lax.ppermute(two, axis, swap(axis, False))  31.1 us
    ppermute x10, waiting for transfers between devices, exchange(): lax.ppermute(two, axis, swap(axis, False))  29 us
    unnamed x36, local copies, waits for them, and re-layouts  10.7 us
  transfers between devices with their start and end apart: 20, of which 10 were waited for; matrix products, arithmetic and copies ran while one was open for 1% of the time, Pallas kernels for 0%

profile of v1, /device:TPU:1, one launch (start us, length us, event | category | flops | bytes accessed | tf_op | source)
XLA Modules:
  0.0 186.7 jit_solution(18438690170409143486)
XLA Ops:
  2.1 0.7 copy-done.12
  2.8 0.7 copy-done.13
  4.1 8.8 %collective-permute-start = (f32[8,128]{1,0:T(8,128)S(1)}, f32[8,128]{1,0:T(8,128)S(1)}, u32[]{:S(2)}, u32[]{:S(2)}) collective-permute-start(f32[8,128]{1,0:T(8,128)S(1)} %get-tuple-element.42), channel_id=1, source_target_pairs={{0,8},{8,0},{16,24},{24,16},{32,40},{40,32},{48,56},{56,48},{64,72... | collective-permute-start | bytes 12296 | tf_op jit(solution)/shard_map/ppermute | solution.py:442
  12.9 1.9 %collective-permute-start.1 = (f32[8,128]{1,0:T(8,128)S(1)}, f32[8,128]{1,0:T(8,128)S(1)}, u32[]{:S(2)}, u32[]{:S(2)}) collective-permute-start(f32[8,128]{1,0:T(8,128)S(1)} %get-tuple-element.43), channel_id=1, source_target_pairs={{0,504},{8,16},{16,8},{24,32},{32,24},{40,48},{48,40},{56,64},{64,... | collective-permute-start | bytes 12296 | tf_op jit(solution)/shard_map/ppermute | solution.py:443
  15.5 2.3 %collective-permute-done.1.two_in = f32[8,128]{1,0:T(8,128)S(1)} collective-permute-done((f32[8,128]{1,0:T(8,128)S(1)}, f32[8,128]{1,0:T(8,128)S(1)}, u32[]{:S(2)}, u32[]{:S(2)}) %collective-permute-start.1) | collective-permute-done | bytes 4128 | tf_op jit(solution)/shard_map/ppermute | solution.py:443
  17.8 0.7 cross.1
  18.6 1.9 %collective-permute-start.2 = (f32[8,128]{1,0:T(8,128)S(1)}, f32[8,128]{1,0:T(8,128)S(1)}, u32[]{:S(2)}, u32[]{:S(2)}) collective-permute-start(f32[8,128]{1,0:T(8,128)S(1)} %get-tuple-element.45), channel_id=1, source_target_pairs={{0,1},{1,0},{2,3},{3,2},{4,5},{5,4},{6,7},{7,6},{8,9},{9,8},{10,11... | collective-permute-start | bytes 12296 | tf_op jit(solution)/shard_map/ppermute | solution.py:442
  20.5 1.9 %collective-permute-start.3 = (f32[8,128]{1,0:T(8,128)S(1)}, f32[8,128]{1,0:T(8,128)S(1)}, u32[]{:S(2)}, u32[]{:S(2)}) collective-permute-start(f32[8,128]{1,0:T(8,128)S(1)} %get-tuple-element.46), channel_id=1, source_target_pairs={{0,7},{1,2},{2,1},{3,4},{4,3},{5,6},{6,5},{7,0},{8,15},{9,10},{10,... | collective-permute-start | bytes 12296 | tf_op jit(solution)/shard_map/ppermute | solution.py:443
  22.5 2.0 %collective-permute-done.2.one_in = f32[8,128]{1,0:T(8,128)S(1)} collective-permute-done((f32[8,128]{1,0:T(8,128)S(1)}, f32[8,128]{1,0:T(8,128)S(1)}, u32[]{:S(2)}, u32[]{:S(2)}) %collective-permute-start.2) | collective-permute-done | bytes 4128 | tf_op jit(solution)/shard_map/ppermute | solution.py:442
  24.4 4.0 %collective-permute-done.3.two_in = f32[8,128]{1,0:T(8,128)S(1)} collective-permute-done((f32[8,128]{1,0:T(8,128)S(1)}, f32[8,128]{1,0:T(8,128)S(1)}, u32[]{:S(2)}, u32[]{:S(2)}) %collective-permute-start.3) | collective-permute-done | bytes 4128 | tf_op jit(solution)/shard_map/ppermute | solution.py:443
  29.2 0.7 settle.1
  29.9 9.2 %collective-permute-start.4 = (f32[8,128]{1,0:T(8,128)S(1)}, f32[8,128]{1,0:T(8,128)S(1)}, u32[]{:S(2)}, u32[]{:S(2)}) collective-permute-start(f32[8,128]{1,0:T(8,128)S(1)} %get-tuple-element.48), channel_id=1, source_target_pairs={{0,8},{8,0},{16,24},{24,16},{32,40},{40,32},{48,56},{56,48},{64,72... | collective-permute-start | bytes 12296 | tf_op jit(solution)/shard_map/ppermute | solution.py:442
  39.1 1.9 %collective-permute-start.5 = (f32[8,128]{1,0:T(8,128)S(1)}, f32[8,128]{1,0:T(8,128)S(1)}, u32[]{:S(2)}, u32[]{:S(2)}) collective-permute-start(f32[8,128]{1,0:T(8,128)S(1)} %get-tuple-element.49), channel_id=1, source_target_pairs={{0,504},{8,16},{16,8},{24,32},{32,24},{40,48},{48,40},{56,64},{64,... | collective-permute-start | bytes 12296 | tf_op jit(solution)/shard_map/ppermute | solution.py:443
  41.8 2.3 %collective-permute-done.5.refs_3_.gx2 = f32[8,128]{1,0:T(8,128)S(1)} collective-permute-done((f32[8,128]{1,0:T(8,128)S(1)}, f32[8,128]{1,0:T(8,128)S(1)}, u32[]{:S(2)}, u32[]{:S(2)}) %collective-permute-start.5) | collective-permute-done | bytes 4128 | tf_op jit(solution)/shard_map/ppermute | solution.py:443
  44.7 1.9 %collective-permute-start.6 = (f32[8,256]{1,0:T(8,128)S(1)}, f32[8,256]{1,0:T(8,128)S(1)}, u32[]{:S(2)}, u32[]{:S(2)}) collective-permute-start(f32[8,256]{1,0:T(8,128)S(1)} %get-tuple-element.50), channel_id=1, source_target_pairs={{0,1},{1,0},{2,3},{3,2},{4,5},{5,4},{6,7},{7,6},{8,9},{9,8},{10,11... | collective-permute-start | bytes 24584 | tf_op jit(solution)/shard_map/ppermute | solution.py:442
  46.7 6.1 %collective-permute-start.7 = (f32[8,256]{1,0:T(8,128)S(1)}, f32[8,256]{1,0:T(8,128)S(1)}, u32[]{:S(2)}, u32[]{:S(2)}) collective-permute-start(f32[8,256]{1,0:T(8,128)S(1)} %get-tuple-element.51), channel_id=1, source_target_pairs={{0,7},{1,2},{2,1},{3,4},{4,3},{5,6},{6,5},{7,0},{8,15},{9,10},{10,... | collective-permute-start | bytes 24584 | tf_op jit(solution)/shard_map/ppermute | solution.py:443
  52.8 0.7 copy-done.4
  53.5 0.8 copy-done.6
  54.3 0.7 copy-done.7
  57.6 0.8 prepare.1
  58.4 0.8 copy-done.1
  59.2 0.7 copy-done.5
  60.6 15.6 %env.1 = (f32[32,512]{1,0:T(8,128)S(1)}, f32[32,128]{1,0:T(8,128)S(1)}, f32[32,128]{1,0:T(8,128)S(1)}, bf16[32,64,512]{2,1,0:T(8,128)(2,1)S(1)}, bf16[32,64,512]...) custom-call(s32[2]{0:T(128)S(1)} %pad_add_fusion.par.refs_0_, ...), custom_call_target="tpu_custom_call" | custom-call | tf_op jit(solution)/shard_map/env/pallas_call | solution.py:419
  76.2 4.6 %collective-permute-start.8 = (f32[32,128]{1,0:T(8,128)S(1)}, f32[32,128]{1,0:T(8,128)S(1)}, u32[]{:S(2)}, u32[]{:S(2)}) collective-permute-start(f32[32,128]{1,0:T(8,128)S(1)} %get-tuple-element.54), channel_id=1, source_target_pairs={{0,8},{8,0},{16,24},{24,16},{32,40},{40,32},{48,56},{56,48},{64,72... | collective-permute-start | bytes 49160 | tf_op jit(solution)/shard_map/ppermute | solution.py:442
  80.8 1.9 %collective-permute-start.9 = (f32[32,128]{1,0:T(8,128)S(1)}, f32[32,128]{1,0:T(8,128)S(1)}, u32[]{:S(2)}, u32[]{:S(2)}) collective-permute-start(f32[32,128]{1,0:T(8,128)S(1)} %get-tuple-element.55), channel_id=1, source_target_pairs={{0,504},{8,16},{16,8},{24,32},{32,24},{40,48},{48,40},{56,64},{64,... | collective-permute-start | bytes 49160 | tf_op jit(solution)/shard_map/ppermute | solution.py:443
  82.7 3.1 %collective-permute-done.9.refs_3_.gx2 = f32[32,128]{1,0:T(8,128)S(1)} collective-permute-done((f32[32,128]{1,0:T(8,128)S(1)}, f32[32,128]{1,0:T(8,128)S(1)}, u32[]{:S(2)}, u32[]{:S(2)}) %collective-permute-start.9) | collective-permute-done | bytes 16416 | tf_op jit(solution)/shard_map/ppermute | solution.py:443
  85.8 0.7 ghost_embed.1
  86.6 1.9 %collective-permute-start.10 = (f32[32,256]{1,0:T(8,128)S(1)}, f32[32,256]{1,0:T(8,128)S(1)}, u32[]{:S(2)}, u32[]{:S(2)}) collective-permute-start(f32[32,256]{1,0:T(8,128)S(1)} %get-tuple-element.56), channel_id=1, source_target_pairs={{0,1},{1,0},{2,3},{3,2},{4,5},{5,4},{6,7},{7,6},{8,9},{9,8},{10,11... | collective-permute-start | bytes 98312 | tf_op jit(solution)/shard_map/ppermute | solution.py:442
  88.5 5.0 %collective-permute-start.11 = (f32[32,256]{1,0:T(8,128)S(1)}, f32[32,256]{1,0:T(8,128)S(1)}, u32[]{:S(2)}, u32[]{:S(2)}) collective-permute-start(f32[32,256]{1,0:T(8,128)S(1)} %get-tuple-element.57), channel_id=1, source_target_pairs={{0,7},{1,2},{2,1},{3,4},{4,3},{5,6},{6,5},{7,0},{8,15},{9,10},{10,... | collective-permute-start | bytes 98312 | tf_op jit(solution)/shard_map/ppermute | solution.py:443
  93.6 3.2 %collective-permute-done.11.gy2 = f32[32,256]{1,0:T(8,128)S(1)} collective-permute-done((f32[32,256]{1,0:T(8,128)S(1)}, f32[32,256]{1,0:T(8,128)S(1)}, u32[]{:S(2)}, u32[]{:S(2)}) %collective-permute-start.11) | collective-permute-done | bytes 32800 | tf_op jit(solution)/shard_map/ppermute | solution.py:443
  96.8 0.8 copy-done.2
  97.6 32.9 %pair.3 = (f32[32,512]{1,0:T(8,128)S(1)}, f32[32,768]{1,0:T(8,128)S(1)}, f32[32,192]{1,0:T(8,128)S(1)}, f32[32,192]{1,0:T(8,128)S(1)}) custom-call(s32[2]{0:T(128)S(1)} %pad_add_fusion.par.refs_0_, f32[32,512]{1,0:T(8,128)S(1)} %get-tuple-element.53.refs_1_.own, f32[32,128]{1,0:T(8,128)S(1)} %collective-permute-done.8.refs_2_.gx1, ...), custom_call_target="tpu_custom_call" | custom-call | tf_op jit(solution)/shard_map/pair/pallas_call | solution.py:419
  130.5 3.7 %collective-permute-start.12 = (f32[32,192]{1,0:T(8,128)S(1)}, f32[32,192]{1,0:T(8,128)S(1)}, u32[]{:S(2)}, u32[]{:S(2)}) collective-permute-start(f32[32,192]{1,0:T(8,128)S(1)} %get-tuple-element.66), channel_id=1, source_target_pairs={{0,1},{1,0},{2,3},{3,2},{4,5},{5,4},{6,7},{7,6},{8,9},{9,8},{10,11... | collective-permute-start | bytes 73736 | tf_op jit(solution)/shard_map/ppermute | solution.py:442
  134.2 3.3 %collective-permute-start.13 = (f32[32,192]{1,0:T(8,128)S(1)}, f32[32,192]{1,0:T(8,128)S(1)}, u32[]{:S(2)}, u32[]{:S(2)}) collective-permute-start(f32[32,192]{1,0:T(8,128)S(1)} %get-tuple-element.67), channel_id=1, source_target_pairs={{0,7},{1,2},{2,1},{3,4},{4,3},{5,6},{6,5},{7,0},{8,15},{9,10},{10,... | collective-permute-start | bytes 73736 | tf_op jit(solution)/shard_map/ppermute | solution.py:443
  137.5 4.9 %collective-permute-done.13.two_in = f32[32,192]{1,0:T(8,128)S(1)} collective-permute-done((f32[32,192]{1,0:T(8,128)S(1)}, f32[32,192]{1,0:T(8,128)S(1)}, u32[]{:S(2)}, u32[]{:S(2)}) %collective-permute-start.13) | collective-permute-done | bytes 24608 | tf_op jit(solution)/shard_map/ppermute | solution.py:443
  142.5 1.3 fold_embed.1
  143.8 6.9 %collective-permute-start.14 = (f32[32,128]{1,0:T(8,128)S(1)}, f32[32,128]{1,0:T(8,128)S(1)}, u32[]{:S(2)}, u32[]{:S(2)}) collective-permute-start(f32[32,128]{1,0:T(8,128)S(1)} %get-tuple-element.69), channel_id=1, source_target_pairs={{0,8},{8,0},{16,24},{24,16},{32,40},{40,32},{48,56},{56,48},{64,72... | collective-permute-start | bytes 49160 | tf_op jit(solution)/shard_map/ppermute | solution.py:442
  150.7 1.9 %collective-permute-start.15 = (f32[32,128]{1,0:T(8,128)S(1)}, f32[32,128]{1,0:T(8,128)S(1)}, u32[]{:S(2)}, u32[]{:S(2)}) collective-permute-start(f32[32,128]{1,0:T(8,128)S(1)} %get-tuple-element.70), channel_id=1, source_target_pairs={{0,504},{8,16},{16,8},{24,32},{32,24},{40,48},{48,40},{56,64},{64,... | collective-permute-start | bytes 49160 | tf_op jit(solution)/shard_map/ppermute | solution.py:443
  152.6 3.1 %collective-permute-done.15.gx2 = f32[32,128]{1,0:T(8,128)S(1)} collective-permute-done((f32[32,128]{1,0:T(8,128)S(1)}, f32[32,128]{1,0:T(8,128)S(1)}, u32[]{:S(2)}, u32[]{:S(2)}) %collective-permute-start.15) | collective-permute-done | bytes 16416 | tf_op jit(solution)/shard_map/ppermute | solution.py:443
  155.8 8.2 %force.1 = (f32[8,768]{1,0:T(8,128)S(1)}, f32[8,192]{1,0:T(8,128)S(1)}, f32[8,192]{1,0:T(8,128)S(1)}) custom-call(s32[2]{0:T(128)S(1)} %pad_add_fusion.par.refs_0_, f32[32,512]{1,0:T(8,128)S(1)} %get-tuple-element.68.own_in, f32[32,128]{1,0:T(8,128)S(1)} %collective-permute-done.14.gx1, f32[32,128]{1,0:T(8,128)S(1)} %collective-permute-done.15.gx2, ...), custom_call_target="tpu_custom_call" | custom-call | tf_op jit(solution)/shard_map/force/pallas_call | solution.py:419
  163.9 1.9 %collective-permute-start.16 = (f32[8,192]{1,0:T(8,128)S(1)}, f32[8,192]{1,0:T(8,128)S(1)}, u32[]{:S(2)}, u32[]{:S(2)}) collective-permute-start(f32[8,192]{1,0:T(8,128)S(1)} %get-tuple-element.74), channel_id=1, source_target_pairs={{0,1},{1,0},{2,3},{3,2},{4,5},{5,4},{6,7},{7,6},{8,9},{9,8},{10,11... | collective-permute-start | bytes 18440 | tf_op jit(solution)/shard_map/ppermute | solution.py:442
  165.9 5.0 %collective-permute-start.17 = (f32[8,192]{1,0:T(8,128)S(1)}, f32[8,192]{1,0:T(8,128)S(1)}, u32[]{:S(2)}, u32[]{:S(2)}) collective-permute-start(f32[8,192]{1,0:T(8,128)S(1)} %get-tuple-element.75), channel_id=1, source_target_pairs={{0,7},{1,2},{2,1},{3,4},{4,3},{5,6},{6,5},{7,0},{8,15},{9,10},{10,... | collective-permute-start | bytes 18440 | tf_op jit(solution)/shard_map/ppermute | solution.py:443
  170.9 2.9 %collective-permute-done.17.two_in = f32[8,192]{1,0:T(8,128)S(1)} collective-permute-done((f32[8,192]{1,0:T(8,128)S(1)}, f32[8,192]{1,0:T(8,128)S(1)}, u32[]{:S(2)}, u32[]{:S(2)}) %collective-permute-start.17) | collective-permute-done | bytes 6176 | tf_op jit(solution)/shard_map/ppermute | solution.py:443
  173.9 1.2 fold_force.1
  175.1 5.2 %collective-permute-start.18 = (f32[8,128]{1,0:T(8,128)S(1)}, f32[8,128]{1,0:T(8,128)S(1)}, u32[]{:S(2)}, u32[]{:S(2)}) collective-permute-start(f32[8,128]{1,0:T(8,128)S(1)} %get-tuple-element.77), channel_id=1, source_target_pairs={{0,8},{8,0},{16,24},{24,16},{32,40},{40,32},{48,56},{56,48},{64,72... | collective-permute-start | bytes 12296 | tf_op jit(solution)/shard_map/ppermute | solution.py:442
  180.3 1.9 %collective-permute-start.19 = (f32[8,128]{1,0:T(8,128)S(1)}, f32[8,128]{1,0:T(8,128)S(1)}, u32[]{:S(2)}, u32[]{:S(2)}) collective-permute-start(f32[8,128]{1,0:T(8,128)S(1)} %get-tuple-element.78), channel_id=1, source_target_pairs={{0,504},{8,16},{16,8},{24,32},{32,24},{40,48},{48,40},{56,64},{64,... | collective-permute-start | bytes 12296 | tf_op jit(solution)/shard_map/ppermute | solution.py:443
  182.3 3.0 %collective-permute-done.19.two = f32[8,128]{1,0:T(8,128)S(1)} collective-permute-done((f32[8,128]{1,0:T(8,128)S(1)}, f32[8,128]{1,0:T(8,128)S(1)}, u32[]{:S(2)}, u32[]{:S(2)}) %collective-permute-start.19) | collective-permute-done | bytes 4128 | tf_op jit(solution)/shard_map/ppermute | solution.py:443
  185.3 1.5 final.1
  (44 shorter events, 8.2 us)
Async XLA Ops:
  1.4 0.7 copy-start.11
  2.1 0.7 copy-start.12
  2.8 0.7 copy-start.13
  4.1 11.4 %collective-permute-start = (f32[8,128]{1,0:T(8,128)S(1)}, f32[8,128]{1,0:T(8,128)S(1)}, u32[]{:S(2)}, u32[]{:S(2)}) collective-permute-start(f32[8,128]{1,0:T(8,128)S(1)} %get-tuple-element.42), channel_id=1, source_target_pairs={{0,8},{8,0},{16,24},{24,16},{32,40},{40,32},{48,56},{56,48},{64,72... | collective-permute-start | bytes 12296 | tf_op jit(solution)/shard_map/ppermute | solution.py:442
  12.9 4.9 %collective-permute-start.1 = (f32[8,128]{1,0:T(8,128)S(1)}, f32[8,128]{1,0:T(8,128)S(1)}, u32[]{:S(2)}, u32[]{:S(2)}) collective-permute-start(f32[8,128]{1,0:T(8,128)S(1)} %get-tuple-element.43), channel_id=1, source_target_pairs={{0,504},{8,16},{16,8},{24,32},{32,24},{40,48},{48,40},{56,64},{64,... | collective-permute-start | bytes 12296 | tf_op jit(solution)/shard_map/ppermute | solution.py:443
  18.6 5.9 %collective-permute-start.2 = (f32[8,128]{1,0:T(8,128)S(1)}, f32[8,128]{1,0:T(8,128)S(1)}, u32[]{:S(2)}, u32[]{:S(2)}) collective-permute-start(f32[8,128]{1,0:T(8,128)S(1)} %get-tuple-element.45), channel_id=1, source_target_pairs={{0,1},{1,0},{2,3},{3,2},{4,5},{5,4},{6,7},{7,6},{8,9},{9,8},{10,11... | collective-permute-start | bytes 12296 | tf_op jit(solution)/shard_map/ppermute | solution.py:442
  20.5 8.0 %collective-permute-start.3 = (f32[8,128]{1,0:T(8,128)S(1)}, f32[8,128]{1,0:T(8,128)S(1)}, u32[]{:S(2)}, u32[]{:S(2)}) collective-permute-start(f32[8,128]{1,0:T(8,128)S(1)} %get-tuple-element.46), channel_id=1, source_target_pairs={{0,7},{1,2},{2,1},{3,4},{4,3},{5,6},{6,5},{7,0},{8,15},{9,10},{10,... | collective-permute-start | bytes 12296 | tf_op jit(solution)/shard_map/ppermute | solution.py:443
  28.5 0.7 copy-start.8
  29.9 11.9 %collective-permute-start.4 = (f32[8,128]{1,0:T(8,128)S(1)}, f32[8,128]{1,0:T(8,128)S(1)}, u32[]{:S(2)}, u32[]{:S(2)}) collective-permute-start(f32[8,128]{1,0:T(8,128)S(1)} %get-tuple-element.48), channel_id=1, source_target_pairs={{0,8},{8,0},{16,24},{24,16},{32,40},{40,32},{48,56},{56,48},{64,72... | collective-permute-start | bytes 12296 | tf_op jit(solution)/shard_map/ppermute | solution.py:442
  39.1 4.9 %collective-permute-start.5 = (f32[8,128]{1,0:T(8,128)S(1)}, f32[8,128]{1,0:T(8,128)S(1)}, u32[]{:S(2)}, u32[]{:S(2)}) collective-permute-start(f32[8,128]{1,0:T(8,128)S(1)} %get-tuple-element.49), channel_id=1, source_target_pairs={{0,504},{8,16},{16,8},{24,32},{32,24},{40,48},{48,40},{56,64},{64,... | collective-permute-start | bytes 12296 | tf_op jit(solution)/shard_map/ppermute | solution.py:443
  44.7 13.7 %collective-permute-start.6 = (f32[8,256]{1,0:T(8,128)S(1)}, f32[8,256]{1,0:T(8,128)S(1)}, u32[]{:S(2)}, u32[]{:S(2)}) collective-permute-start(f32[8,256]{1,0:T(8,128)S(1)} %get-tuple-element.50), channel_id=1, source_target_pairs={{0,1},{1,0},{2,3},{3,2},{4,5},{5,4},{6,7},{7,6},{8,9},{9,8},{10,11... | collective-permute-start | bytes 24584 | tf_op jit(solution)/shard_map/ppermute | solution.py:442
  46.7 11.7 %collective-permute-start.7 = (f32[8,256]{1,0:T(8,128)S(1)}, f32[8,256]{1,0:T(8,128)S(1)}, u32[]{:S(2)}, u32[]{:S(2)}) collective-permute-start(f32[8,256]{1,0:T(8,128)S(1)} %get-tuple-element.51), channel_id=1, source_target_pairs={{0,7},{1,2},{2,1},{3,4},{4,3},{5,6},{6,5},{7,0},{8,15},{9,10},{10,... | collective-permute-start | bytes 24584 | tf_op jit(solution)/shard_map/ppermute | solution.py:443
  52.8 0.7 copy-start.4
  53.5 0.8 copy-start.6
  54.2 0.7 copy-start.7
  55.0 0.7 copy-start.14
  55.7 0.7 copy-start.15
  56.3 0.7 copy-start.16
  57.0 0.7 copy-start.17
  58.4 0.8 copy-start.1
  59.2 0.7 copy-start.5
  60.0 0.7 copy-start.9
  76.2 6.5 %collective-permute-start.8 = (f32[32,128]{1,0:T(8,128)S(1)}, f32[32,128]{1,0:T(8,128)S(1)}, u32[]{:S(2)}, u32[]{:S(2)}) collective-permute-start(f32[32,128]{1,0:T(8,128)S(1)} %get-tuple-element.54), channel_id=1, source_target_pairs={{0,8},{8,0},{16,24},{24,16},{32,40},{40,32},{48,56},{56,48},{64,72... | collective-permute-start | bytes 49160 | tf_op jit(solution)/shard_map/ppermute | solution.py:442
  80.8 5.1 %collective-permute-start.9 = (f32[32,128]{1,0:T(8,128)S(1)}, f32[32,128]{1,0:T(8,128)S(1)}, u32[]{:S(2)}, u32[]{:S(2)}) collective-permute-start(f32[32,128]{1,0:T(8,128)S(1)} %get-tuple-element.55), channel_id=1, source_target_pairs={{0,504},{8,16},{16,8},{24,32},{32,24},{40,48},{48,40},{56,64},{64,... | collective-permute-start | bytes 49160 | tf_op jit(solution)/shard_map/ppermute | solution.py:443
  86.6 7.0 %collective-permute-start.10 = (f32[32,256]{1,0:T(8,128)S(1)}, f32[32,256]{1,0:T(8,128)S(1)}, u32[]{:S(2)}, u32[]{:S(2)}) collective-permute-start(f32[32,256]{1,0:T(8,128)S(1)} %get-tuple-element.56), channel_id=1, source_target_pairs={{0,1},{1,0},{2,3},{3,2},{4,5},{5,4},{6,7},{7,6},{8,9},{9,8},{10,11... | collective-permute-start | bytes 98312 | tf_op jit(solution)/shard_map/ppermute | solution.py:442
  88.5 8.3 %collective-permute-start.11 = (f32[32,256]{1,0:T(8,128)S(1)}, f32[32,256]{1,0:T(8,128)S(1)}, u32[]{:S(2)}, u32[]{:S(2)}) collective-permute-start(f32[32,256]{1,0:T(8,128)S(1)} %get-tuple-element.57), channel_id=1, source_target_pairs={{0,7},{1,2},{2,1},{3,4},{4,3},{5,6},{6,5},{7,0},{8,15},{9,10},{10,... | collective-permute-start | bytes 98312 | tf_op jit(solution)/shard_map/ppermute | solution.py:443
  96.8 0.8 copy-start.2
  97.6 58.1 %copy-start = (f32[32,64,512]{2,1,0:T(8,128)S(1)}, f32[32,64,512]{2,1,0:T(8,128)}, u32[]{:S(2)}) copy-start(f32[32,64,512]{2,1,0:T(8,128)} %get-tuple-element.60.slope) | copy-start | bytes 12582916
  97.6 58.1 %copy-start.3 = (s32[1,32,512]{2,1,0:T(8,128)S(1)}, s32[1,32,512]{2,1,0:T(8,128)}, u32[]{:S(2)}) copy-start(s32[1,32,512]{2,1,0:T(8,128)} %param.18) | copy-start | bytes 196612
  97.6 58.1 %copy-start.10 = (s32[1,2,128]{2,1,0:T(2,128)S(1)}, s32[1,2,128]{2,1,0:T(2,128)}, u32[]{:S(2)}) copy-start(s32[1,2,128]{2,1,0:T(2,128)} %param.19) | copy-start | bytes 3076
  130.5 7.0 %collective-permute-start.12 = (f32[32,192]{1,0:T(8,128)S(1)}, f32[32,192]{1,0:T(8,128)S(1)}, u32[]{:S(2)}, u32[]{:S(2)}) collective-permute-start(f32[32,192]{1,0:T(8,128)S(1)} %get-tuple-element.66), channel_id=1, source_target_pairs={{0,1},{1,0},{2,3},{3,2},{4,5},{5,4},{6,7},{7,6},{8,9},{9,8},{10,11... | collective-permute-start | bytes 73736 | tf_op jit(solution)/shard_map/ppermute | solution.py:442
  134.2 8.3 %collective-permute-start.13 = (f32[32,192]{1,0:T(8,128)S(1)}, f32[32,192]{1,0:T(8,128)S(1)}, u32[]{:S(2)}, u32[]{:S(2)}) collective-permute-start(f32[32,192]{1,0:T(8,128)S(1)} %get-tuple-element.67), channel_id=1, source_target_pairs={{0,7},{1,2},{2,1},{3,4},{4,3},{5,6},{6,5},{7,0},{8,15},{9,10},{10,... | collective-permute-start | bytes 73736 | tf_op jit(solution)/shard_map/ppermute | solution.py:443
  143.8 8.8 %collective-permute-start.14 = (f32[32,128]{1,0:T(8,128)S(1)}, f32[32,128]{1,0:T(8,128)S(1)}, u32[]{:S(2)}, u32[]{:S(2)}) collective-permute-start(f32[32,128]{1,0:T(8,128)S(1)} %get-tuple-element.69), channel_id=1, source_target_pairs={{0,8},{8,0},{16,24},{24,16},{32,40},{40,32},{48,56},{56,48},{64,72... | collective-permute-start | bytes 49160 | tf_op jit(solution)/shard_map/ppermute | solution.py:442
  150.7 5.1 %collective-permute-start.15 = (f32[32,128]{1,0:T(8,128)S(1)}, f32[32,128]{1,0:T(8,128)S(1)}, u32[]{:S(2)}, u32[]{:S(2)}) collective-permute-start(f32[32,128]{1,0:T(8,128)S(1)} %get-tuple-element.70), channel_id=1, source_target_pairs={{0,504},{8,16},{16,8},{24,32},{32,24},{40,48},{48,40},{56,64},{64,... | collective-permute-start | bytes 49160 | tf_op jit(solution)/shard_map/ppermute | solution.py:443
  163.9 7.0 %collective-permute-start.16 = (f32[8,192]{1,0:T(8,128)S(1)}, f32[8,192]{1,0:T(8,128)S(1)}, u32[]{:S(2)}, u32[]{:S(2)}) collective-permute-start(f32[8,192]{1,0:T(8,128)S(1)} %get-tuple-element.74), channel_id=1, source_target_pairs={{0,1},{1,0},{2,3},{3,2},{4,5},{5,4},{6,7},{7,6},{8,9},{9,8},{10,11... | collective-permute-start | bytes 18440 | tf_op jit(solution)/shard_map/ppermute | solution.py:442
  165.9 8.0 %collective-permute-start.17 = (f32[8,192]{1,0:T(8,128)S(1)}, f32[8,192]{1,0:T(8,128)S(1)}, u32[]{:S(2)}, u32[]{:S(2)}) collective-permute-start(f32[8,192]{1,0:T(8,128)S(1)} %get-tuple-element.75), channel_id=1, source_target_pairs={{0,7},{1,2},{2,1},{3,4},{4,3},{5,6},{6,5},{7,0},{8,15},{9,10},{10,... | collective-permute-start | bytes 18440 | tf_op jit(solution)/shard_map/ppermute | solution.py:443
  175.1 7.1 %collective-permute-start.18 = (f32[8,128]{1,0:T(8,128)S(1)}, f32[8,128]{1,0:T(8,128)S(1)}, u32[]{:S(2)}, u32[]{:S(2)}) collective-permute-start(f32[8,128]{1,0:T(8,128)S(1)} %get-tuple-element.77), channel_id=1, source_target_pairs={{0,8},{8,0},{16,24},{24,16},{32,40},{40,32},{48,56},{56,48},{64,72... | collective-permute-start | bytes 12296 | tf_op jit(solution)/shard_map/ppermute | solution.py:442
  180.3 4.9 %collective-permute-start.19 = (f32[8,128]{1,0:T(8,128)S(1)}, f32[8,128]{1,0:T(8,128)S(1)}, u32[]{:S(2)}, u32[]{:S(2)}) collective-permute-start(f32[8,128]{1,0:T(8,128)S(1)} %get-tuple-element.78), channel_id=1, source_target_pairs={{0,504},{8,16},{16,8},{24,32},{32,24},{40,48},{48,40},{56,64},{64,... | collective-permute-start | bytes 12296 | tf_op jit(solution)/shard_map/ppermute | solution.py:443

commit v2 on v1

--- a/solution.py
+++ b/solution.py
@@ -30,6 +30,10 @@
 HALF = 256
 LEVELS = -(-EXT // HALF)
 BIG = 48 * 1024 * 1024
+GROUP = 4
+CHUNK = 512
+UNROLL_ENV = 8
+UNROLL_FORCE = 4
 
 
 def half_split(value):
@@ -84,23 +88,49 @@
     return jnp.where(lax.broadcasted_iota(I32, (rows, 1), 0) == row, amount, 0.0)
 
 
-def place(bundle, slots, message):
-    lane = lax.broadcasted_iota(I32, bundle.shape, 1)
-    for k in range(MIG):
-        bundle = jnp.where(lane == slots[:, k : k + 1], message[:, k : k + 1], bundle)
-    return bundle
-
-
-def take_migrants(scratch, lists, row, first, second):
-    pair = []
-    for chosen, shift in (first, second):
-        pair.append(take_lanes(tile_reader(scratch), 8, OWN // LANES, chosen) + unit_row(8, row, shift))
-    return pair
+def place(record, slots, message, base):
+    lane = lax.broadcasted_iota(I32, record.shape, 1)
+    moved = record
+    for k in range(base, base + MIG):
+        moved = jnp.where(lane == slots[:, k : k + 1], message[:, k : k + 1], moved)
+    return jnp.where(lax.broadcasted_iota(I32, record.shape, 0) < 6, moved, record)
+
+
+def value_reader(value):
+    return lambda r, g: value[8 * r : 8 * r + 8, LANES * g : LANES * (g + 1)]
+
+
+def side_list(record, side):
+    return record[6:7, 2 * GX + LANES * side : 2 * GX + LANES * (side + 1)].astype(I32)
+
+
+def ghost_list(record, side):
+    return record[6:7, GX * side : GX * (side + 1)].astype(I32)
+
+
+def narrow_list(record, side):
+    return record[7:8, HALF * side : HALF * (side + 1)].astype(I32)
+
+
+def leavers(record, side, row):
+    shift = -1.0 if side == 0 else 1.0
+    return take_lanes(value_reader(record), 8, OWN // LANES, side_list(record, side)) + unit_row(8, row, shift)
+
+
+def fetch(sources, targets, sems):
+    copies = [pltpu.make_async_copy(src, dst, sems.at[k]) for k, (src, dst) in enumerate(zip(sources, targets))]
+    for copy in copies:
+        copy.start()
+    for copy in copies:
+        copy.wait()
 
 
 def prepare_kernel(
-    par, basis_t, pair, mix_t, w_embed, b_basis, b_pair, w_out, basis, ahead, back, w_back, columns
+    par, basis_t, pair, mix_t, w_embed, b_basis, b_pair, w_out, basis, ahead, back, w_back, columns, *scratch
 ):
+    held = scratch[:-1]
+    fetch((basis_t, pair, mix_t, w_embed, b_basis, b_pair, w_out), held, scratch[-1])
+    basis_t, pair, mix_t, w_embed, b_basis, b_pair, w_out = held
     high, low = half_split(basis_t[...])
     high, low = high.astype(F32), low.astype(F32)
     parts = [part.astype(F32) for part in third_split(b_basis[...])]
@@ -120,53 +150,97 @@
     ahead[H : 2 * H, :] = jnp.concatenate([low, nothing], axis=0).T.astype(BF16)
 
 
-def start_kernel(par, pos, vel, frc, mx, bundle_out, one, two):
+def start_kernel(par, pos, vel, frc, gx, gy, mx, my, record, message, gx_out, gy_out, *scratch):
+    held = scratch[:-1]
+    fetch((pos, vel, frc, gx, gy, mx, my), held, scratch[-1])
+    pos, vel, frc, gx, gy, mx, my = held
     speeds = vel[...] + (0.5 * TIME_STEP) * frc[...]
-    coords = pos[...] + TIME_STEP * speeds
-    bundle_out[0:3, :] = coords
-    bundle_out[3:6, :] = speeds
-    bundle_out[6:8, :] = jnp.zeros((2, OWN), F32)
+    record[0:3, :] = pos[...] + TIME_STEP * speeds
+    record[3:6, :] = speeds
+    record[6:8, :] = jnp.zeros((2, OWN), F32)
+    gy_out[...] = jnp.zeros((2, HALF), I32)
+    gx_out[...] = gx[0]
+    gy_out[:, 0:GY] = gy[0]
+    for side in range(2):
+        start = 2 * GX + LANES * side
+        record[6:7, GX * side : GX * (side + 1)] = gx[0, side : side + 1, :].astype(F32)
+        record[6:7, start : start + MIG] = mx[0, side : side + 1, :].astype(F32)
+        record[6:7, start + MIG : start + 2 * MIG] = my[0, side : side + 1, :].astype(F32)
+        record[7:8, HALF * side : HALF * side + GY] = gy[0, side : side + 1, :].astype(F32)
+    whole = record[...]
+    message[...] = by_parity(par[0], leavers(whole, 0, 0), leavers(whole, 1, 0))
+
+
+def cross_kernel(par, record, message, joined, out):
     p = par[0]
-    first = (by_parity(p, mx[0:1, :], mx[1:2, :]), by_parity(p, -1.0, 1.0))
-    second = (by_parity(p, mx[1:2, :], mx[0:1, :]), by_parity(p, 1.0, -1.0))
-    one[...], two[...] = take_migrants(bundle_out, mx, 0, first, second)
-
-
-def arrive(bundle, par, p_index, lists, one, two):
-    p = par[p_index]
-    from_lower = by_parity(p, two[...], one[...])
-    from_upper = by_parity(p, one[...], two[...])
-    bundle = place(bundle, lists[1:2, :], from_lower)
-    return place(bundle, lists[0:1, :], from_upper)
-
-
-def cross_kernel(par, bundle, one_in, two_in, mx, my, bundle_out, one, two):
-    bundle_out[...] = arrive(bundle[...], par, 0, mx, one_in, two_in)
+    own = record[...]
+    other = joined[:, 0:OWN]
+    mine = message[...]
+    theirs = joined[:, OWN : OWN + LANES]
+    low = by_parity(p, other, own)
+    high = by_parity(p, own, other)
+    from_below = by_parity(p, theirs, mine)
+    from_above = by_parity(p, mine, theirs)
+    new_low = place(low, side_list(low, 1), from_below, 0)
+    new_low = place(new_low, side_list(low, 0), leavers(high, 1, 0), 0)
+    new_high = place(high, side_list(high, 1), leavers(low, 0, 0), 0)
+    new_high = place(new_high, side_list(high, 0), from_above, 0)
+    for b in range(out.shape[0]):
+        out[b, 0:8, :] = new_low
+        out[b, 8:16, :] = new_high
+
+
+def settle(par, records, narrow_count, bundle, table, inner):
+    p = par[0]
+
+    def record_of(long_step, narrow_step):
+        number = p + 1 + long_step
+        column = lax.rem(par[2] + (narrow_step + narrow_count), narrow_count)
+        return records[((number >> 1) * narrow_count + column) * 2 + (number & 1)]
+
+    def settled(long_step, narrow_step):
+        own = record_of(long_step, narrow_step)
+        moved = place(own, side_list(own, 1), leavers(record_of(long_step, narrow_step - 1), 0, 1), MIG)
+        return place(moved, side_list(own, 0), leavers(record_of(long_step, narrow_step + 1), 1, 1), MIG)
+
+    for narrow_step in (-1, 1, 0):
+        middle = settled(0, narrow_step)
+        low = settled(-1, narrow_step)
+        high = settled(1, narrow_step)
+        inner[:, 0:OWN] = middle
+        inner[:, OWN : OWN + GX] = (
+            take_lanes(value_reader(low), 8, OWN // LANES, ghost_list(low, 0)) + unit_row(8, 0, -1.0)
+        )
+        inner[:, OWN + GX : INNER] = (
+            take_lanes(value_reader(high), 8, OWN // LANES, ghost_list(high, 1)) + unit_row(8, 0, 1.0)
+        )
+        if narrow_step == 0:
+            bundle[...] = middle
+            table[:, 0:INNER] = inner[...]
+            continue
+        side = 0 if narrow_step < 0 else 1
+        chosen = narrow_list(middle, side)
+        taken = jnp.concatenate(
+            [
+                take_lanes(tile_reader(inner), 8, INNER // LANES, chosen[:, LANES * c : LANES * (c + 1)])
+                for c in range(2)
+            ],
+            axis=1,
+        )
+        base = INNER + GY * side
+        table[:, base : base + GY] = taken[:, 0:GY] + unit_row(8, 1, float(narrow_step))
+
+
+def narrow_messages(par, table, rows, gy, one, two):
     p = par[1]
-    first = (by_parity(p, my[0:1, :], my[1:2, :]), by_parity(p, -1.0, 1.0))
-    second = (by_parity(p, my[1:2, :], my[0:1, :]), by_parity(p, 1.0, -1.0))
-    one[...], two[...] = take_migrants(bundle_out, my, 1, first, second)
-
-
-def settle_kernel(par, bundle, one_in, two_in, my, gx, bundle_out, one, two):
-    bundle_out[...] = arrive(bundle[...], par, 1, my, one_in, two_in)
-    p = par[0]
-    first = (by_parity(p, gx[0:1, :], gx[1:2, :]), by_parity(p, -1.0, 1.0))
-    second = (by_parity(p, gx[1:2, :], gx[0:1, :]), by_parity(p, 1.0, -1.0))
-    one[...], two[...] = take_migrants(bundle_out, gx, 0, first, second)
-
-
-def narrow_messages(par, table, rows, gy, row, one, two):
-    p = par[1]
-    for out, chosen, shift in (
-        (one, by_parity(p, gy[0:1, :], gy[1:2, :]), by_parity(p, -1.0, 1.0)),
-        (two, by_parity(p, gy[1:2, :], gy[0:1, :]), by_parity(p, 1.0, -1.0)),
+    for out, chosen in (
+        (one, by_parity(p, gy[0:1, :], gy[1:2, :])),
+        (two, by_parity(p, gy[1:2, :], gy[0:1, :])),
     ):
         for c in range(2):
-            taken = take_lanes(tile_reader(table), rows, INNER // LANES, chosen[:, LANES * c : LANES * (c + 1)])
-            if row is not None:
-                taken = taken + unit_row(rows, row, shift)
-            out[:, LANES * c : LANES * (c + 1)] = taken
+            out[:, LANES * c : LANES * (c + 1)] = take_lanes(
+                tile_reader(table), rows, INNER // LANES, chosen[:, LANES * c : LANES * (c + 1)]
+            )
 
 
 def inner_table(par, own, one, two, table):
@@ -182,17 +256,19 @@
     table[:, INNER + GY : EXT] = by_parity(p, one[:, 0:GY], two[:, 0:GY])
 
 
-def ghost_kernel(shift_row, par, own, one_in, two_in, gy, one, two, table):
+def ghost_kernel(par, own, one_in, two_in, gy, one, two, table):
     inner_table(par, own[...], one_in, two_in, table)
-    narrow_messages(par, table, own.shape[0], gy, shift_row, one, two)
+    narrow_messages(par, table, own.shape[0], gy, one, two)
 
 
 def env_kernel(
-    par, own, gx1, gx2, gy1, gy2, nbr, basis, w_embed, gx,
-    embed, one, two, lat_high, lat_low, slope, geo, table, square,
+    narrow_count, par, records, neighbours, basis, w_embed, gx,
+    own, embed, one, two, lat_high, lat_low, slope, geo, nbr, table, square, inner, sem,
 ):
-    inner_table(par, own[...], gx1, gx2, table)
-    outer_table(par, gy1, gy2, table)
+    copy = pltpu.make_async_copy(neighbours.at[0], nbr, sem.at[0])
+    copy.start()
+    settle(par, records, narrow_count, own, table, inner)
+    copy.wait()
     for b in range(OWN // LANES):
         lanes = slice(LANES * b, LANES * (b + 1))
         for q in range(NEI // 8):
@@ -244,7 +320,7 @@
             lat_low[n, :, lanes] = low
             return gathered + latent
 
-        gathered = lax.fori_loop(0, NEI, turn, jnp.zeros((H, HALF), F32))
+        gathered = lax.fori_loop(0, NEI, turn, jnp.zeros((H, HALF), F32), unroll=UNROLL_ENV)
         environ = gathered * (1.0 / math.sqrt(NEI))
         embed[:, lanes] = jnp.dot(w_embed[...], environ, precision=HIGHEST, preferred_element_type=F32)
     p = par[0]
@@ -268,7 +344,7 @@
 
 def pair_kernel(
     par, own, gx1, gx2, gy1, gy2, nbr, lat_high, lat_low, slope, geo, ahead, back, columns,
-    rise, inner, one, two, table, spread_sum, own_sum, joined,
+    rise, inner, one, two, table, spread_sum, own_sum,
 ):
     inner_table(par, own[...], gx1, gx2, table)
     outer_table(par, gy1, gy2, table)
@@ -279,49 +355,64 @@
     bias = columns[:, 0:1]
     readout = columns[:, 1:2]
 
-    def turn(n, carry):
-        for half in range(OWN // HALF):
-            lanes = slice(HALF * half, HALF * (half + 1))
-            index = nbr[pl.ds(n, 1), lanes]
-            weight = geo[3, pl.ds(n, 1), lanes]
-            partner = jnp.concatenate(
-                [
-                    take_lanes(tile_reader(table), EMB, GROUPS, index[:, LANES * c : LANES * (c + 1)])
-                    for c in range(HALF // LANES)
-                ],
-                axis=1,
-            )
-            embed_own = own[:, lanes]
-            product_high, product_low = half_split(partner * embed_own)
-            right = jnp.concatenate(
-                [lat_high[n, :, lanes], product_high, lat_low[n, :, lanes], product_low], axis=0
-            )
-            sums = lax.dot_general(left, right, (((1,), (0,)), ((), ())), preferred_element_type=F32)
-            value = sums[:H] + sums[H:] + bias
-            gate = 0.5 * jnp.tanh(0.5 * value) + 0.5
-            hidden = value * gate
-            dvalue = (gate + hidden * (1.0 - gate)) * (readout * weight)
-            dhigh, dlow = half_split(dvalue)
-            sums = lax.dot_general(
-                right_back, jnp.concatenate([dhigh, dlow], axis=0), (((1,), (0,)), ((), ())),
-                preferred_element_type=F32,
-            )
-            total = sums[: H + EMB] + sums[H + EMB :]
-            dlatent = total[:H]
-            dproduct = total[H:]
-            dsum = dlatent * slope[n, :, lanes] - (weight * weight) * (hidden * readout)
-            rise[pl.ds(n, 1), lanes] = jnp.sum(dsum, axis=0, keepdims=True)
-            own_sum[:, lanes] = own_sum[:, lanes] + dproduct * partner
-            high, low = half_split(dproduct * embed_own)
-            joined[:, lanes] = jnp.concatenate([high, low], axis=0)
-        index = nbr[pl.ds(n, 1), :]
+    def row(ref, n, lanes):
+        return ref[pl.ds(n, 1), lanes]
+
+    def scatter(g, joined):
+        index = jnp.concatenate([nbr[pl.ds(GROUP * g + j, 1), :] for j in range(GROUP)], axis=1)
         spread_sum[...] += lax.dot_general(
-            level_rows(joined[...], index >> 8), hot_rows(index & (HALF - 1), OWN),
+            level_rows(joined, index >> 8), hot_rows(index & (HALF - 1), GROUP * OWN),
             (((1,), (1,)), ((), ())), preferred_element_type=F32,
         )
-        return carry
-
-    lax.fori_loop(0, NEI, turn, 0)
+
+    def chunk(n, lanes, width):
+        index = nbr[pl.ds(n, 1), lanes]
+        weight = geo[3, pl.ds(n, 1), lanes]
+        partner = jnp.concatenate(
+            [
+                take_lanes(tile_reader(table), EMB, GROUPS, index[:, LANES * c : LANES * (c + 1)])
+                for c in range(width // LANES)
+            ],
+            axis=1,
+        )
+        embed_own = own[:, lanes]
+        product_high, product_low = half_split(partner * embed_own)
+        right = jnp.concatenate(
+            [lat_high[n, :, lanes], product_high, lat_low[n, :, lanes], product_low], axis=0
+        )
+        sums = lax.dot_general(left, right, (((1,), (0,)), ((), ())), preferred_element_type=F32)
+        value = sums[:H] + sums[H:] + bias
+        gate = 0.5 * jnp.tanh(0.5 * value) + 0.5
+        hidden = value * gate
+        dvalue = (gate + hidden * (1.0 - gate)) * (readout * weight)
+        dhigh, dlow = half_split(dvalue)
+        sums = lax.dot_general(
+            right_back, jnp.concatenate([dhigh, dlow], axis=0), (((1,), (0,)), ((), ())),
+            preferred_element_type=F32,
+        )
+        total = sums[: H + EMB] + sums[H + EMB :]
+        dlatent = total[:H]
+        dproduct = total[H:]
+        dsum = dlatent * slope[n, :, lanes] - (weight * weight) * (hidden * readout)
+        rise[pl.ds(n, 1), lanes] = jnp.sum(dsum, axis=0, keepdims=True)
+        high, low = half_split(dproduct * embed_own)
+        return dproduct * partner, jnp.concatenate([high, low], axis=0)
+
+    def turn(g, joined):
+        scatter(jnp.maximum(g - 1, 0), joined)
+        pieces = {}
+        for part in range(OWN // CHUNK):
+            lanes = slice(CHUNK * part, CHUNK * (part + 1))
+            grown = own_sum[:, lanes]
+            for j in range(GROUP):
+                more, piece = chunk(GROUP * g + j, lanes, CHUNK)
+                grown = grown + more
+                pieces[j, part] = piece
+            own_sum[:, lanes] = grown
+        return jnp.concatenate([pieces[j, part] for j in range(GROUP) for part in range(OWN // CHUNK)], axis=1)
+
+    joined = lax.fori_loop(0, NEI // GROUP, turn, jnp.zeros((2 * EMB, GROUP * OWN), BF16))
+    scatter(NEI // GROUP - 1, joined)
     for k in range(LEVELS):
         base = 2 * EMB * k
         width = min(HALF, EXT - HALF * k)
@@ -396,7 +487,7 @@
         return carry
 
     pushes[...] = jnp.zeros(pushes.shape, F32)
-    lax.fori_loop(0, NEI, turn, 0)
+    lax.fori_loop(0, NEI, turn, 0, unroll=UNROLL_FORCE)
     table[...] = jnp.zeros(table.shape, F32)
     for k in range(LEVELS):
         width = min(HALF, EXT - HALF * k)
@@ -415,17 +506,23 @@
     frc_out[...] = forces
 
 
-def call(kernel, name, shapes, scratch, par, *operands):
+def call(kernel, name, shapes, scratch, par, *operands, far=(), limit=BIG):
+    specs = [pl.BlockSpec(memory_space=pl.ANY if k in far else pltpu.VMEM) for k in range(len(operands))]
     return pl.pallas_call(
         kernel,
         name=name,
         out_shape=[jax.ShapeDtypeStruct(shape, kind) for shape, kind in shapes],
-        in_specs=[pl.BlockSpec(memory_space=pltpu.SMEM)]
-        + [pl.BlockSpec(memory_space=pltpu.VMEM)] * len(operands),
+        in_specs=[pl.BlockSpec(memory_space=pltpu.SMEM)] + specs,
         out_specs=[pl.BlockSpec(memory_space=pltpu.VMEM)] * len(shapes),
-        scratch_shapes=[pltpu.VMEM(shape, kind) for shape, kind in scratch],
-        compiler_params=pltpu.CompilerParams(vmem_limit_bytes=BIG),
+        scratch_shapes=[
+            pltpu.SemaphoreType.DMA(shape) if kind is None else pltpu.VMEM(shape, kind) for shape, kind in scratch
+        ],
+        compiler_params=pltpu.CompilerParams(vmem_limit_bytes=limit),
     )(par, *operands)
+
+
+def holds(*arrays):
+    return [(a.shape, a.dtype) for a in arrays] + [((len(arrays),), None)]
 
 
 def swap(axis, first):
@@ -448,13 +545,21 @@
     positions, velocities, forces, neighbours, ghost_x, ghost_y, migrate_x, migrate_y,
     w_basis, b_basis, w_embed, w_pair, w_mix, b_pair, w_out,
 ):
-    par = jnp.stack([lax.axis_index("gx") % 2, lax.axis_index("gy") % 2]).astype(I32)
-    near = neighbours[0]
-    gx = ghost_x[0]
-    gy = jnp.pad(ghost_y[0], ((0, 0), (0, HALF - GY)))
-    mx = jnp.pad(migrate_x[0], ((0, 0), (0, LANES - MIG)))
-    my = jnp.pad(migrate_y[0], ((0, 0), (0, LANES - MIG)))
-
+    row = lax.axis_index("gx")
+    column = lax.axis_index("gy")
+    narrow_count = lax.axis_size("gy")
+    par = jnp.stack([row % 2, column % 2, column]).astype(I32)
+
+    tile = ((8, LANES), F32)
+    wide = ((8, OWN), F32)
+    given = (positions, velocities, forces, ghost_x, ghost_y, migrate_x, migrate_y)
+    record, message, gx, gy = call(
+        start_kernel, "start", [wide, tile, ((2, GX), I32), ((2, HALF), I32)], holds(*given), par, *given,
+        far=range(len(given)),
+    )
+    given = (
+        w_basis.T, w_pair, w_mix.T, w_embed, b_basis.reshape(1, H), b_pair.reshape(1, H), w_out.reshape(1, H),
+    )
     basis, ahead, back, w_back, columns = call(
         prepare_kernel,
         "prepare",
@@ -462,39 +567,30 @@
             ((H, 4 * NB), BF16), ((2 * H, 2 * (H + EMB)), BF16), ((2 * (H + EMB), 2 * H), BF16),
             ((H, EMB), F32), ((H, NB), F32),
         ],
-        [],
-        par, w_basis.T, w_pair, w_mix.T, w_embed,
-        b_basis.reshape(1, H), b_pair.reshape(1, H), w_out.reshape(1, H),
-    )
-
-    tile = ((8, LANES), F32)
-    wide = ((8, OWN), F32)
-    bundle, one, two = call(start_kernel, "start", [wide, tile, tile], [], par, positions, velocities, forces, mx)
-    one, two = exchange("gx", one, two)
-    bundle, one, two = call(cross_kernel, "cross", [wide, tile, tile], [], par, bundle, one, two, mx, my)
-    one, two = exchange("gy", one, two)
-    bundle, one, two = call(settle_kernel, "settle", [wide, tile, tile], [], par, bundle, one, two, my, gx)
-    px = exchange("gx", one, two)
-    message = ((8, HALF), F32)
-    one, two = call(
-        lambda *refs: ghost_kernel(1, *refs), "ghost", [message, message], [((8, INNER), F32)], par, bundle, *px, gy
-    )
-    py = exchange("gy", one, two)
-
-    embed, one, two, lat_high, lat_low, slope, geo = call(
-        env_kernel,
+        holds(*given), par, *given, far=range(len(given)),
+    )
+    message = lax.ppermute(message, "gx", swap("gx", True))
+    joined = lax.ppermute(jnp.concatenate([record, message], axis=1), "gx", swap("gx", False))
+    group = 2 * narrow_count
+    (records,) = call(cross_kernel, "cross", [((group, 16, OWN), F32)], [], par, record, message, joined)
+    members = [list(range(group * k, group * (k + 1))) for k in range(lax.axis_size("gx") // 2)]
+    records = lax.all_to_all(records, ("gx", "gy"), 0, 0, axis_index_groups=members)
+
+    bundle, embed, one, two, lat_high, lat_low, slope, geo, near = call(
+        lambda *refs: env_kernel(narrow_count, *refs),
         "env",
         [
-            ((EMB, OWN), F32), ((EMB, GX), F32), ((EMB, GX), F32),
+            wide, ((EMB, OWN), F32), ((EMB, GX), F32), ((EMB, GX), F32),
             ((NEI, H, OWN), BF16), ((NEI, H, OWN), BF16), ((NEI, H, OWN), F32), ((4, NEI, OWN), F32),
+            ((NEI, OWN), I32),
         ],
-        [((8, EXT), F32), ((NEI, OWN), F32)],
-        par, bundle, *px, *py, near, basis, w_embed, gx,
+        [((8, EXT), F32), ((NEI, OWN), F32), ((8, INNER), F32), ((1,), None)],
+        par, records.reshape(2 * group, 8, OWN), neighbours, basis, w_embed, gx, far=(1,),
     )
     ex = exchange("gx", one, two)
     message = ((EMB, HALF), F32)
     one, two = call(
-        lambda *refs: ghost_kernel(None, *refs), "ghost_embed", [message, message], [((EMB, INNER), F32)],
+        ghost_kernel, "ghost_embed", [message, message], [((EMB, INNER), F32)],
         par, embed, *ex, gy,
     )
     ey = exchange("gy", one, two)
@@ -504,7 +600,7 @@
         "pair",
         [((NEI, OWN), F32), ((EMB, INNER), F32), message, message],
         [
-            ((EMB, EXT), F32), ((LEVELS * 2 * EMB, HALF), F32), ((EMB, OWN), F32), ((2 * EMB, OWN), BF16),
+            ((EMB, EXT), F32), ((LEVELS * 2 * EMB, HALF), F32), ((EMB, OWN), F32),
         ],
         par, embed, *ex, *ey, near, lat_high, lat_low, slope, geo, ahead, back, columns,
     )

time: 188 us -> 146 us (0.78)
  Pallas kernels: 64.9 us -> 39.7 us
  starting transfers between devices: 77.1 us -> 63.9 us
    pallas_call x12 -> x10, Pallas kernels: 64.9 us -> 39.7 us  [call(): pl.pallas_call(kernel, name=name, out_shape=[jax.ShapeDtypeStruct(shape,...]
    ppermute x10 -> x6, starting transfers between devices: 46 us -> 24.4 us  [exchange(): lax.ppermute(one, axis, swap(axis, True))]
    ppermute x10 -> x6, starting transfers between devices: 31.1 us -> 18.7 us  [exchange(): lax.ppermute(two, axis, swap(axis, False))]
    ppermute x0 -> x2, starting transfers between devices: none -> 10.7 us  [the longest x1 8.79 us: on_device(): message = lax.ppermute(message, 'gx', swap('gx', True))]
    all_to_all x0 -> x1, starting transfers between devices: none -> 10.1 us  [on_device(): lax.all_to_all(records, ('gx', 'gy'), 0, 0, axis_index_groups=members)]
    ppermute x10 -> x6, waiting for transfers between devices: 29 us -> 20.8 us  [exchange(): lax.ppermute(two, axis, swap(axis, False))]
    all_to_all x0 -> x1, waiting for transfers between devices: none -> 4.4 us  [on_device(): lax.all_to_all(records, ('gx', 'gy'), 0, 0, axis_index_groups=members)]
    ppermute x0 -> x2, waiting for transfers between devices: none -> 3.97 us  [the longest x1 3.17 us: on_device(): lax.ppermute(jnp.concatenate([record, message], axis=1), 'gx', swap('gx',...]
  transfers between devices with their start and end apart: 20 -> 15, of which waited for: 10 -> 9; matrix products, arithmetic and copies ran while one was open for 1% -> 0% of each run, Pallas kernels for 0% -> 1%
where the time goes in v2:
time: 146 us; the launch traced here: 145 us
  starting transfers between devices  63.9 us (44%)
  Pallas kernels  39.7 us (27%)
  waiting for transfers between devices  29.2 us (20%)
  local copies, waits for them, and re-layouts  11.2 us (8%)
    pallas_call x10, Pallas kernels, call(): pl.pallas_call(kernel, name=name, out_shape=[jax.ShapeDtypeStruct(shape,...  39.7 us
    ppermute x6, starting transfers between devices, exchange(): lax.ppermute(one, axis, swap(axis, True))  24.4 us
    ppermute x6, waiting for transfers between devices, exchange(): lax.ppermute(two, axis, swap(axis, False))  20.8 us
    ppermute x6, starting transfers between devices, exchange(): lax.ppermute(two, axis, swap(axis, False))  18.7 us
    unnamed x34, local copies, waits for them, and re-layouts  11.2 us
    all_to_all x1, starting transfers between devices, on_device(): lax.all_to_all(records, ('gx', 'gy'), 0, 0, axis_index_groups=members)  10.1 us
    ppermute x1, starting transfers between devices, on_device(): message = lax.ppermute(message, 'gx', swap('gx', True))  8.79 us
    all_to_all x1, waiting for transfers between devices, on_device(): lax.all_to_all(records, ('gx', 'gy'), 0, 0, axis_index_groups=members)  4.4 us
  transfers between devices with their start and end apart: 15, of which 9 were waited for; matrix products, arithmetic and copies ran while one was open for 0% of the time, Pallas kernels for 1%

profile of v2, /device:TPU:1, one launch (start us, length us, event | category | flops | bytes accessed | tf_op | source)
XLA Modules:
  0.0 144.9 jit_solution(2111614857424799311)
XLA Ops:
  0.7 0.7 copy-done.6
  1.4 0.7 copy-done.7
  2.1 0.7 copy-done.8
  2.8 0.7 copy-done.10
  3.5 0.7 copy-done.11
  4.2 0.7 copy-done.12
  4.9 0.7 copy-done.13
  5.5 0.8 start.1
  6.4 8.8 %collective-permute-start = (f32[8,128]{1,0:T(8,128)S(1)}, f32[8,128]{1,0:T(8,128)S(1)}, u32[]{:S(2)}, u32[]{:S(2)}) collective-permute-start(f32[8,128]{1,0:T(8,128)S(1)} %get-tuple-element.37), channel_id=1, source_target_pairs={{0,8},{8,0},{16,24},{24,16},{32,40},{40,32},{48,56},{56,48},{64,72... | collective-permute-start | bytes 12296 | tf_op jit(solution)/shard_map/ppermute | solution.py:572
  15.2 0.8 collective-permute-done.message
  16.0 1.9 %collective-permute-start.1 = (f32[8,640]{1,0:T(8,128)S(1)}, f32[8,640]{1,0:T(8,128)S(1)}, u32[]{:S(2)}, u32[]{:S(2)}) collective-permute-start(f32[8,640]{1,0:T(8,128)S(1)} %pad_maximum_fusion), channel_id=1, source_target_pairs={{0,504},{8,16},{16,8},{24,32},{32,24},{40,48},{48,40},{56,64},{64,... | collective-permute-start | bytes 61448 | tf_op jit(solution)/shard_map/ppermute | solution.py:573
  17.9 3.2 %collective-permute-done.1.joined = f32[8,640]{1,0:T(8,128)S(1)} collective-permute-done((f32[8,640]{1,0:T(8,128)S(1)}, f32[8,640]{1,0:T(8,128)S(1)}, u32[]{:S(2)}, u32[]{:S(2)}) %collective-permute-start.1) | collective-permute-done | bytes 20512 | tf_op jit(solution)/shard_map/ppermute | solution.py:573
  21.1 1.6 %cross.1 = f32[16,16,512]{2,1,0:T(8,128)} custom-call(s32[3]{0:T(128)S(1)} %pad_add_fusion.par.refs_0_, f32[8,512]{1,0:T(8,128)S(1)} %get-tuple-element.36.record, f32[8,128]{1,0:T(8,128)S(1)} %collective-permute-done.message, f32[8,640]{1,0:T(8,128)S(1)} %collective-permute-done.1.joined), custom_call_target="tpu_custom_call" | custom-call | tf_op jit(solution)/shard_map/cross/pallas_call | solution.py:511
  22.7 10.1 %all-to-all-start = ((f32[16,16,512]{2,1,0:T(8,128)}), f32[16,16,512]{2,1,0:T(8,128)S(1)}, u32[]{:S(2)}, u32[]{:S(2)}) async-start(f32[16,16,512]{2,1,0:T(8,128)} %cross.1), calls=%async_computation | async-start | bytes 1048576 | tf_op jit(solution)/shard_map/all_to_all | solution.py:577
  32.8 0.7 copy-done.1
  33.5 0.8 copy-done.4
  34.2 0.7 copy-done.5
  34.9 0.7 copy-done.9
  35.6 0.7 copy-done.14
  37.6 0.9 prepare.1
  38.5 4.4 %all-to-all-done = f32[16,16,512]{2,1,0:T(8,128)S(1)} async-done(((f32[16,16,512]{2,1,0:T(8,128)}), f32[16,16,512]{2,1,0:T(8,128)S(1)}, u32[]{:S(2)}, u32[]{:S(2)}) %all-to-all-start) | async-done | bytes 524320 | tf_op jit(solution)/shard_map/all_to_all | solution.py:577
  42.9 0.7 copy-done.2
  43.6 0.8 copy-done.3
  44.5 9.0 %env.1 = (f32[8,512]{1,0:T(8,128)S(1)}, f32[32,512]{1,0:T(8,128)S(1)}, f32[32,128]{1,0:T(8,128)S(1)}, f32[32,128]{1,0:T(8,128)S(1)}, bf16[32,64,512]{2,1,0:T(8,1...) custom-call(s32[3]{0:T(128)S(1)} %pad_add_fusion.par.refs_0_, ...), custom_call_target="tpu_custom_call" | custom-call | tf_op jit(solution)/shard_map/env/pallas_call | solution.py:511
  53.5 3.5 %collective-permute-start.2 = (f32[32,128]{1,0:T(8,128)S(1)}, f32[32,128]{1,0:T(8,128)S(1)}, u32[]{:S(2)}, u32[]{:S(2)}) collective-permute-start(f32[32,128]{1,0:T(8,128)S(1)} %get-tuple-element.41), channel_id=1, source_target_pairs={{0,8},{8,0},{16,24},{24,16},{32,40},{40,32},{48,56},{56,48},{64,72... | collective-permute-start | bytes 49160 | tf_op jit(solution)/shard_map/ppermute | solution.py:539
  57.0 1.9 %collective-permute-start.3 = (f32[32,128]{1,0:T(8,128)S(1)}, f32[32,128]{1,0:T(8,128)S(1)}, u32[]{:S(2)}, u32[]{:S(2)}) collective-permute-start(f32[32,128]{1,0:T(8,128)S(1)} %get-tuple-element.42), channel_id=1, source_target_pairs={{0,504},{8,16},{16,8},{24,32},{32,24},{40,48},{48,40},{56,64},{64,... | collective-permute-start | bytes 49160 | tf_op jit(solution)/shard_map/ppermute | solution.py:540
  59.0 3.1 %collective-permute-done.3.two_in.gx2 = f32[32,128]{1,0:T(8,128)S(1)} collective-permute-done((f32[32,128]{1,0:T(8,128)S(1)}, f32[32,128]{1,0:T(8,128)S(1)}, u32[]{:S(2)}, u32[]{:S(2)}) %collective-permute-start.3) | collective-permute-done | bytes 16416 | tf_op jit(solution)/shard_map/ppermute | solution.py:540
  62.1 0.7 ghost_embed.1
  62.8 2.8 %collective-permute-start.4 = (f32[32,256]{1,0:T(8,128)S(1)}, f32[32,256]{1,0:T(8,128)S(1)}, u32[]{:S(2)}, u32[]{:S(2)}) collective-permute-start(f32[32,256]{1,0:T(8,128)S(1)} %get-tuple-element.44), channel_id=1, source_target_pairs={{0,1},{1,0},{2,3},{3,2},{4,5},{5,4},{6,7},{7,6},{8,9},{9,8},{10,11... | collective-permute-start | bytes 98312 | tf_op jit(solution)/shard_map/ppermute | solution.py:539
  65.6 4.6 %collective-permute-start.5 = (f32[32,256]{1,0:T(8,128)S(1)}, f32[32,256]{1,0:T(8,128)S(1)}, u32[]{:S(2)}, u32[]{:S(2)}) collective-permute-start(f32[32,256]{1,0:T(8,128)S(1)} %get-tuple-element.45), channel_id=1, source_target_pairs={{0,7},{1,2},{2,1},{3,4},{4,3},{5,6},{6,5},{7,0},{8,15},{9,10},{10,... | collective-permute-start | bytes 98312 | tf_op jit(solution)/shard_map/ppermute | solution.py:540
  70.3 3.6 %collective-permute-done.5.gy2 = f32[32,256]{1,0:T(8,128)S(1)} collective-permute-done((f32[32,256]{1,0:T(8,128)S(1)}, f32[32,256]{1,0:T(8,128)S(1)}, u32[]{:S(2)}, u32[]{:S(2)}) %collective-permute-start.5) | collective-permute-done | bytes 32800 | tf_op jit(solution)/shard_map/ppermute | solution.py:540
  73.9 17.1 %pair.3 = (f32[32,512]{1,0:T(8,128)S(1)}, f32[32,768]{1,0:T(8,128)S(1)}, f32[32,192]{1,0:T(8,128)S(1)}, f32[32,192]{1,0:T(8,128)S(1)}) custom-call(s32[3]{0:T(128)S(1)} %pad_add_fusion.par.refs_0_, f32[32,512]{1,0:T(8,128)S(1)} %get-tuple-element.40.own, f32[32,128]{1,0:T(8,128)S(1)} %collective-permute-done.2.one_in.gx1, ...), custom_call_target="tpu_custom_call" | custom-call | tf_op jit(solution)/shard_map/pair/pallas_call | solution.py:511
  91.1 2.8 %collective-permute-start.6 = (f32[32,192]{1,0:T(8,128)S(1)}, f32[32,192]{1,0:T(8,128)S(1)}, u32[]{:S(2)}, u32[]{:S(2)}) collective-permute-start(f32[32,192]{1,0:T(8,128)S(1)} %get-tuple-element.55), channel_id=1, source_target_pairs={{0,1},{1,0},{2,3},{3,2},{4,5},{5,4},{6,7},{7,6},{8,9},{9,8},{10,11... | collective-permute-start | bytes 73736 | tf_op jit(solution)/shard_map/ppermute | solution.py:539
  93.9 3.8 %collective-permute-start.7 = (f32[32,192]{1,0:T(8,128)S(1)}, f32[32,192]{1,0:T(8,128)S(1)}, u32[]{:S(2)}, u32[]{:S(2)}) collective-permute-start(f32[32,192]{1,0:T(8,128)S(1)} %get-tuple-element.56), channel_id=1, source_target_pairs={{0,7},{1,2},{2,1},{3,4},{4,3},{5,6},{6,5},{7,0},{8,15},{9,10},{10,... | collective-permute-start | bytes 73736 | tf_op jit(solution)/shard_map/ppermute | solution.py:540
  97.6 4.5 %collective-permute-done.7.two_in = f32[32,192]{1,0:T(8,128)S(1)} collective-permute-done((f32[32,192]{1,0:T(8,128)S(1)}, f32[32,192]{1,0:T(8,128)S(1)}, u32[]{:S(2)}, u32[]{:S(2)}) %collective-permute-start.7) | collective-permute-done | bytes 24608 | tf_op jit(solution)/shard_map/ppermute | solution.py:540
  102.1 1.3 fold_embed.1
  103.5 6.9 %collective-permute-start.8 = (f32[32,128]{1,0:T(8,128)S(1)}, f32[32,128]{1,0:T(8,128)S(1)}, u32[]{:S(2)}, u32[]{:S(2)}) collective-permute-start(f32[32,128]{1,0:T(8,128)S(1)} %get-tuple-element.58), channel_id=1, source_target_pairs={{0,8},{8,0},{16,24},{24,16},{32,40},{40,32},{48,56},{56,48},{64,72... | collective-permute-start | bytes 49160 | tf_op jit(solution)/shard_map/ppermute | solution.py:539
  110.4 1.9 %collective-permute-start.9 = (f32[32,128]{1,0:T(8,128)S(1)}, f32[32,128]{1,0:T(8,128)S(1)}, u32[]{:S(2)}, u32[]{:S(2)}) collective-permute-start(f32[32,128]{1,0:T(8,128)S(1)} %get-tuple-element.59), channel_id=1, source_target_pairs={{0,504},{8,16},{16,8},{24,32},{32,24},{40,48},{48,40},{56,64},{64,... | collective-permute-start | bytes 49160 | tf_op jit(solution)/shard_map/ppermute | solution.py:540
  112.3 3.1 %collective-permute-done.9.gx2 = f32[32,128]{1,0:T(8,128)S(1)} collective-permute-done((f32[32,128]{1,0:T(8,128)S(1)}, f32[32,128]{1,0:T(8,128)S(1)}, u32[]{:S(2)}, u32[]{:S(2)}) %collective-permute-start.9) | collective-permute-done | bytes 16416 | tf_op jit(solution)/shard_map/ppermute | solution.py:540
  115.4 5.5 %force.1 = (f32[8,768]{1,0:T(8,128)S(1)}, f32[8,192]{1,0:T(8,128)S(1)}, f32[8,192]{1,0:T(8,128)S(1)}) custom-call(s32[3]{0:T(128)S(1)} %pad_add_fusion.par.refs_0_, f32[32,512]{1,0:T(8,128)S(1)} %get-tuple-element.57.own_in, f32[32,128]{1,0:T(8,128)S(1)} %collective-permute-done.8.gx1, f32[32,128]{1,0:T(8,128)S(1)} %collective-permute-done.9.gx2, ...), custom_call_target="tpu_custom_call" | custom-call | tf_op jit(solution)/shard_map/force/pallas_call | solution.py:511
  120.9 2.9 %collective-permute-start.10 = (f32[8,192]{1,0:T(8,128)S(1)}, f32[8,192]{1,0:T(8,128)S(1)}, u32[]{:S(2)}, u32[]{:S(2)}) collective-permute-start(f32[8,192]{1,0:T(8,128)S(1)} %get-tuple-element.63), channel_id=1, source_target_pairs={{0,1},{1,0},{2,3},{3,2},{4,5},{5,4},{6,7},{7,6},{8,9},{9,8},{10,11... | collective-permute-start | bytes 18440 | tf_op jit(solution)/shard_map/ppermute | solution.py:539
  123.8 4.5 %collective-permute-start.11 = (f32[8,192]{1,0:T(8,128)S(1)}, f32[8,192]{1,0:T(8,128)S(1)}, u32[]{:S(2)}, u32[]{:S(2)}) collective-permute-start(f32[8,192]{1,0:T(8,128)S(1)} %get-tuple-element.64), channel_id=1, source_target_pairs={{0,7},{1,2},{2,1},{3,4},{4,3},{5,6},{6,5},{7,0},{8,15},{9,10},{10,... | collective-permute-start | bytes 18440 | tf_op jit(solution)/shard_map/ppermute | solution.py:540
  128.3 3.5 %collective-permute-done.11.two_in = f32[8,192]{1,0:T(8,128)S(1)} collective-permute-done((f32[8,192]{1,0:T(8,128)S(1)}, f32[8,192]{1,0:T(8,128)S(1)}, u32[]{:S(2)}, u32[]{:S(2)}) %collective-permute-start.11) | collective-permute-done | bytes 6176 | tf_op jit(solution)/shard_map/ppermute | solution.py:540
  131.8 1.2 fold_force.1
  133.1 5.5 %collective-permute-start.12 = (f32[8,128]{1,0:T(8,128)S(1)}, f32[8,128]{1,0:T(8,128)S(1)}, u32[]{:S(2)}, u32[]{:S(2)}) collective-permute-start(f32[8,128]{1,0:T(8,128)S(1)} %get-tuple-element.66), channel_id=1, source_target_pairs={{0,8},{8,0},{16,24},{24,16},{32,40},{40,32},{48,56},{56,48},{64,72... | collective-permute-start | bytes 12296 | tf_op jit(solution)/shard_map/ppermute | solution.py:539
  138.5 1.9 %collective-permute-start.13 = (f32[8,128]{1,0:T(8,128)S(1)}, f32[8,128]{1,0:T(8,128)S(1)}, u32[]{:S(2)}, u32[]{:S(2)}) collective-permute-start(f32[8,128]{1,0:T(8,128)S(1)} %get-tuple-element.67), channel_id=1, source_target_pairs={{0,504},{8,16},{16,8},{24,32},{32,24},{40,48},{48,40},{56,64},{64,... | collective-permute-start | bytes 12296 | tf_op jit(solution)/shard_map/ppermute | solution.py:540
  140.5 3.0 %collective-permute-done.13.two = f32[8,128]{1,0:T(8,128)S(1)} collective-permute-done((f32[8,128]{1,0:T(8,128)S(1)}, f32[8,128]{1,0:T(8,128)S(1)}, u32[]{:S(2)}, u32[]{:S(2)}) %collective-permute-start.13) | collective-permute-done | bytes 4128 | tf_op jit(solution)/shard_map/ppermute | solution.py:540
  143.5 1.5 %final.1 = (f32[3,512]{1,0:T(4,128)}, f32[3,512]{1,0:T(4,128)}, f32[3,512]{1,0:T(4,128)}) custom-call(s32[3]{0:T(128)S(1)} %pad_add_fusion.par.refs_0_, f32[8,512]{1,0:T(8,128)S(1)} %get-tuple-element.65.own, f32[8,128]{1,0:T(8,128)S(1)} %collective-permute-done.12.one, f32[8,128]{1,0:T(8,128)S(1)} %collective-permute-done.13.two, ...), custom_call_target="tpu_custom_call" | custom-call | tf_op jit(solution)/shard_map/final/pallas_call | solution.py:511
  (28 shorter events, 1.4 us)
Async XLA Ops:
  0.7 0.7 copy-start.6
  1.4 0.7 copy-start.7
  2.1 0.7 copy-start.8
  2.8 0.7 copy-start.10
  3.5 0.7 copy-start.11
  4.2 0.7 copy-start.12
  4.9 0.7 copy-start.13
  6.4 9.6 %collective-permute-start = (f32[8,128]{1,0:T(8,128)S(1)}, f32[8,128]{1,0:T(8,128)S(1)}, u32[]{:S(2)}, u32[]{:S(2)}) collective-permute-start(f32[8,128]{1,0:T(8,128)S(1)} %get-tuple-element.37), channel_id=1, source_target_pairs={{0,8},{8,0},{16,24},{24,16},{32,40},{40,32},{48,56},{56,48},{64,72... | collective-permute-start | bytes 12296 | tf_op jit(solution)/shard_map/ppermute | solution.py:572
  16.0 5.1 %collective-permute-start.1 = (f32[8,640]{1,0:T(8,128)S(1)}, f32[8,640]{1,0:T(8,128)S(1)}, u32[]{:S(2)}, u32[]{:S(2)}) collective-permute-start(f32[8,640]{1,0:T(8,128)S(1)} %pad_maximum_fusion), channel_id=1, source_target_pairs={{0,504},{8,16},{16,8},{24,32},{32,24},{40,48},{48,40},{56,64},{64,... | collective-permute-start | bytes 61448 | tf_op jit(solution)/shard_map/ppermute | solution.py:573
  22.7 20.3 %all-to-all-start = ((f32[16,16,512]{2,1,0:T(8,128)}), f32[16,16,512]{2,1,0:T(8,128)S(1)}, u32[]{:S(2)}, u32[]{:S(2)}) async-start(f32[16,16,512]{2,1,0:T(8,128)} %cross.1), calls=%async_computation | async-start | bytes 1048576 | tf_op jit(solution)/shard_map/all_to_all | solution.py:577
  32.7 0.7 copy-start.1
  33.5 0.8 copy-start.4
  34.2 0.7 copy-start.5
  34.9 0.7 copy-start.9
  35.6 0.7 copy-start.14
  36.3 0.7 copy-start.15
  36.9 0.7 copy-start.16
  42.9 0.7 copy-start.2
  43.6 0.8 copy-start.3
  53.5 5.5 %collective-permute-start.2 = (f32[32,128]{1,0:T(8,128)S(1)}, f32[32,128]{1,0:T(8,128)S(1)}, u32[]{:S(2)}, u32[]{:S(2)}) collective-permute-start(f32[32,128]{1,0:T(8,128)S(1)} %get-tuple-element.41), channel_id=1, source_target_pairs={{0,8},{8,0},{16,24},{24,16},{32,40},{40,32},{48,56},{56,48},{64,72... | collective-permute-start | bytes 49160 | tf_op jit(solution)/shard_map/ppermute | solution.py:539
  57.0 5.1 %collective-permute-start.3 = (f32[32,128]{1,0:T(8,128)S(1)}, f32[32,128]{1,0:T(8,128)S(1)}, u32[]{:S(2)}, u32[]{:S(2)}) collective-permute-start(f32[32,128]{1,0:T(8,128)S(1)} %get-tuple-element.42), channel_id=1, source_target_pairs={{0,504},{8,16},{16,8},{24,32},{32,24},{40,48},{48,40},{56,64},{64,... | collective-permute-start | bytes 49160 | tf_op jit(solution)/shard_map/ppermute | solution.py:540
  62.8 7.4 %collective-permute-start.4 = (f32[32,256]{1,0:T(8,128)S(1)}, f32[32,256]{1,0:T(8,128)S(1)}, u32[]{:S(2)}, u32[]{:S(2)}) collective-permute-start(f32[32,256]{1,0:T(8,128)S(1)} %get-tuple-element.44), channel_id=1, source_target_pairs={{0,1},{1,0},{2,3},{3,2},{4,5},{5,4},{6,7},{7,6},{8,9},{9,8},{10,11... | collective-permute-start | bytes 98312 | tf_op jit(solution)/shard_map/ppermute | solution.py:539
  65.6 8.3 %collective-permute-start.5 = (f32[32,256]{1,0:T(8,128)S(1)}, f32[32,256]{1,0:T(8,128)S(1)}, u32[]{:S(2)}, u32[]{:S(2)}) collective-permute-start(f32[32,256]{1,0:T(8,128)S(1)} %get-tuple-element.45), channel_id=1, source_target_pairs={{0,7},{1,2},{2,1},{3,4},{4,3},{5,6},{6,5},{7,0},{8,15},{9,10},{10,... | collective-permute-start | bytes 98312 | tf_op jit(solution)/shard_map/ppermute | solution.py:540
  73.9 41.5 %copy-start = (f32[32,64,512]{2,1,0:T(8,128)S(1)}, f32[32,64,512]{2,1,0:T(8,128)}, u32[]{:S(2)}) copy-start(f32[32,64,512]{2,1,0:T(8,128)} %get-tuple-element.49.slope) | copy-start | bytes 12582916
  91.1 6.6 %collective-permute-start.6 = (f32[32,192]{1,0:T(8,128)S(1)}, f32[32,192]{1,0:T(8,128)S(1)}, u32[]{:S(2)}, u32[]{:S(2)}) collective-permute-start(f32[32,192]{1,0:T(8,128)S(1)} %get-tuple-element.55), channel_id=1, source_target_pairs={{0,1},{1,0},{2,3},{3,2},{4,5},{5,4},{6,7},{7,6},{8,9},{9,8},{10,11... | collective-permute-start | bytes 73736 | tf_op jit(solution)/shard_map/ppermute | solution.py:539
  93.9 8.3 %collective-permute-start.7 = (f32[32,192]{1,0:T(8,128)S(1)}, f32[32,192]{1,0:T(8,128)S(1)}, u32[]{:S(2)}, u32[]{:S(2)}) collective-permute-start(f32[32,192]{1,0:T(8,128)S(1)} %get-tuple-element.56), channel_id=1, source_target_pairs={{0,7},{1,2},{2,1},{3,4},{4,3},{5,6},{6,5},{7,0},{8,15},{9,10},{10,... | collective-permute-start | bytes 73736 | tf_op jit(solution)/shard_map/ppermute | solution.py:540
  103.5 8.8 %collective-permute-start.8 = (f32[32,128]{1,0:T(8,128)S(1)}, f32[32,128]{1,0:T(8,128)S(1)}, u32[]{:S(2)}, u32[]{:S(2)}) collective-permute-start(f32[32,128]{1,0:T(8,128)S(1)} %get-tuple-element.58), channel_id=1, source_target_pairs={{0,8},{8,0},{16,24},{24,16},{32,40},{40,32},{48,56},{56,48},{64,72... | collective-permute-start | bytes 49160 | tf_op jit(solution)/shard_map/ppermute | solution.py:539
  110.4 5.1 %collective-permute-start.9 = (f32[32,128]{1,0:T(8,128)S(1)}, f32[32,128]{1,0:T(8,128)S(1)}, u32[]{:S(2)}, u32[]{:S(2)}) collective-permute-start(f32[32,128]{1,0:T(8,128)S(1)} %get-tuple-element.59), channel_id=1, source_target_pairs={{0,504},{8,16},{16,8},{24,32},{32,24},{40,48},{48,40},{56,64},{64,... | collective-permute-start | bytes 49160 | tf_op jit(solution)/shard_map/ppermute | solution.py:540
  120.9 7.5 %collective-permute-start.10 = (f32[8,192]{1,0:T(8,128)S(1)}, f32[8,192]{1,0:T(8,128)S(1)}, u32[]{:S(2)}, u32[]{:S(2)}) collective-permute-start(f32[8,192]{1,0:T(8,128)S(1)} %get-tuple-element.63), channel_id=1, source_target_pairs={{0,1},{1,0},{2,3},{3,2},{4,5},{5,4},{6,7},{7,6},{8,9},{9,8},{10,11... | collective-permute-start | bytes 18440 | tf_op jit(solution)/shard_map/ppermute | solution.py:539
  123.8 8.0 %collective-permute-start.11 = (f32[8,192]{1,0:T(8,128)S(1)}, f32[8,192]{1,0:T(8,128)S(1)}, u32[]{:S(2)}, u32[]{:S(2)}) collective-permute-start(f32[8,192]{1,0:T(8,128)S(1)} %get-tuple-element.64), channel_id=1, source_target_pairs={{0,7},{1,2},{2,1},{3,4},{4,3},{5,6},{6,5},{7,0},{8,15},{9,10},{10,... | collective-permute-start | bytes 18440 | tf_op jit(solution)/shard_map/ppermute | solution.py:540
  133.1 7.4 %collective-permute-start.12 = (f32[8,128]{1,0:T(8,128)S(1)}, f32[8,128]{1,0:T(8,128)S(1)}, u32[]{:S(2)}, u32[]{:S(2)}) collective-permute-start(f32[8,128]{1,0:T(8,128)S(1)} %get-tuple-element.66), channel_id=1, source_target_pairs={{0,8},{8,0},{16,24},{24,16},{32,40},{40,32},{48,56},{56,48},{64,72... | collective-permute-start | bytes 12296 | tf_op jit(solution)/shard_map/ppermute | solution.py:539
  138.5 4.9 %collective-permute-start.13 = (f32[8,128]{1,0:T(8,128)S(1)}, f32[8,128]{1,0:T(8,128)S(1)}, u32[]{:S(2)}, u32[]{:S(2)}) collective-permute-start(f32[8,128]{1,0:T(8,128)S(1)} %get-tuple-element.67), channel_id=1, source_target_pairs={{0,504},{8,16},{16,8},{24,32},{32,24},{40,48},{48,40},{56,64},{64,... | collective-permute-start | bytes 12296 | tf_op jit(solution)/shard_map/ppermute | solution.py:540

commit v3 on v2

--- a/solution.py
+++ b/solution.py
@@ -29,11 +29,11 @@
 GROUPS = EXT // LANES
 HALF = 256
 LEVELS = -(-EXT // HALF)
-BIG = 48 * 1024 * 1024
+BIG = 24 * 1024 * 1024
+WHOLE = 60 * 1024 * 1024
 GROUP = 4
 CHUNK = 512
 UNROLL_ENV = 8
-UNROLL_FORCE = 4
 
 
 def half_split(value):
@@ -126,31 +126,34 @@
 
 
 def prepare_kernel(
-    par, basis_t, pair, mix_t, w_embed, b_basis, b_pair, w_out, basis, ahead, back, w_back, columns, *scratch
+    par, neighbours, basis_t, pair, mix_t, w_embed, vectors, near, basis, pair_ahead, mix_ahead, pair_back, mix_back, w_ahead, w_back, columns, *scratch
 ):
     held = scratch[:-1]
-    fetch((basis_t, pair, mix_t, w_embed, b_basis, b_pair, w_out), held, scratch[-1])
-    basis_t, pair, mix_t, w_embed, b_basis, b_pair, w_out = held
+    near[...] = neighbours[0]
+    fetch((basis_t, pair, mix_t, w_embed, vectors), held, scratch[-1])
+    basis_t, pair, mix_t, w_embed, vectors = held
+    b_basis = vectors[0:1, :]
     high, low = half_split(basis_t[...])
     high, low = high.astype(F32), low.astype(F32)
-    parts = [part.astype(F32) for part in third_split(b_basis[...])]
+    parts = [part.astype(F32) for part in third_split(b_basis)]
     parts = jnp.concatenate(parts + [jnp.zeros((NB - 3, H), F32)], axis=0)
     basis[...] = jnp.concatenate([high, high, low, parts], axis=0).T.astype(BF16)
-    rows = jnp.concatenate([b_pair[...], w_out[...], jnp.zeros((NB - 2, H), F32)], axis=0)
+    rows = jnp.concatenate([vectors[1:3, :], jnp.zeros((NB - 2, H), F32)], axis=0)
     columns[...] = rows.T
+    w_ahead[...] = w_embed[...]
     w_back[...] = w_embed[...].T
-    layer_t = jnp.concatenate([pair[...].T, mix_t[...]], axis=0)
-    high, low = half_split(layer_t)
-    high, low = high.astype(F32), low.astype(F32)
-    nothing = jnp.zeros((H + EMB, H), F32)
-    back[...] = jnp.concatenate(
-        [jnp.concatenate([high, high], axis=1), jnp.concatenate([low, nothing], axis=1)], axis=0
-    ).astype(BF16)
-    ahead[0:H, :] = jnp.concatenate([high, high], axis=0).T.astype(BF16)
-    ahead[H : 2 * H, :] = jnp.concatenate([low, nothing], axis=0).T.astype(BF16)
-
-
-def start_kernel(par, pos, vel, frc, gx, gy, mx, my, record, message, gx_out, gy_out, *scratch):
+    for layer_t, ahead, back in ((pair[...].T, pair_ahead, pair_back), (mix_t[...], mix_ahead, mix_back)):
+        high, low = half_split(layer_t)
+        high, low = high.astype(F32), low.astype(F32)
+        nothing = jnp.zeros(high.shape, F32)
+        back[...] = jnp.concatenate(
+            [jnp.concatenate([high, high], axis=1), jnp.concatenate([low, nothing], axis=1)], axis=0
+        ).astype(BF16)
+        ahead[0:H, :] = jnp.concatenate([high, high], axis=0).T.astype(BF16)
+        ahead[H : 2 * H, :] = jnp.concatenate([low, nothing], axis=0).T.astype(BF16)
+
+
+def start_kernel(par, pos, vel, frc, gx, gy, mx, my, record, message, *scratch):
     held = scratch[:-1]
     fetch((pos, vel, frc, gx, gy, mx, my), held, scratch[-1])
     pos, vel, frc, gx, gy, mx, my = held
@@ -158,9 +161,6 @@
     record[0:3, :] = pos[...] + TIME_STEP * speeds
     record[3:6, :] = speeds
     record[6:8, :] = jnp.zeros((2, OWN), F32)
-    gy_out[...] = jnp.zeros((2, HALF), I32)
-    gx_out[...] = gx[0]
-    gy_out[:, 0:GY] = gy[0]
     for side in range(2):
         start = 2 * GX + LANES * side
         record[6:7, GX * side : GX * (side + 1)] = gx[0, side : side + 1, :].astype(F32)
@@ -171,11 +171,11 @@
     message[...] = by_parity(par[0], leavers(whole, 0, 0), leavers(whole, 1, 0))
 
 
-def cross_kernel(par, record, message, joined, out):
+def cross_kernel(par, kept, joined, out):
     p = par[0]
-    own = record[...]
+    own = kept[:, 0:OWN]
     other = joined[:, 0:OWN]
-    mine = message[...]
+    mine = kept[:, OWN : OWN + LANES]
     theirs = joined[:, OWN : OWN + LANES]
     low = by_parity(p, other, own)
     high = by_parity(p, own, other)
@@ -261,14 +261,84 @@
     narrow_messages(par, table, own.shape[0], gy, one, two)
 
 
+def product(left, right):
+    return lax.dot_general(left, right, (((1,), (0,)), ((), ())), preferred_element_type=F32)
+
+
+def centres():
+    return lax.broadcasted_iota(I32, (NB, 1), 0).astype(F32) * (CENTRE_SPAN / (NB - 1))
+
+
+def basis_rows(radial, last):
+    high = radial.astype(BF16).astype(F32)
+    return jnp.concatenate([high, radial - high, high, last], axis=0)
+
+
+def slope_kernel(half, par, square, geo, basis, slope):
+    lanes = slice(HALF * half, HALF * (half + 1))
+    centre = centres()
+    ones = jnp.ones((NB, HALF), F32)
+    left = basis[...]
+
+    def turn(n, carry):
+        offset = square[pl.ds(n, 1), lanes] - centre
+        weight = geo[3, pl.ds(n, 1), lanes]
+        radial = jnp.exp(-(offset * offset))
+        right = [basis_rows(radial, ones), basis_rows(-2.0 * offset * radial, 0.0 * ones)]
+        both = product(left, jnp.concatenate(right, axis=1).astype(BF16))
+        value = both[:, :HALF]
+        gate = 0.5 * jnp.tanh(0.5 * value) + 0.5
+        raw = value * gate
+        slope[n] = weight * ((gate + raw * (1.0 - gate)) * both[:, HALF:] - raw * weight)
+        return carry
+
+    lax.fori_loop(0, NEI, turn, 0, unroll=UNROLL_ENV)
+
+
+def grouped(ref, g):
+    return jnp.concatenate([ref[GROUP * g + j] for j in range(GROUP)], axis=1)
+
+
+def first_kernel(par, latent, pair_ahead, columns, first):
+    left = pair_ahead[...]
+    bias = columns[:, 0:1]
+
+    def turn(g, carry):
+        sums = product(left, grouped(latent, g))
+        for j in range(GROUP):
+            lanes = slice(OWN * j, OWN * (j + 1))
+            first[GROUP * g + j] = sums[:H, lanes] + sums[H:, lanes] + bias
+        return carry
+
+    lax.fori_loop(0, NEI // GROUP, turn, 0)
+
+
+def rise_kernel(par, dvalue, part, slope1, slope2, pair_back, rise):
+    left = pair_back[...]
+
+    def turn(g, carry):
+        sums = product(left, grouped(dvalue, g))
+        for j in range(GROUP):
+            n = GROUP * g + j
+            for half, slope in enumerate((slope1, slope2)):
+                lanes = slice(HALF * half, HALF * (half + 1))
+                wide = slice(OWN * j + HALF * half, OWN * j + HALF * (half + 1))
+                dlatent = sums[:H, wide] + sums[H:, wide]
+                total = jnp.sum(dlatent * slope[n], axis=0, keepdims=True)
+                rise[pl.ds(n, 1), lanes] = total + part[pl.ds(n, 1), lanes]
+        return carry
+
+    lax.fori_loop(0, NEI // GROUP, turn, 0)
+
+
 def env_kernel(
-    narrow_count, par, records, neighbours, basis, w_embed, gx,
-    own, embed, one, two, lat_high, lat_low, slope, geo, nbr, table, square, inner, sem,
+    narrow_count, par, records, nbr, basis, w_embed,
+    own, gx, gy, embed, one, two, latent_out, geo, square, table, inner,
 ):
-    copy = pltpu.make_async_copy(neighbours.at[0], nbr, sem.at[0])
-    copy.start()
     settle(par, records, narrow_count, own, table, inner)
-    copy.wait()
+    for side in range(2):
+        gx[side : side + 1, :] = ghost_list(own, side)
+        gy[side : side + 1, :] = narrow_list(own, side)
     for b in range(OWN // LANES):
         lanes = slice(LANES * b, LANES * (b + 1))
         for q in range(NEI // 8):
@@ -288,7 +358,7 @@
             square[rows, lanes] = total
             geo[3, rows, lanes] = jnp.where(index >= 0, 1.0 / (1.0 + total), 0.0)
 
-    centre = lax.broadcasted_iota(I32, (NB, 1), 0).astype(F32) * (CENTRE_SPAN / (NB - 1))
+    centre = centres()
     ones = jnp.ones((NB, HALF), F32)
     left = basis[...]
     for half in range(OWN // HALF):
@@ -296,28 +366,12 @@
 
         def turn(n, gathered):
             offset = square[pl.ds(n, 1), lanes] - centre
-            weight = geo[3, pl.ds(n, 1), lanes]
-            radial = jnp.exp(-(offset * offset))
-            falling = -2.0 * offset * radial
-            radial_high = radial.astype(BF16).astype(F32)
-            falling_high = falling.astype(BF16).astype(F32)
-            right = jnp.concatenate(
-                [
-                    jnp.concatenate([radial_high, radial - radial_high, radial_high, ones], axis=0),
-                    jnp.concatenate([falling_high, falling - falling_high, falling_high, 0.0 * ones], axis=0),
-                ],
-                axis=1,
-            ).astype(BF16)
-            both = lax.dot_general(left, right, (((1,), (0,)), ((), ())), preferred_element_type=F32)
-            value = both[:, :HALF]
-            rate = both[:, HALF:]
+            value = product(left, basis_rows(jnp.exp(-(offset * offset)), ones).astype(BF16))
             gate = 0.5 * jnp.tanh(0.5 * value) + 0.5
-            raw = value * gate
-            latent = raw * weight
-            slope[n, :, lanes] = weight * ((gate + raw * (1.0 - gate)) * rate - latent)
+            latent = value * gate * geo[3, pl.ds(n, 1), lanes]
             high, low = half_split(latent)
-            lat_high[n, :, lanes] = high
-            lat_low[n, :, lanes] = low
+            latent_out[n, 0:H, lanes] = high
+            latent_out[n, H : 2 * H, lanes] = low
             return gathered + latent
 
         gathered = lax.fori_loop(0, NEI, turn, jnp.zeros((H, HALF), F32), unroll=UNROLL_ENV)
@@ -329,8 +383,8 @@
     two[...] = take_lanes(reader, EMB, OWN // LANES, by_parity(p, gx[1:2, :], gx[0:1, :]))
 
 
-def hot_rows(low_row, count):
-    level = lax.broadcasted_iota(I32, (HALF, count), 0)
+def hot_rows(low_row):
+    level = lax.broadcasted_iota(I32, (HALF, low_row.shape[1]), 0)
     return jnp.where(level == low_row, 1.0, 0.0).astype(BF16)
 
 
@@ -343,8 +397,8 @@
 
 
 def pair_kernel(
-    par, own, gx1, gx2, gy1, gy2, nbr, lat_high, lat_low, slope, geo, ahead, back, columns,
-    rise, inner, one, two, table, spread_sum, own_sum,
+    par, own, gx1, gx2, gy1, gy2, nbr, first, geo, ahead, back, columns,
+    dvalue_out, part, inner, one, two, table, spread_sum, own_sum,
 ):
     inner_table(par, own[...], gx1, gx2, table)
     outer_table(par, gy1, gy2, table)
@@ -352,16 +406,12 @@
     own_sum[...] = jnp.zeros(own_sum.shape, F32)
     left = ahead[...]
     right_back = back[...]
-    bias = columns[:, 0:1]
     readout = columns[:, 1:2]
-
-    def row(ref, n, lanes):
-        return ref[pl.ds(n, 1), lanes]
 
     def scatter(g, joined):
         index = jnp.concatenate([nbr[pl.ds(GROUP * g + j, 1), :] for j in range(GROUP)], axis=1)
         spread_sum[...] += lax.dot_general(
-            level_rows(joined, index >> 8), hot_rows(index & (HALF - 1), GROUP * OWN),
+            level_rows(joined, index >> 8), hot_rows(index & (HALF - 1)),
             (((1,), (1,)), ((), ())), preferred_element_type=F32,
         )
 
@@ -377,24 +427,17 @@
         )
         embed_own = own[:, lanes]
         product_high, product_low = half_split(partner * embed_own)
-        right = jnp.concatenate(
-            [lat_high[n, :, lanes], product_high, lat_low[n, :, lanes], product_low], axis=0
-        )
-        sums = lax.dot_general(left, right, (((1,), (0,)), ((), ())), preferred_element_type=F32)
-        value = sums[:H] + sums[H:] + bias
+        sums = product(left, jnp.concatenate([product_high, product_low], axis=0))
+        value = first[n, :, lanes] + sums[:H] + sums[H:]
         gate = 0.5 * jnp.tanh(0.5 * value) + 0.5
         hidden = value * gate
         dvalue = (gate + hidden * (1.0 - gate)) * (readout * weight)
         dhigh, dlow = half_split(dvalue)
-        sums = lax.dot_general(
-            right_back, jnp.concatenate([dhigh, dlow], axis=0), (((1,), (0,)), ((), ())),
-            preferred_element_type=F32,
-        )
-        total = sums[: H + EMB] + sums[H + EMB :]
-        dlatent = total[:H]
-        dproduct = total[H:]
-        dsum = dlatent * slope[n, :, lanes] - (weight * weight) * (hidden * readout)
-        rise[pl.ds(n, 1), lanes] = jnp.sum(dsum, axis=0, keepdims=True)
+        dvalue = jnp.concatenate([dhigh, dlow], axis=0)
+        dvalue_out[n, :, lanes] = dvalue
+        sums = product(right_back, dvalue)
+        dproduct = sums[:EMB] + sums[EMB:]
+        part[pl.ds(n, 1), lanes] = -(weight * weight) * jnp.sum(hidden * readout, axis=0, keepdims=True)
         high, low = half_split(dproduct * embed_own)
         return dproduct * partner, jnp.concatenate([high, low], axis=0)
 
@@ -461,33 +504,46 @@
 
 
 def force_kernel(
-    par, own_in, gx1, gx2, gx, w_back, slope, rise, geo, nbr, inner, one, two, table, spread_sum, pushes, grown,
+    par, own_in, gx1, gx2, gx, w_back, slope1, slope2, rise, geo, nbr,
+    inner, one, two, table, spread_sum, pushes, grown,
 ):
     grad = fold_long(par, own_in, gx1, gx2, gx)
     grown[...] = jnp.dot(w_back[...], grad, precision=HIGHEST, preferred_element_type=F32) * (1.0 / math.sqrt(NEI))
     spread_sum[...] = jnp.zeros(spread_sum.shape, F32)
-
-    def turn(n, carry):
-        rate = jnp.sum(slope[n] * grown[...], axis=0, keepdims=True) + rise[pl.ds(n, 1), :]
-        twice = 2.0 * rate
-        push = [geo[c, pl.ds(n, 1), :] * twice for c in range(3)]
-        highs = [v.astype(BF16).astype(F32) for v in push]
-        rows = highs + [v - h for v, h in zip(push, highs)]
-        empty = jnp.zeros((2, OWN), F32)
-        value = jnp.concatenate(rows + [empty], axis=0)
-        pushes[...] += value
-        index = nbr[pl.ds(n, 1), :]
-        high_row = index >> 8
-        lifted = jnp.concatenate(
-            [jnp.where(high_row == k, value, 0.0) for k in range(LEVELS)], axis=0
-        ).astype(BF16)
+    pushes[...] = jnp.zeros(pushes.shape, F32)
+
+    def turn(g, carry):
+        lifted = []
+        hot = []
+        pushed = pushes[...]
+        for j in range(GROUP):
+            n = GROUP * g + j
+            rate = jnp.concatenate(
+                [
+                    jnp.sum(slope[n] * grown[:, HALF * h : HALF * (h + 1)], axis=0, keepdims=True)
+                    for h, slope in enumerate((slope1, slope2))
+                ],
+                axis=1,
+            )
+            twice = 2.0 * (rate + rise[pl.ds(n, 1), :])
+            push = [geo[c, pl.ds(n, 1), :] * twice for c in range(3)]
+            highs = [v.astype(BF16).astype(F32) for v in push]
+            rows = highs + [v - h for v, h in zip(push, highs)]
+            value = jnp.concatenate(rows + [jnp.zeros((2, OWN), F32)], axis=0)
+            pushed = pushed + value
+            index = nbr[pl.ds(n, 1), :]
+            high_row = index >> 8
+            hot.append(hot_rows(index & (HALF - 1)))
+            lifted.append(
+                jnp.concatenate([jnp.where(high_row == k, value, 0.0) for k in range(LEVELS)], axis=0).astype(BF16)
+            )
+        pushes[...] = pushed
         spread_sum[...] += lax.dot_general(
-            lifted, hot_rows(index & (HALF - 1), OWN), (((1,), (1,)), ((), ())), preferred_element_type=F32
+            jnp.concatenate(lifted, axis=1), jnp.concatenate(hot, axis=1), (((1,), (1,)), ((), ())), preferred_element_type=F32
         )
         return carry
 
-    pushes[...] = jnp.zeros(pushes.shape, F32)
-    lax.fori_loop(0, NEI, turn, 0, unroll=UNROLL_FORCE)
+    lax.fori_loop(0, NEI // GROUP, turn, 0)
     table[...] = jnp.zeros(table.shape, F32)
     for k in range(LEVELS):
         width = min(HALF, EXT - HALF * k)
@@ -506,19 +562,24 @@
     frc_out[...] = forces
 
 
-def call(kernel, name, shapes, scratch, par, *operands, far=(), limit=BIG):
-    specs = [pl.BlockSpec(memory_space=pl.ANY if k in far else pltpu.VMEM) for k in range(len(operands))]
+def call(kernel, name, shapes, scratch, *operands, far=(), limit=BIG):
+    specs = [pl.BlockSpec(memory_space=pltpu.HBM if k in far else pltpu.VMEM) for k in range(len(operands))]
+
+    def placed(*refs):
+        column = lax.axis_index("gy")
+        kernel((lax.rem(lax.axis_index("gx"), 2), lax.rem(column, 2), column), *refs)
+
     return pl.pallas_call(
-        kernel,
+        placed,
         name=name,
         out_shape=[jax.ShapeDtypeStruct(shape, kind) for shape, kind in shapes],
-        in_specs=[pl.BlockSpec(memory_space=pltpu.SMEM)] + specs,
+        in_specs=specs,
         out_specs=[pl.BlockSpec(memory_space=pltpu.VMEM)] * len(shapes),
         scratch_shapes=[
             pltpu.SemaphoreType.DMA(shape) if kind is None else pltpu.VMEM(shape, kind) for shape, kind in scratch
         ],
         compiler_params=pltpu.CompilerParams(vmem_limit_bytes=limit),
-    )(par, *operands)
+    )(*operands)
 
 
 def holds(*arrays):
@@ -545,69 +606,75 @@
     positions, velocities, forces, neighbours, ghost_x, ghost_y, migrate_x, migrate_y,
     w_basis, b_basis, w_embed, w_pair, w_mix, b_pair, w_out,
 ):
-    row = lax.axis_index("gx")
-    column = lax.axis_index("gy")
     narrow_count = lax.axis_size("gy")
-    par = jnp.stack([row % 2, column % 2, column]).astype(I32)
-
     tile = ((8, LANES), F32)
     wide = ((8, OWN), F32)
     given = (positions, velocities, forces, ghost_x, ghost_y, migrate_x, migrate_y)
-    record, message, gx, gy = call(
-        start_kernel, "start", [wide, tile, ((2, GX), I32), ((2, HALF), I32)], holds(*given), par, *given,
-        far=range(len(given)),
+    record, message = call(
+        start_kernel, "start", [wide, tile], holds(*given), *given,
+        far=range(len(given)), limit=WHOLE,
     )
     given = (
-        w_basis.T, w_pair, w_mix.T, w_embed, b_basis.reshape(1, H), b_pair.reshape(1, H), w_out.reshape(1, H),
-    )
-    basis, ahead, back, w_back, columns = call(
+        w_basis.T, w_pair, w_mix.T, w_embed, jnp.stack([b_basis, b_pair, w_out]),
+    )
+    doubled = ((2 * H, 2 * H), BF16)
+    near, basis, pair_ahead, mix_ahead, pair_back, mix_back, w_ahead, w_back, columns = call(
         prepare_kernel,
         "prepare",
         [
-            ((H, 4 * NB), BF16), ((2 * H, 2 * (H + EMB)), BF16), ((2 * (H + EMB), 2 * H), BF16),
-            ((H, EMB), F32), ((H, NB), F32),
+            ((NEI, OWN), I32), ((H, 4 * NB), BF16), doubled, ((2 * H, 2 * EMB), BF16), doubled, ((2 * EMB, 2 * H), BF16),
+            ((EMB, H), F32), ((H, EMB), F32), ((H, NB), F32),
         ],
-        holds(*given), par, *given, far=range(len(given)),
+        holds(*given), neighbours, *given, far=range(1, len(given) + 1),
     )
     message = lax.ppermute(message, "gx", swap("gx", True))
-    joined = lax.ppermute(jnp.concatenate([record, message], axis=1), "gx", swap("gx", False))
+    mine = jnp.concatenate([record, message], axis=1)
+    joined = lax.ppermute(mine, "gx", swap("gx", False))
     group = 2 * narrow_count
-    (records,) = call(cross_kernel, "cross", [((group, 16, OWN), F32)], [], par, record, message, joined)
+    (records,) = call(cross_kernel, "cross", [((group, 16, OWN), F32)], [], mine, joined)
     members = [list(range(group * k, group * (k + 1))) for k in range(lax.axis_size("gx") // 2)]
     records = lax.all_to_all(records, ("gx", "gy"), 0, 0, axis_index_groups=members)
 
-    bundle, embed, one, two, lat_high, lat_low, slope, geo, near = call(
+    bundle, gx, gy, embed, one, two, latent, geo, square = call(
         lambda *refs: env_kernel(narrow_count, *refs),
         "env",
         [
-            wide, ((EMB, OWN), F32), ((EMB, GX), F32), ((EMB, GX), F32),
-            ((NEI, H, OWN), BF16), ((NEI, H, OWN), BF16), ((NEI, H, OWN), F32), ((4, NEI, OWN), F32),
-            ((NEI, OWN), I32),
+            wide, ((2, GX), I32), ((2, HALF), I32), ((EMB, OWN), F32), ((EMB, GX), F32), ((EMB, GX), F32),
+            ((NEI, 2 * H, OWN), BF16), ((4, NEI, OWN), F32), ((NEI, OWN), F32),
         ],
-        [((8, EXT), F32), ((NEI, OWN), F32), ((8, INNER), F32), ((1,), None)],
-        par, records.reshape(2 * group, 8, OWN), neighbours, basis, w_embed, gx, far=(1,),
-    )
+        [((8, EXT), F32), ((8, INNER), F32)],
+        records.reshape(2 * group, 8, OWN), near, basis, w_ahead,
+    )
+    (first,) = call(first_kernel, "first", [((NEI, H, OWN), F32)], [], latent, pair_ahead, columns)
+    slopes = [
+        call(
+            lambda *refs, half=half: slope_kernel(half, *refs), f"slope{half}", [((NEI, H, HALF), F32)], [],
+            square, geo, basis,
+        )[0]
+        for half in range(OWN // HALF)
+    ]
     ex = exchange("gx", one, two)
+    *ex, slopes[0] = lax.optimization_barrier((*ex, slopes[0]))
     message = ((EMB, HALF), F32)
     one, two = call(
         ghost_kernel, "ghost_embed", [message, message], [((EMB, INNER), F32)],
-        par, embed, *ex, gy,
+        embed, *ex, gy,
     )
     ey = exchange("gy", one, two)
     message = ((EMB, GY), F32)
-    rise, inner, one, two = call(
+    dvalue, part, inner, one, two = call(
         pair_kernel,
         "pair",
-        [((NEI, OWN), F32), ((EMB, INNER), F32), message, message],
-        [
-            ((EMB, EXT), F32), ((LEVELS * 2 * EMB, HALF), F32), ((EMB, OWN), F32),
-        ],
-        par, embed, *ex, *ey, near, lat_high, lat_low, slope, geo, ahead, back, columns,
+        [((NEI, 2 * H, OWN), BF16), ((NEI, OWN), F32), ((EMB, INNER), F32), message, message],
+        [((EMB, EXT), F32), ((LEVELS * 2 * EMB, HALF), F32), ((EMB, OWN), F32)],
+        embed, *ex, *ey, near, first, geo, mix_ahead, mix_back, columns,
     )
     one, two = exchange("gy", one, two)
+    one, two, slopes[1] = lax.optimization_barrier((one, two, slopes[1]))
+    (rise,) = call(rise_kernel, "rise", [((NEI, OWN), F32)], [], dvalue, part, *slopes, pair_back)
     message = ((EMB, GX), F32)
     own, one, two = call(
-        fold_kernel, "fold_embed", [((EMB, OWN), F32), message, message], [], par, inner, one, two, gy
+        fold_kernel, "fold_embed", [((EMB, OWN), F32), message, message], [], inner, one, two, gy
     )
     one, two = exchange("gx", one, two)
     message = ((8, GY), F32)
@@ -616,13 +683,13 @@
         "force",
         [((8, INNER), F32), message, message],
         [((8, EXT), F32), ((8 * LEVELS, HALF), F32), ((8, OWN), F32), ((H, OWN), F32)],
-        par, own, one, two, gx, w_back, slope, rise, geo, near,
+        own, one, two, gx, w_back, *slopes, rise, geo, near,
     )
     one, two = exchange("gy", one, two)
-    own, one, two = call(fold_kernel, "fold_force", [wide, tile, tile], [], par, inner, one, two, gy)
+    own, one, two = call(fold_kernel, "fold_force", [wide, tile, tile], [], inner, one, two, gy)
     one, two = exchange("gx", one, two)
     flat = ((3, OWN), F32)
-    return tuple(call(final_kernel, "final", [flat, flat, flat], [], par, own, one, two, gx, bundle))
+    return tuple(call(final_kernel, "final", [flat, flat, flat], [], own, one, two, gx, bundle))
 
 
 def solution(mesh):

time: 146 us -> 130 us (0.89)
  waiting for transfers between devices: 29.2 us -> 22.1 us
  local copies, waits for them, and re-layouts: 11.2 us -> 4.44 us
  Pallas kernels: 39.7 us -> 36.8 us
    ppermute x6, waiting for transfers between devices: 20.8 us -> 13.2 us  [exchange(): lax.ppermute(two, axis, swap(axis, False))]
    unnamed x34 -> x11, local copies, waits for them, and re-layouts: 11.2 us -> 4.44 us
    pallas_call x10 -> x14, Pallas kernels: 39.7 us -> 36.8 us  [call(): pl.pallas_call(placed, name=name, out_shape=[jax.ShapeDtypeStruct(shape,...]
  transfers between devices with their start and end apart: 15 -> 15, of which waited for: 9 -> 9; matrix products, arithmetic and copies ran while one was open for 0% -> 1% of each run, Pallas kernels for 1% -> 6%
where the time goes in v3:
time: 130 us; the launch traced here: 129 us
  starting transfers between devices  63.9 us (49%)
  Pallas kernels  36.8 us (28%)
  waiting for transfers between devices  22.1 us (17%)
  local copies, waits for them, and re-layouts  4.44 us (3%)
    pallas_call x14, Pallas kernels, call(): pl.pallas_call(placed, name=name, out_shape=[jax.ShapeDtypeStruct(shape,...  36.8 us
    ppermute x6, starting transfers between devices, exchange(): lax.ppermute(one, axis, swap(axis, True))  24.5 us
    ppermute x6, starting transfers between devices, exchange(): lax.ppermute(two, axis, swap(axis, False))  18.6 us
    ppermute x6, waiting for transfers between devices, exchange(): lax.ppermute(two, axis, swap(axis, False))  13.2 us
    all_to_all x1, starting transfers between devices, on_device(): lax.all_to_all(records, ('gx', 'gy'), 0, 0, axis_index_groups=members)  10.1 us
    ppermute x1, starting transfers between devices, on_device(): message = lax.ppermute(message, 'gx', swap('gx', True))  8.79 us
    all_to_all x1, waiting for transfers between devices, on_device(): lax.all_to_all(records, ('gx', 'gy'), 0, 0, axis_index_groups=members)  5.4 us
    unnamed x11, local copies, waits for them, and re-layouts  4.44 us
  transfers between devices with their start and end apart: 15, of which 9 were waited for; matrix products, arithmetic and copies ran while one was open for 1% of the time, Pallas kernels for 6%

profile of v3, /device:TPU:1, one launch (start us, length us, event | category | flops | bytes accessed | tf_op | source)
XLA Modules:
  0.0 128.8 jit_solution(6667969737205225345)
XLA Ops:
  0.6 1.6 %start.1 = (f32[8,512]{1,0:T(8,128)}, f32[8,128]{1,0:T(8,128)}) custom-call(f32[3,512]{1,0:T(4,128)} %refs_0_.2, f32[3,512]{1,0:T(4,128)} %refs_1_.1, f32[3,512]{1,0:T(4,128)} %refs_2_.2, s32[1,2,128]{2,1,0:T(2,128)} %refs_3_.1, s32[1,2,192]{2,1,0:T(2,128)} %refs_4_.2, s32[1,2,8]{2,1,0:T(2,128)} %refs_5_.1, s32[1,2,8]{2,1,0:T(2,128)} %refs_6_.1), custom_call_target="tpu_custom_call" | custom-call | tf_op jit(solution)/shard_map/start/pallas_call | solution.py:572
  2.2 8.8 %collective-permute-start = (f32[8,128]{1,0:T(8,128)}, f32[8,128]{1,0:T(8,128)S(1)}, u32[]{:S(2)}, u32[]{:S(2)}) collective-permute-start(f32[8,128]{1,0:T(8,128)} %get-tuple-element.46), channel_id=1, source_target_pairs={{0,8},{8,0},{16,24},{24,16},{32,40},{40,32},{48,56},{56,48},{64,72... | collective-permute-start | bytes 12296 | tf_op jit(solution)/shard_map/ppermute | solution.py:630
  11.0 0.7 constant_dynamic-update-slice_fusion.1
  11.8 0.3 collective-permute-done
  12.0 1.9 %collective-permute-start.1 = (f32[8,640]{1,0:T(8,128)S(1)}, f32[8,640]{1,0:T(8,128)S(1)}, u32[]{:S(2)}, u32[]{:S(2)}) collective-permute-start(f32[8,640]{1,0:T(8,128)S(1)} %constant_dynamic-update-slice_fusion.refs_0_), channel_id=1, source_target_pairs={{0,504},{8,16},{16,8},{24,32},{32,24},{40,48},{48,40},{56,64},{64,... | collective-permute-start | bytes 61448 | tf_op jit(solution)/shard_map/ppermute | solution.py:632
  14.0 3.2 %collective-permute-done.1.refs_1_ = f32[8,640]{1,0:T(8,128)S(1)} collective-permute-done((f32[8,640]{1,0:T(8,128)S(1)}, f32[8,640]{1,0:T(8,128)S(1)}, u32[]{:S(2)}, u32[]{:S(2)}) %collective-permute-start.1) | collective-permute-done | bytes 20512 | tf_op jit(solution)/shard_map/ppermute | solution.py:632
  17.1 1.1 cross.1
  18.2 10.1 %all-to-all-start = ((f32[16,16,512]{2,1,0:T(8,128)}), f32[16,16,512]{2,1,0:T(8,128)S(1)}, u32[]{:S(2)}, u32[]{:S(2)}) async-start(f32[16,16,512]{2,1,0:T(8,128)} %cross.1), calls=%async_computation | async-start | bytes 1048576 | tf_op jit(solution)/shard_map/all_to_all | solution.py:636
  28.3 0.7 pad_maximum_fusion.refs_5_
  29.0 0.8 copy-done
  29.8 0.8 copy-done.1
  30.6 0.7 copy-done.2
  31.3 0.7 copy-done.3
  32.0 0.7 copy-done.4
  32.7 0.4 prepare.1
  33.1 5.4 %all-to-all-done = f32[16,16,512]{2,1,0:T(8,128)S(1)} async-done(((f32[16,16,512]{2,1,0:T(8,128)}), f32[16,16,512]{2,1,0:T(8,128)S(1)}, u32[]{:S(2)}, u32[]{:S(2)}) %all-to-all-start) | async-done | bytes 524320 | tf_op jit(solution)/shard_map/all_to_all | solution.py:636
  38.5 5.8 %env.1 = (f32[8,512]{1,0:T(8,128)S(1)}, s32[2,128]{1,0:T(2,128)S(1)}, s32[2,256]{1,0:T(2,128)S(1)}, f32[32,512]{1,0:T(8,128)S(1)}, f32[32,128]{1,0:T(8,128)S(1)}...) custom-call(f32[32,8,512]{2,1,0:T(8,128)S(1)} %bitcast.6, ...), custom_call_target="tpu_custom_call" | custom-call | tf_op jit(solution)/shard_map/env/pallas_call | solution.py:572
  44.3 3.5 %collective-permute-start.2 = (f32[32,128]{1,0:T(8,128)S(1)}, f32[32,128]{1,0:T(8,128)S(1)}, u32[]{:S(2)}, u32[]{:S(2)}) collective-permute-start(f32[32,128]{1,0:T(8,128)S(1)} %get-tuple-element.51), channel_id=1, source_target_pairs={{0,8},{8,0},{16,24},{24,16},{32,40},{40,32},{48,56},{56,48},{64,72... | collective-permute-start | bytes 49160 | tf_op jit(solution)/shard_map/ppermute | solution.py:600
  47.8 1.9 %collective-permute-start.3 = (f32[32,128]{1,0:T(8,128)S(1)}, f32[32,128]{1,0:T(8,128)S(1)}, u32[]{:S(2)}, u32[]{:S(2)}) collective-permute-start(f32[32,128]{1,0:T(8,128)S(1)} %get-tuple-element.52), channel_id=1, source_target_pairs={{0,504},{8,16},{16,8},{24,32},{32,24},{40,48},{48,40},{56,64},{64,... | collective-permute-start | bytes 49160 | tf_op jit(solution)/shard_map/ppermute | solution.py:601
  49.7 1.5 %slope0.1.refs_2_.refs_5_ = f32[32,64,256]{2,1,0:T(8,128)S(1)} custom-call(f32[32,512]{1,0:T(8,128)S(1)} %get-tuple-element.53.refs_0_, f32[4,32,512]{2,1,0:T(8,128)S(1)} %get-tuple-element.54.refs_1_.refs_7_.refs_8_, bf16[64,32]{1,0:T(8,128)(2,1)S(1)} %get-tuple-element.48.refs_2_), custom_call_target="tpu_custom_call" | custom-call | tf_op jit(solution)/shard_map/slope0/pallas_call | solution.py:572
  51.2 0.0 collective-permute-done.2.refs_1_
  51.2 1.6 %collective-permute-done.3.refs_2_ = f32[32,128]{1,0:T(8,128)S(1)} collective-permute-done((f32[32,128]{1,0:T(8,128)S(1)}, f32[32,128]{1,0:T(8,128)S(1)}, u32[]{:S(2)}, u32[]{:S(2)}) %collective-permute-start.3) | collective-permute-done | bytes 16416 | tf_op jit(solution)/shard_map/ppermute | solution.py:601
  52.9 0.2 ghost_embed.1
  53.1 2.8 %collective-permute-start.4 = (f32[32,256]{1,0:T(8,128)S(1)}, f32[32,256]{1,0:T(8,128)S(1)}, u32[]{:S(2)}, u32[]{:S(2)}) collective-permute-start(f32[32,256]{1,0:T(8,128)S(1)} %get-tuple-element.58), channel_id=1, source_target_pairs={{0,1},{1,0},{2,3},{3,2},{4,5},{5,4},{6,7},{7,6},{8,9},{9,8},{10,11... | collective-permute-start | bytes 98312 | tf_op jit(solution)/shard_map/ppermute | solution.py:600
  55.9 4.6 %collective-permute-start.5 = (f32[32,256]{1,0:T(8,128)S(1)}, f32[32,256]{1,0:T(8,128)S(1)}, u32[]{:S(2)}, u32[]{:S(2)}) collective-permute-start(f32[32,256]{1,0:T(8,128)S(1)} %get-tuple-element.59), channel_id=1, source_target_pairs={{0,7},{1,2},{2,1},{3,4},{4,3},{5,6},{6,5},{7,0},{8,15},{9,10},{10,... | collective-permute-start | bytes 98312 | tf_op jit(solution)/shard_map/ppermute | solution.py:601
  60.5 2.3 %first.1.refs_6_ = f32[32,64,512]{2,1,0:T(8,128)S(1)} custom-call(bf16[32,128,512]{2,1,0:T(8,128)(2,1)S(1)} %get-tuple-element.60.refs_0_, bf16[128,128]{1,0:T(8,128)(2,1)S(1)} %get-tuple-element.61.refs_1_, f32[64,8]{1,0:T(8,128)S(1)} %get-tuple-element.62.refs_2_.refs_10_), custom_call_target="tpu_custom_call" | custom-call | tf_op jit(solution)/shard_map/first/pallas_call | solution.py:572
  62.8 0.0 collective-permute-done.4.refs_3_
  62.8 1.3 %collective-permute-done.5.refs_4_ = f32[32,256]{1,0:T(8,128)S(1)} collective-permute-done((f32[32,256]{1,0:T(8,128)S(1)}, f32[32,256]{1,0:T(8,128)S(1)}, u32[]{:S(2)}, u32[]{:S(2)}) %collective-permute-start.5) | collective-permute-done | bytes 32800 | tf_op jit(solution)/shard_map/ppermute | solution.py:601
  64.1 12.9 %pair.1 = (bf16[32,128,512]{2,1,0:T(8,128)(2,1)S(1)}, f32[32,512]{1,0:T(8,128)S(1)}, f32[32,768]{1,0:T(8,128)S(1)}, f32[32,192]{1,0:T(8,128)S(1)}, f32[32,192]{1,0:T(8,128)S(1)}) custom-call(f32[32,512]{1,0:T(8,128)S(1)} %get-tuple-element.50.refs_0_, f32[32,128]{1,0:T(8,128)S(1)} %collective-permute-done.2.refs_1_, ...), custom_call_target="tpu_custom_call" | custom-call | tf_op jit(solution)/shard_map/pair/pallas_call | solution.py:572
  77.1 2.8 %collective-permute-start.6 = (f32[32,192]{1,0:T(8,128)S(1)}, f32[32,192]{1,0:T(8,128)S(1)}, u32[]{:S(2)}, u32[]{:S(2)}) collective-permute-start(f32[32,192]{1,0:T(8,128)S(1)} %get-tuple-element.66), channel_id=1, source_target_pairs={{0,1},{1,0},{2,3},{3,2},{4,5},{5,4},{6,7},{7,6},{8,9},{9,8},{10,11... | collective-permute-start | bytes 73736 | tf_op jit(solution)/shard_map/ppermute | solution.py:600
  79.8 3.8 %collective-permute-start.7 = (f32[32,192]{1,0:T(8,128)S(1)}, f32[32,192]{1,0:T(8,128)S(1)}, u32[]{:S(2)}, u32[]{:S(2)}) collective-permute-start(f32[32,192]{1,0:T(8,128)S(1)} %get-tuple-element.67), channel_id=1, source_target_pairs={{0,7},{1,2},{2,1},{3,4},{4,3},{5,6},{6,5},{7,0},{8,15},{9,10},{10,... | collective-permute-start | bytes 73736 | tf_op jit(solution)/shard_map/ppermute | solution.py:601
  83.6 1.5 %slope1.1.refs_3_.refs_6_ = f32[32,64,256]{2,1,0:T(8,128)S(1)} custom-call(f32[32,512]{1,0:T(8,128)S(1)} %get-tuple-element.53.refs_0_, f32[4,32,512]{2,1,0:T(8,128)S(1)} %get-tuple-element.54.refs_1_.refs_7_.refs_8_, bf16[64,32]{1,0:T(8,128)(2,1)S(1)} %get-tuple-element.48.refs_2_), custom_call_target="tpu_custom_call" | custom-call | tf_op jit(solution)/shard_map/slope1/pallas_call | solution.py:572
  85.1 0.0 collective-permute-done.6.refs_1_
  85.1 3.0 %collective-permute-done.7.refs_2_ = f32[32,192]{1,0:T(8,128)S(1)} collective-permute-done((f32[32,192]{1,0:T(8,128)S(1)}, f32[32,192]{1,0:T(8,128)S(1)}, u32[]{:S(2)}, u32[]{:S(2)}) %collective-permute-start.7) | collective-permute-done | bytes 24608 | tf_op jit(solution)/shard_map/ppermute | solution.py:601
  88.1 0.8 fold_embed.1
  88.9 6.9 %collective-permute-start.8 = (f32[32,128]{1,0:T(8,128)S(1)}, f32[32,128]{1,0:T(8,128)S(1)}, u32[]{:S(2)}, u32[]{:S(2)}) collective-permute-start(f32[32,128]{1,0:T(8,128)S(1)} %get-tuple-element.71), channel_id=1, source_target_pairs={{0,8},{8,0},{16,24},{24,16},{32,40},{40,32},{48,56},{56,48},{64,72... | collective-permute-start | bytes 49160 | tf_op jit(solution)/shard_map/ppermute | solution.py:600
  95.8 1.9 %collective-permute-start.9 = (f32[32,128]{1,0:T(8,128)S(1)}, f32[32,128]{1,0:T(8,128)S(1)}, u32[]{:S(2)}, u32[]{:S(2)}) collective-permute-start(f32[32,128]{1,0:T(8,128)S(1)} %get-tuple-element.72), channel_id=1, source_target_pairs={{0,504},{8,16},{16,8},{24,32},{32,24},{40,48},{48,40},{56,64},{64,... | collective-permute-start | bytes 49160 | tf_op jit(solution)/shard_map/ppermute | solution.py:601
  97.7 2.4 %rise.1.refs_7_ = f32[32,512]{1,0:T(8,128)S(1)} custom-call(bf16[32,128,512]{2,1,0:T(8,128)(2,1)S(1)} %get-tuple-element.77.refs_0_, f32[32,512]{1,0:T(8,128)S(1)} %get-tuple-element.78.refs_1_, f32[32,64,256]{2,1,0:T(8,128)S(1)} %slope0.1.refs_2_.refs_5_, f32[32,64,256]{2,1,0:T(8,128)S(1)} %slope1.1.refs_3_.refs_6_, ...), custom_call_target="tpu_custom_call" | custom-call | tf_op jit(solution)/shard_map/rise/pallas_call | solution.py:572
  100.1 0.8 collective-permute-done.9.refs_2_
  100.9 4.9 %force.1 = (f32[8,768]{1,0:T(8,128)S(1)}, f32[8,192]{1,0:T(8,128)S(1)}, f32[8,192]{1,0:T(8,128)S(1)}) custom-call(f32[32,512]{1,0:T(8,128)S(1)} %get-tuple-element.70.refs_0_, f32[32,128]{1,0:T(8,128)S(1)} %collective-permute-done.8.refs_1_, f32[32,128]{1,0:T(8,128)S(1)} %collective-permute-done.9.refs_2_, s32[2,128]{1,0:T(2,128)S(1)} %get-tuple-element.73.refs_3_, ...), custom_call_target="tpu_custom_call" | custom-call | tf_op jit(solution)/shard_map/force/pallas_call | solution.py:572
  105.7 3.0 %collective-permute-start.10 = (f32[8,192]{1,0:T(8,128)S(1)}, f32[8,192]{1,0:T(8,128)S(1)}, u32[]{:S(2)}, u32[]{:S(2)}) collective-permute-start(f32[8,192]{1,0:T(8,128)S(1)} %get-tuple-element.81), channel_id=1, source_target_pairs={{0,1},{1,0},{2,3},{3,2},{4,5},{5,4},{6,7},{7,6},{8,9},{9,8},{10,11... | collective-permute-start | bytes 18440 | tf_op jit(solution)/shard_map/ppermute | solution.py:600
  108.8 4.4 %collective-permute-start.11 = (f32[8,192]{1,0:T(8,128)S(1)}, f32[8,192]{1,0:T(8,128)S(1)}, u32[]{:S(2)}, u32[]{:S(2)}) collective-permute-start(f32[8,192]{1,0:T(8,128)S(1)} %get-tuple-element.82), channel_id=1, source_target_pairs={{0,7},{1,2},{2,1},{3,4},{4,3},{5,6},{6,5},{7,0},{8,15},{9,10},{10,... | collective-permute-start | bytes 18440 | tf_op jit(solution)/shard_map/ppermute | solution.py:601
  113.2 3.6 %collective-permute-done.11.refs_2_ = f32[8,192]{1,0:T(8,128)S(1)} collective-permute-done((f32[8,192]{1,0:T(8,128)S(1)}, f32[8,192]{1,0:T(8,128)S(1)}, u32[]{:S(2)}, u32[]{:S(2)}) %collective-permute-start.11) | collective-permute-done | bytes 6176 | tf_op jit(solution)/shard_map/ppermute | solution.py:601
  116.8 0.7 fold_force.1
  117.5 5.5 %collective-permute-start.12 = (f32[8,128]{1,0:T(8,128)S(1)}, f32[8,128]{1,0:T(8,128)S(1)}, u32[]{:S(2)}, u32[]{:S(2)}) collective-permute-start(f32[8,128]{1,0:T(8,128)S(1)} %get-tuple-element.84), channel_id=1, source_target_pairs={{0,8},{8,0},{16,24},{24,16},{32,40},{40,32},{48,56},{56,48},{64,72... | collective-permute-start | bytes 12296 | tf_op jit(solution)/shard_map/ppermute | solution.py:600
  123.0 1.9 %collective-permute-start.13 = (f32[8,128]{1,0:T(8,128)S(1)}, f32[8,128]{1,0:T(8,128)S(1)}, u32[]{:S(2)}, u32[]{:S(2)}) collective-permute-start(f32[8,128]{1,0:T(8,128)S(1)} %get-tuple-element.85), channel_id=1, source_target_pairs={{0,504},{8,16},{16,8},{24,32},{32,24},{40,48},{48,40},{56,64},{64,... | collective-permute-start | bytes 12296 | tf_op jit(solution)/shard_map/ppermute | solution.py:601
  124.9 3.0 %collective-permute-done.13.refs_2_ = f32[8,128]{1,0:T(8,128)S(1)} collective-permute-done((f32[8,128]{1,0:T(8,128)S(1)}, f32[8,128]{1,0:T(8,128)S(1)}, u32[]{:S(2)}, u32[]{:S(2)}) %collective-permute-start.13) | collective-permute-done | bytes 4128 | tf_op jit(solution)/shard_map/ppermute | solution.py:601
  127.9 0.9 final.1
  (9 shorter events, 0.0 us)
Async XLA Ops:
  2.2 9.8 %collective-permute-start = (f32[8,128]{1,0:T(8,128)}, f32[8,128]{1,0:T(8,128)S(1)}, u32[]{:S(2)}, u32[]{:S(2)}) collective-permute-start(f32[8,128]{1,0:T(8,128)} %get-tuple-element.46), channel_id=1, source_target_pairs={{0,8},{8,0},{16,24},{24,16},{32,40},{40,32},{48,56},{56,48},{64,72... | collective-permute-start | bytes 12296 | tf_op jit(solution)/shard_map/ppermute | solution.py:630
  12.0 5.1 %collective-permute-start.1 = (f32[8,640]{1,0:T(8,128)S(1)}, f32[8,640]{1,0:T(8,128)S(1)}, u32[]{:S(2)}, u32[]{:S(2)}) collective-permute-start(f32[8,640]{1,0:T(8,128)S(1)} %constant_dynamic-update-slice_fusion.refs_0_), channel_id=1, source_target_pairs={{0,504},{8,16},{16,8},{24,32},{32,24},{40,48},{48,40},{56,64},{64,... | collective-permute-start | bytes 61448 | tf_op jit(solution)/shard_map/ppermute | solution.py:632
  18.2 20.3 %all-to-all-start = ((f32[16,16,512]{2,1,0:T(8,128)}), f32[16,16,512]{2,1,0:T(8,128)S(1)}, u32[]{:S(2)}, u32[]{:S(2)}) async-start(f32[16,16,512]{2,1,0:T(8,128)} %cross.1), calls=%async_computation | async-start | bytes 1048576 | tf_op jit(solution)/shard_map/all_to_all | solution.py:636
  29.0 0.8 copy-start
  29.8 0.8 copy-start.1
  30.6 0.7 copy-start.2
  31.3 0.7 copy-start.3
  32.0 0.7 copy-start.4
  44.3 7.0 %collective-permute-start.2 = (f32[32,128]{1,0:T(8,128)S(1)}, f32[32,128]{1,0:T(8,128)S(1)}, u32[]{:S(2)}, u32[]{:S(2)}) collective-permute-start(f32[32,128]{1,0:T(8,128)S(1)} %get-tuple-element.51), channel_id=1, source_target_pairs={{0,8},{8,0},{16,24},{24,16},{32,40},{40,32},{48,56},{56,48},{64,72... | collective-permute-start | bytes 49160 | tf_op jit(solution)/shard_map/ppermute | solution.py:600
  47.8 5.1 %collective-permute-start.3 = (f32[32,128]{1,0:T(8,128)S(1)}, f32[32,128]{1,0:T(8,128)S(1)}, u32[]{:S(2)}, u32[]{:S(2)}) collective-permute-start(f32[32,128]{1,0:T(8,128)S(1)} %get-tuple-element.52), channel_id=1, source_target_pairs={{0,504},{8,16},{16,8},{24,32},{32,24},{40,48},{48,40},{56,64},{64,... | collective-permute-start | bytes 49160 | tf_op jit(solution)/shard_map/ppermute | solution.py:601
  53.1 9.7 %collective-permute-start.4 = (f32[32,256]{1,0:T(8,128)S(1)}, f32[32,256]{1,0:T(8,128)S(1)}, u32[]{:S(2)}, u32[]{:S(2)}) collective-permute-start(f32[32,256]{1,0:T(8,128)S(1)} %get-tuple-element.58), channel_id=1, source_target_pairs={{0,1},{1,0},{2,3},{3,2},{4,5},{5,4},{6,7},{7,6},{8,9},{9,8},{10,11... | collective-permute-start | bytes 98312 | tf_op jit(solution)/shard_map/ppermute | solution.py:600
  55.9 8.3 %collective-permute-start.5 = (f32[32,256]{1,0:T(8,128)S(1)}, f32[32,256]{1,0:T(8,128)S(1)}, u32[]{:S(2)}, u32[]{:S(2)}) collective-permute-start(f32[32,256]{1,0:T(8,128)S(1)} %get-tuple-element.59), channel_id=1, source_target_pairs={{0,7},{1,2},{2,1},{3,4},{4,3},{5,6},{6,5},{7,0},{8,15},{9,10},{10,... | collective-permute-start | bytes 98312 | tf_op jit(solution)/shard_map/ppermute | solution.py:601
  77.1 8.1 %collective-permute-start.6 = (f32[32,192]{1,0:T(8,128)S(1)}, f32[32,192]{1,0:T(8,128)S(1)}, u32[]{:S(2)}, u32[]{:S(2)}) collective-permute-start(f32[32,192]{1,0:T(8,128)S(1)} %get-tuple-element.66), channel_id=1, source_target_pairs={{0,1},{1,0},{2,3},{3,2},{4,5},{5,4},{6,7},{7,6},{8,9},{9,8},{10,11... | collective-permute-start | bytes 73736 | tf_op jit(solution)/shard_map/ppermute | solution.py:600
  79.8 8.3 %collective-permute-start.7 = (f32[32,192]{1,0:T(8,128)S(1)}, f32[32,192]{1,0:T(8,128)S(1)}, u32[]{:S(2)}, u32[]{:S(2)}) collective-permute-start(f32[32,192]{1,0:T(8,128)S(1)} %get-tuple-element.67), channel_id=1, source_target_pairs={{0,7},{1,2},{2,1},{3,4},{4,3},{5,6},{6,5},{7,0},{8,15},{9,10},{10,... | collective-permute-start | bytes 73736 | tf_op jit(solution)/shard_map/ppermute | solution.py:601
  88.9 11.2 %collective-permute-start.8 = (f32[32,128]{1,0:T(8,128)S(1)}, f32[32,128]{1,0:T(8,128)S(1)}, u32[]{:S(2)}, u32[]{:S(2)}) collective-permute-start(f32[32,128]{1,0:T(8,128)S(1)} %get-tuple-element.71), channel_id=1, source_target_pairs={{0,8},{8,0},{16,24},{24,16},{32,40},{40,32},{48,56},{56,48},{64,72... | collective-permute-start | bytes 49160 | tf_op jit(solution)/shard_map/ppermute | solution.py:600
  95.8 5.1 %collective-permute-start.9 = (f32[32,128]{1,0:T(8,128)S(1)}, f32[32,128]{1,0:T(8,128)S(1)}, u32[]{:S(2)}, u32[]{:S(2)}) collective-permute-start(f32[32,128]{1,0:T(8,128)S(1)} %get-tuple-element.72), channel_id=1, source_target_pairs={{0,504},{8,16},{16,8},{24,32},{32,24},{40,48},{48,40},{56,64},{64,... | collective-permute-start | bytes 49160 | tf_op jit(solution)/shard_map/ppermute | solution.py:601
  105.7 7.4 %collective-permute-start.10 = (f32[8,192]{1,0:T(8,128)S(1)}, f32[8,192]{1,0:T(8,128)S(1)}, u32[]{:S(2)}, u32[]{:S(2)}) collective-permute-start(f32[8,192]{1,0:T(8,128)S(1)} %get-tuple-element.81), channel_id=1, source_target_pairs={{0,1},{1,0},{2,3},{3,2},{4,5},{5,4},{6,7},{7,6},{8,9},{9,8},{10,11... | collective-permute-start | bytes 18440 | tf_op jit(solution)/shard_map/ppermute | solution.py:600
  108.8 8.0 %collective-permute-start.11 = (f32[8,192]{1,0:T(8,128)S(1)}, f32[8,192]{1,0:T(8,128)S(1)}, u32[]{:S(2)}, u32[]{:S(2)}) collective-permute-start(f32[8,192]{1,0:T(8,128)S(1)} %get-tuple-element.82), channel_id=1, source_target_pairs={{0,7},{1,2},{2,1},{3,4},{4,3},{5,6},{6,5},{7,0},{8,15},{9,10},{10,... | collective-permute-start | bytes 18440 | tf_op jit(solution)/shard_map/ppermute | solution.py:601
  117.5 7.4 %collective-permute-start.12 = (f32[8,128]{1,0:T(8,128)S(1)}, f32[8,128]{1,0:T(8,128)S(1)}, u32[]{:S(2)}, u32[]{:S(2)}) collective-permute-start(f32[8,128]{1,0:T(8,128)S(1)} %get-tuple-element.84), channel_id=1, source_target_pairs={{0,8},{8,0},{16,24},{24,16},{32,40},{40,32},{48,56},{56,48},{64,72... | collective-permute-start | bytes 12296 | tf_op jit(solution)/shard_map/ppermute | solution.py:600
  123.0 4.9 %collective-permute-start.13 = (f32[8,128]{1,0:T(8,128)S(1)}, f32[8,128]{1,0:T(8,128)S(1)}, u32[]{:S(2)}, u32[]{:S(2)}) collective-permute-start(f32[8,128]{1,0:T(8,128)S(1)} %get-tuple-element.85), channel_id=1, source_target_pairs={{0,504},{8,16},{16,8},{24,32},{32,24},{40,48},{48,40},{56,64},{64,... | collective-permute-start | bytes 12296 | tf_op jit(solution)/shard_map/ppermute | solution.py:601

commit v4 on v3

--- a/solution.py
+++ b/solution.py
@@ -88,20 +88,23 @@
     return jnp.where(lax.broadcasted_iota(I32, (rows, 1), 0) == row, amount, 0.0)
 
 
-def place(record, slots, message, base):
-    lane = lax.broadcasted_iota(I32, record.shape, 1)
-    moved = record
-    for k in range(base, base + MIG):
-        moved = jnp.where(lane == slots[:, k : k + 1], message[:, k : k + 1], moved)
-    return jnp.where(lax.broadcasted_iota(I32, record.shape, 0) < 6, moved, record)
+def place(spots, values, slots, from_lower, from_upper, base=0):
+    for k in range(MIG):
+        down = slice(MIG + k, MIG + k + 1)
+        up = slice(k, k + 1)
+        message_up = from_lower[:, base + k : base + k + 1]
+        message_down = from_upper[:, base + MIG + k : base + MIG + k + 1]
+        values = jnp.where(spots == slots[:, down], message_up, values)
+        values = jnp.where(spots == slots[:, up], message_down, values)
+    return values
 
 
 def value_reader(value):
     return lambda r, g: value[8 * r : 8 * r + 8, LANES * g : LANES * (g + 1)]
 
 
-def side_list(record, side):
-    return record[6:7, 2 * GX + LANES * side : 2 * GX + LANES * (side + 1)].astype(I32)
+LONG_SLOTS = slice(2 * GX, 2 * GX + LANES)
+NARROW_SLOTS = slice(2 * GX + LANES, 2 * GX + 2 * LANES)
 
 
 def ghost_list(record, side):
@@ -112,9 +115,12 @@
     return record[7:8, HALF * side : HALF * (side + 1)].astype(I32)
 
 
-def leavers(record, side, row):
-    shift = -1.0 if side == 0 else 1.0
-    return take_lanes(value_reader(record), 8, OWN // LANES, side_list(record, side)) + unit_row(8, row, shift)
+def leavers(record, lanes, row):
+    lane = lax.broadcasted_iota(I32, (8, LANES), 1) & (2 * MIG - 1)
+    shift = jnp.where(lane < MIG, -1.0, 1.0)
+    rows = lax.broadcasted_iota(I32, (8, LANES), 0)
+    taken = take_lanes(value_reader(record), 8, OWN // LANES, record[6:7, lanes].astype(I32))
+    return taken + jnp.where(rows == row, shift, 0.0)
 
 
 def fetch(sources, targets, sems):
@@ -162,64 +168,87 @@
     record[3:6, :] = speeds
     record[6:8, :] = jnp.zeros((2, OWN), F32)
     for side in range(2):
-        start = 2 * GX + LANES * side
+        long_start = LONG_SLOTS.start + MIG * side
         record[6:7, GX * side : GX * (side + 1)] = gx[0, side : side + 1, :].astype(F32)
-        record[6:7, start : start + MIG] = mx[0, side : side + 1, :].astype(F32)
-        record[6:7, start + MIG : start + 2 * MIG] = my[0, side : side + 1, :].astype(F32)
+        record[6:7, long_start : long_start + MIG] = mx[0, side : side + 1, :].astype(F32)
+        for again in range(2):
+            start = NARROW_SLOTS.start + MIG * (side + 2 * again)
+            record[6:7, start : start + MIG] = my[0, side : side + 1, :].astype(F32)
         record[7:8, HALF * side : HALF * side + GY] = gy[0, side : side + 1, :].astype(F32)
-    whole = record[...]
-    message[...] = by_parity(par[0], leavers(whole, 0, 0), leavers(whole, 1, 0))
-
-
-def cross_kernel(par, kept, joined, out):
+    message[...] = leavers(record[...], LONG_SLOTS, 0)
+
+
+def crossed(record, from_lower, from_upper):
+    lane = lax.broadcasted_iota(I32, record.shape, 1)
+    moved = place(lane, record, record[6:7, LONG_SLOTS].astype(I32), from_lower, from_upper)
+    return jnp.where(lax.broadcasted_iota(I32, record.shape, 0) < 6, moved, record)
+
+
+AREAS = [slice(LANES * k, LANES * (k + 1)) for k in range(4)]
+
+
+def cross_kernel(par, kept, joined, own_out, out, block):
     p = par[0]
     own = kept[:, 0:OWN]
     other = joined[:, 0:OWN]
-    mine = kept[:, OWN : OWN + LANES]
-    theirs = joined[:, OWN : OWN + LANES]
-    low = by_parity(p, other, own)
-    high = by_parity(p, own, other)
-    from_below = by_parity(p, theirs, mine)
-    from_above = by_parity(p, mine, theirs)
-    new_low = place(low, side_list(low, 1), from_below, 0)
-    new_low = place(new_low, side_list(low, 0), leavers(high, 1, 0), 0)
-    new_high = place(high, side_list(high, 1), leavers(low, 0, 0), 0)
-    new_high = place(new_high, side_list(high, 0), from_above, 0)
+    near_side = kept[:, OWN : OWN + LANES]
+    far_side = joined[:, OWN : OWN + LANES]
+    from_other = leavers(other, LONG_SLOTS, 0)
+    from_own = leavers(own, LONG_SLOTS, 0)
+    own = crossed(own, by_parity(p, from_other, near_side), by_parity(p, near_side, from_other))
+    other = crossed(other, by_parity(p, far_side, from_own), by_parity(p, from_own, far_side))
+    own_out[...] = own
+    block[0:3, :] = own[0:3, :]
+    block[3:4, :] = own[7:8, :]
+    for area, record in ((AREAS[0], other), (AREAS[1], own)):
+        chosen = by_parity(p, ghost_list(record, 0), ghost_list(record, 1))
+        block[4:7, area] = take_lanes(value_reader(record), 8, OWN // LANES, chosen)[0:3, :]
+        block[7:8, area] = chosen.astype(F32)
+    lane = lax.broadcasted_iota(I32, (3, LANES), 1)
+    for area, record in ((AREAS[2], own), (AREAS[3], other)):
+        leave = leavers(record, NARROW_SLOTS, 1)
+        block[4:7, area] = jnp.where(lane < 2 * MIG, leave[0:3, :], leave[3:6, :])
+        block[7:8, area] = record[6:7, NARROW_SLOTS]
     for b in range(out.shape[0]):
-        out[b, 0:8, :] = new_low
-        out[b, 8:16, :] = new_high
-
-
-def settle(par, records, narrow_count, bundle, table, inner):
+        out[b] = block[...]
+
+
+def settle(par, blocks, record, narrow_count, bundle, table, inner):
     p = par[0]
 
-    def record_of(long_step, narrow_step):
-        number = p + 1 + long_step
-        column = lax.rem(par[2] + (narrow_step + narrow_count), narrow_count)
-        return records[((number >> 1) * narrow_count + column) * 2 + (number & 1)]
-
-    def settled(long_step, narrow_step):
-        own = record_of(long_step, narrow_step)
-        moved = place(own, side_list(own, 1), leavers(record_of(long_step, narrow_step - 1), 0, 1), MIG)
-        return place(moved, side_list(own, 0), leavers(record_of(long_step, narrow_step + 1), 1, 1), MIG)
-
+    def number(member, narrow_step):
+        return member * narrow_count + lax.rem(par[2] + (narrow_step + narrow_count), narrow_count)
+
+    def settled(member, narrow_step, spots, values, leave, base=0):
+        slots = blocks[number(member, narrow_step), 7:8, leave].astype(I32)
+        from_lower = blocks[number(member, narrow_step - 1), 4:7, leave]
+        from_upper = blocks[number(member, narrow_step + 1), 4:7, leave]
+        return place(spots, values, slots, from_lower, from_upper, base)
+
+    lane = lax.broadcasted_iota(I32, (3, OWN), 1)
+    inner[...] = jnp.zeros(inner.shape, F32)
+    toward = by_parity(p, -1.0, 1.0)
     for narrow_step in (-1, 1, 0):
-        middle = settled(0, narrow_step)
-        low = settled(-1, narrow_step)
-        high = settled(1, narrow_step)
-        inner[:, 0:OWN] = middle
-        inner[:, OWN : OWN + GX] = (
-            take_lanes(value_reader(low), 8, OWN // LANES, ghost_list(low, 0)) + unit_row(8, 0, -1.0)
-        )
-        inner[:, OWN + GX : INNER] = (
-            take_lanes(value_reader(high), 8, OWN // LANES, ghost_list(high, 1)) + unit_row(8, 0, 1.0)
-        )
+        here = number(p, narrow_step)
+        there = number(1 - p, narrow_step)
+        middle = settled(p, narrow_step, lane, blocks[here, 0:3, :], AREAS[2])
+        second = settled(
+            p, narrow_step, blocks[here, 7:8, AREAS[0]].astype(I32), blocks[here, 4:7, AREAS[0]], AREAS[3]
+        ) + unit_row(3, 0, toward)
+        first = settled(
+            1 - p, narrow_step, blocks[there, 7:8, AREAS[1]].astype(I32), blocks[there, 4:7, AREAS[1]], AREAS[2]
+        ) - unit_row(3, 0, toward)
+        inner[0:3, 0:OWN] = middle
+        inner[0:3, OWN : OWN + GX] = by_parity(p, second, first)
+        inner[0:3, OWN + GX : INNER] = by_parity(p, first, second)
         if narrow_step == 0:
-            bundle[...] = middle
+            bundle[0:3, :] = middle
+            bundle[3:6, :] = settled(p, 0, lane, record[3:6, :], AREAS[2], 2 * MIG)
+            bundle[6:8, :] = record[6:8, :]
             table[:, 0:INNER] = inner[...]
             continue
         side = 0 if narrow_step < 0 else 1
-        chosen = narrow_list(middle, side)
+        chosen = blocks[here, 3:4, HALF * side : HALF * (side + 1)].astype(I32)
         taken = jnp.concatenate(
             [
                 take_lanes(tile_reader(inner), 8, INNER // LANES, chosen[:, LANES * c : LANES * (c + 1)])
@@ -332,10 +361,10 @@
 
 
 def env_kernel(
-    narrow_count, par, records, nbr, basis, w_embed,
+    narrow_count, par, blocks, record, nbr, basis, w_embed,
     own, gx, gy, embed, one, two, latent_out, geo, square, table, inner,
 ):
-    settle(par, records, narrow_count, own, table, inner)
+    settle(par, blocks, record, narrow_count, own, table, inner)
     for side in range(2):
         gx[side : side + 1, :] = ghost_list(own, side)
         gy[side : side + 1, :] = narrow_list(own, side)
@@ -631,9 +660,9 @@
     mine = jnp.concatenate([record, message], axis=1)
     joined = lax.ppermute(mine, "gx", swap("gx", False))
     group = 2 * narrow_count
-    (records,) = call(cross_kernel, "cross", [((group, 16, OWN), F32)], [], mine, joined)
+    own, blocks = call(cross_kernel, "cross", [wide, ((group, 8, OWN), F32)], [wide], mine, joined)
     members = [list(range(group * k, group * (k + 1))) for k in range(lax.axis_size("gx") // 2)]
-    records = lax.all_to_all(records, ("gx", "gy"), 0, 0, axis_index_groups=members)
+    blocks = lax.all_to_all(blocks, ("gx", "gy"), 0, 0, axis_index_groups=members)
 
     bundle, gx, gy, embed, one, two, latent, geo, square = call(
         lambda *refs: env_kernel(narrow_count, *refs),
@@ -643,7 +672,7 @@
             ((NEI, 2 * H, OWN), BF16), ((4, NEI, OWN), F32), ((NEI, OWN), F32),
         ],
         [((8, EXT), F32), ((8, INNER), F32)],
-        records.reshape(2 * group, 8, OWN), near, basis, w_ahead,
+        blocks, own, near, basis, w_ahead,
     )
     (first,) = call(first_kernel, "first", [((NEI, H, OWN), F32)], [], latent, pair_ahead, columns)
     slopes = [

time: 130 us -> 126 us (0.969)
  waiting for transfers between devices: 22.1 us -> 20.6 us
    all_to_all x1, waiting for transfers between devices: 5.4 us -> 3.3 us  [on_device(): lax.all_to_all(blocks, ('gx', 'gy'), 0, 0, axis_index_groups=members)]
where the time goes in v4:
time: 126 us; the launch traced here: 125 us
  starting transfers between devices  62.7 us (50%)
  Pallas kernels  35.6 us (28%)
  waiting for transfers between devices  20.6 us (16%)
  local copies, waits for them, and re-layouts  4.44 us (4%)
    pallas_call x14, Pallas kernels, call(): pl.pallas_call(placed, name=name, out_shape=[jax.ShapeDtypeStruct(shape,...  35.6 us
    ppermute x6, starting transfers between devices, exchange(): lax.ppermute(one, axis, swap(axis, True))  24 us
    ppermute x6, starting transfers between devices, exchange(): lax.ppermute(two, axis, swap(axis, False))  18 us
    ppermute x6, waiting for transfers between devices, exchange(): lax.ppermute(two, axis, swap(axis, False))  13.9 us
    all_to_all x1, starting transfers between devices, on_device(): lax.all_to_all(blocks, ('gx', 'gy'), 0, 0, axis_index_groups=members)  10.1 us
    ppermute x1, starting transfers between devices, on_device(): message = lax.ppermute(message, 'gx', swap('gx', True))  8.79 us
    unnamed x11, local copies, waits for them, and re-layouts  4.44 us
    all_to_all x1, waiting for transfers between devices, on_device(): lax.all_to_all(blocks, ('gx', 'gy'), 0, 0, axis_index_groups=members)  3.3 us
  transfers between devices with their start and end apart: 15, of which 9 were waited for; matrix products, arithmetic and copies ran while one was open for 1% of the time, Pallas kernels for 6%

profile of v4, /device:TPU:1, one launch (start us, length us, event | category | flops | bytes accessed | tf_op | source)
XLA Modules:
  0.0 125.0 jit_solution(6450388417796326526)
XLA Ops:
  0.6 1.6 %start.1 = (f32[8,512]{1,0:T(8,128)}, f32[8,128]{1,0:T(8,128)}) custom-call(f32[3,512]{1,0:T(4,128)} %refs_0_.2, f32[3,512]{1,0:T(4,128)} %refs_1_.1, f32[3,512]{1,0:T(4,128)} %refs_2_.2, s32[1,2,128]{2,1,0:T(2,128)} %refs_3_.1, s32[1,2,192]{2,1,0:T(2,128)} %refs_4_.2, s32[1,2,8]{2,1,0:T(2,128)} %refs_5_.1, s32[1,2,8]{2,1,0:T(2,128)} %refs_6_.1), custom_call_target="tpu_custom_call" | custom-call | tf_op jit(solution)/shard_map/start/pallas_call | solution.py:601
  2.2 8.8 %collective-permute-start = (f32[8,128]{1,0:T(8,128)}, f32[8,128]{1,0:T(8,128)S(1)}, u32[]{:S(2)}, u32[]{:S(2)}) collective-permute-start(f32[8,128]{1,0:T(8,128)} %get-tuple-element.48), channel_id=1, source_target_pairs={{0,8},{8,0},{16,24},{24,16},{32,40},{40,32},{48,56},{56,48},{64,72... | collective-permute-start | bytes 12296 | tf_op jit(solution)/shard_map/ppermute | solution.py:659
  11.0 0.7 constant_dynamic-update-slice_fusion.1
  11.7 0.3 collective-permute-done
  12.0 1.9 %collective-permute-start.1 = (f32[8,640]{1,0:T(8,128)S(1)}, f32[8,640]{1,0:T(8,128)S(1)}, u32[]{:S(2)}, u32[]{:S(2)}) collective-permute-start(f32[8,640]{1,0:T(8,128)S(1)} %constant_dynamic-update-slice_fusion.refs_0_), channel_id=1, source_target_pairs={{0,504},{8,16},{16,8},{24,32},{32,24},{40,48},{48,40},{56,64},{64,... | collective-permute-start | bytes 61448 | tf_op jit(solution)/shard_map/ppermute | solution.py:661
  14.0 3.2 %collective-permute-done.1.refs_1_ = f32[8,640]{1,0:T(8,128)S(1)} collective-permute-done((f32[8,640]{1,0:T(8,128)S(1)}, f32[8,640]{1,0:T(8,128)S(1)}, u32[]{:S(2)}, u32[]{:S(2)}) %collective-permute-start.1) | collective-permute-done | bytes 20512 | tf_op jit(solution)/shard_map/ppermute | solution.py:661
  17.1 1.1 cross.1
  18.2 10.1 %all-to-all-start = ((f32[16,8,512]{2,1,0:T(8,128)}), f32[16,8,512]{2,1,0:T(8,128)S(1)}, u32[]{:S(2)}, u32[]{:S(2)}) async-start(f32[16,8,512]{2,1,0:T(8,128)} %get-tuple-element.49), calls=%async_computation | async-start | bytes 524288 | tf_op jit(solution)/shard_map/all_to_all | solution.py:665
  28.3 0.7 pad_maximum_fusion.refs_5_
  29.0 0.8 copy-done
  29.8 0.8 copy-done.1
  30.6 0.7 copy-done.2
  31.3 0.7 copy-done.3
  32.0 0.7 copy-done.4
  32.7 0.4 prepare.1
  33.1 3.3 %all-to-all-done.refs_0_ = f32[16,8,512]{2,1,0:T(8,128)S(1)} async-done(((f32[16,8,512]{2,1,0:T(8,128)}), f32[16,8,512]{2,1,0:T(8,128)S(1)}, u32[]{:S(2)}, u32[]{:S(2)}) %all-to-all-start) | async-done | bytes 262176 | tf_op jit(solution)/shard_map/all_to_all | solution.py:665
  36.4 4.6 %env.1 = (f32[8,512]{1,0:T(8,128)S(1)}, s32[2,128]{1,0:T(2,128)S(1)}, s32[2,256]{1,0:T(2,128)S(1)}, f32[32,512]{1,0:T(8,128)S(1)}, f32[32,128]{1,0:T(8,128)S(1)}...) custom-call(f32[16,8,512]{2,1,0:T(8,128)S(1)} %all-to-all-done.refs_, ...), custom_call_target="tpu_custom_call" | custom-call | tf_op jit(solution)/shard_map/env/pallas_call | solution.py:601
  40.9 3.4 %collective-permute-start.2 = (f32[32,128]{1,0:T(8,128)S(1)}, f32[32,128]{1,0:T(8,128)S(1)}, u32[]{:S(2)}, u32[]{:S(2)}) collective-permute-start(f32[32,128]{1,0:T(8,128)S(1)} %get-tuple-element.55), channel_id=1, source_target_pairs={{0,8},{8,0},{16,24},{24,16},{32,40},{40,32},{48,56},{56,48},{64,72... | collective-permute-start | bytes 49160 | tf_op jit(solution)/shard_map/ppermute | solution.py:629
  44.4 1.9 %collective-permute-start.3 = (f32[32,128]{1,0:T(8,128)S(1)}, f32[32,128]{1,0:T(8,128)S(1)}, u32[]{:S(2)}, u32[]{:S(2)}) collective-permute-start(f32[32,128]{1,0:T(8,128)S(1)} %get-tuple-element.56), channel_id=1, source_target_pairs={{0,504},{8,16},{16,8},{24,32},{32,24},{40,48},{48,40},{56,64},{64,... | collective-permute-start | bytes 49160 | tf_op jit(solution)/shard_map/ppermute | solution.py:630
  46.3 1.5 %slope0.1.refs_2_.refs_5_ = f32[32,64,256]{2,1,0:T(8,128)S(1)} custom-call(f32[32,512]{1,0:T(8,128)S(1)} %get-tuple-element.57.refs_0_, f32[4,32,512]{2,1,0:T(8,128)S(1)} %get-tuple-element.58.refs_1_.refs_7_.refs_8_, bf16[64,32]{1,0:T(8,128)(2,1)S(1)} %get-tuple-element.52.refs_3_.refs_2_), custom_call_target="tpu_custom_call" | custom-call | tf_op jit(solution)/shard_map/slope0/pallas_call | solution.py:601
  47.8 0.0 collective-permute-done.2.refs_1_
  47.8 1.6 %collective-permute-done.3.refs_2_ = f32[32,128]{1,0:T(8,128)S(1)} collective-permute-done((f32[32,128]{1,0:T(8,128)S(1)}, f32[32,128]{1,0:T(8,128)S(1)}, u32[]{:S(2)}, u32[]{:S(2)}) %collective-permute-start.3) | collective-permute-done | bytes 16416 | tf_op jit(solution)/shard_map/ppermute | solution.py:630
  49.4 0.2 ghost_embed.1
  49.6 2.4 %collective-permute-start.4 = (f32[32,256]{1,0:T(8,128)S(1)}, f32[32,256]{1,0:T(8,128)S(1)}, u32[]{:S(2)}, u32[]{:S(2)}) collective-permute-start(f32[32,256]{1,0:T(8,128)S(1)} %get-tuple-element.62), channel_id=1, source_target_pairs={{0,1},{1,0},{2,3},{3,2},{4,5},{5,4},{6,7},{7,6},{8,9},{9,8},{10,11... | collective-permute-start | bytes 98312 | tf_op jit(solution)/shard_map/ppermute | solution.py:629
  52.0 4.4 %collective-permute-start.5 = (f32[32,256]{1,0:T(8,128)S(1)}, f32[32,256]{1,0:T(8,128)S(1)}, u32[]{:S(2)}, u32[]{:S(2)}) collective-permute-start(f32[32,256]{1,0:T(8,128)S(1)} %get-tuple-element.63), channel_id=1, source_target_pairs={{0,7},{1,2},{2,1},{3,4},{4,3},{5,6},{6,5},{7,0},{8,15},{9,10},{10,... | collective-permute-start | bytes 98312 | tf_op jit(solution)/shard_map/ppermute | solution.py:630
  56.5 2.3 %first.1.refs_6_ = f32[32,64,512]{2,1,0:T(8,128)S(1)} custom-call(bf16[32,128,512]{2,1,0:T(8,128)(2,1)S(1)} %get-tuple-element.64.refs_0_, bf16[128,128]{1,0:T(8,128)(2,1)S(1)} %get-tuple-element.65.refs_1_, f32[64,8]{1,0:T(8,128)S(1)} %get-tuple-element.66.refs_2_.refs_10_), custom_call_target="tpu_custom_call" | custom-call | tf_op jit(solution)/shard_map/first/pallas_call | solution.py:601
  58.8 0.0 collective-permute-done.4.refs_3_
  58.8 1.5 %collective-permute-done.5.refs_4_ = f32[32,256]{1,0:T(8,128)S(1)} collective-permute-done((f32[32,256]{1,0:T(8,128)S(1)}, f32[32,256]{1,0:T(8,128)S(1)}, u32[]{:S(2)}, u32[]{:S(2)}) %collective-permute-start.5) | collective-permute-done | bytes 32800 | tf_op jit(solution)/shard_map/ppermute | solution.py:630
  60.3 12.9 %pair.1 = (bf16[32,128,512]{2,1,0:T(8,128)(2,1)S(1)}, f32[32,512]{1,0:T(8,128)S(1)}, f32[32,768]{1,0:T(8,128)S(1)}, f32[32,192]{1,0:T(8,128)S(1)}, f32[32,192]{1,0:T(8,128)S(1)}) custom-call(f32[32,512]{1,0:T(8,128)S(1)} %get-tuple-element.54.refs_0_, f32[32,128]{1,0:T(8,128)S(1)} %collective-permute-done.2.refs_1_, ...), custom_call_target="tpu_custom_call" | custom-call | tf_op jit(solution)/shard_map/pair/pallas_call | solution.py:601
  73.2 3.2 %collective-permute-start.6 = (f32[32,192]{1,0:T(8,128)S(1)}, f32[32,192]{1,0:T(8,128)S(1)}, u32[]{:S(2)}, u32[]{:S(2)}) collective-permute-start(f32[32,192]{1,0:T(8,128)S(1)} %get-tuple-element.70), channel_id=1, source_target_pairs={{0,1},{1,0},{2,3},{3,2},{4,5},{5,4},{6,7},{7,6},{8,9},{9,8},{10,11... | collective-permute-start | bytes 73736 | tf_op jit(solution)/shard_map/ppermute | solution.py:629
  76.4 3.2 %collective-permute-start.7 = (f32[32,192]{1,0:T(8,128)S(1)}, f32[32,192]{1,0:T(8,128)S(1)}, u32[]{:S(2)}, u32[]{:S(2)}) collective-permute-start(f32[32,192]{1,0:T(8,128)S(1)} %get-tuple-element.71), channel_id=1, source_target_pairs={{0,7},{1,2},{2,1},{3,4},{4,3},{5,6},{6,5},{7,0},{8,15},{9,10},{10,... | collective-permute-start | bytes 73736 | tf_op jit(solution)/shard_map/ppermute | solution.py:630
  79.6 1.5 %slope1.1.refs_3_.refs_6_ = f32[32,64,256]{2,1,0:T(8,128)S(1)} custom-call(f32[32,512]{1,0:T(8,128)S(1)} %get-tuple-element.57.refs_0_, f32[4,32,512]{2,1,0:T(8,128)S(1)} %get-tuple-element.58.refs_1_.refs_7_.refs_8_, bf16[64,32]{1,0:T(8,128)(2,1)S(1)} %get-tuple-element.52.refs_3_.refs_2_), custom_call_target="tpu_custom_call" | custom-call | tf_op jit(solution)/shard_map/slope1/pallas_call | solution.py:601
  81.1 3.6 %collective-permute-done.7.refs_2_ = f32[32,192]{1,0:T(8,128)S(1)} collective-permute-done((f32[32,192]{1,0:T(8,128)S(1)}, f32[32,192]{1,0:T(8,128)S(1)}, u32[]{:S(2)}, u32[]{:S(2)}) %collective-permute-start.7) | collective-permute-done | bytes 24608 | tf_op jit(solution)/shard_map/ppermute | solution.py:630
  84.7 0.8 fold_embed.1
  85.5 6.9 %collective-permute-start.8 = (f32[32,128]{1,0:T(8,128)S(1)}, f32[32,128]{1,0:T(8,128)S(1)}, u32[]{:S(2)}, u32[]{:S(2)}) collective-permute-start(f32[32,128]{1,0:T(8,128)S(1)} %get-tuple-element.75), channel_id=1, source_target_pairs={{0,8},{8,0},{16,24},{24,16},{32,40},{40,32},{48,56},{56,48},{64,72... | collective-permute-start | bytes 49160 | tf_op jit(solution)/shard_map/ppermute | solution.py:629
  92.4 1.9 %collective-permute-start.9 = (f32[32,128]{1,0:T(8,128)S(1)}, f32[32,128]{1,0:T(8,128)S(1)}, u32[]{:S(2)}, u32[]{:S(2)}) collective-permute-start(f32[32,128]{1,0:T(8,128)S(1)} %get-tuple-element.76), channel_id=1, source_target_pairs={{0,504},{8,16},{16,8},{24,32},{32,24},{40,48},{48,40},{56,64},{64,... | collective-permute-start | bytes 49160 | tf_op jit(solution)/shard_map/ppermute | solution.py:630
  94.3 2.4 %rise.1.refs_7_ = f32[32,512]{1,0:T(8,128)S(1)} custom-call(bf16[32,128,512]{2,1,0:T(8,128)(2,1)S(1)} %get-tuple-element.81.refs_0_, f32[32,512]{1,0:T(8,128)S(1)} %get-tuple-element.82.refs_1_, f32[32,64,256]{2,1,0:T(8,128)S(1)} %slope0.1.refs_2_.refs_5_, f32[32,64,256]{2,1,0:T(8,128)S(1)} %slope1.1.refs_3_.refs_6_, ...), custom_call_target="tpu_custom_call" | custom-call | tf_op jit(solution)/shard_map/rise/pallas_call | solution.py:601
  96.7 0.0 collective-permute-done.8.refs_1_
  96.7 0.8 collective-permute-done.9.refs_2_
  97.4 4.9 %force.1 = (f32[8,768]{1,0:T(8,128)S(1)}, f32[8,192]{1,0:T(8,128)S(1)}, f32[8,192]{1,0:T(8,128)S(1)}) custom-call(f32[32,512]{1,0:T(8,128)S(1)} %get-tuple-element.74.refs_0_, f32[32,128]{1,0:T(8,128)S(1)} %collective-permute-done.8.refs_1_, f32[32,128]{1,0:T(8,128)S(1)} %collective-permute-done.9.refs_2_, s32[2,128]{1,0:T(2,128)S(1)} %get-tuple-element.77.refs_3_, ...), custom_call_target="tpu_custom_call" | custom-call | tf_op jit(solution)/shard_map/force/pallas_call | solution.py:601
  102.3 2.6 %collective-permute-start.10 = (f32[8,192]{1,0:T(8,128)S(1)}, f32[8,192]{1,0:T(8,128)S(1)}, u32[]{:S(2)}, u32[]{:S(2)}) collective-permute-start(f32[8,192]{1,0:T(8,128)S(1)} %get-tuple-element.85), channel_id=1, source_target_pairs={{0,1},{1,0},{2,3},{3,2},{4,5},{5,4},{6,7},{7,6},{8,9},{9,8},{10,11... | collective-permute-start | bytes 18440 | tf_op jit(solution)/shard_map/ppermute | solution.py:629
  104.9 4.6 %collective-permute-start.11 = (f32[8,192]{1,0:T(8,128)S(1)}, f32[8,192]{1,0:T(8,128)S(1)}, u32[]{:S(2)}, u32[]{:S(2)}) collective-permute-start(f32[8,192]{1,0:T(8,128)S(1)} %get-tuple-element.86), channel_id=1, source_target_pairs={{0,7},{1,2},{2,1},{3,4},{4,3},{5,6},{6,5},{7,0},{8,15},{9,10},{10,... | collective-permute-start | bytes 18440 | tf_op jit(solution)/shard_map/ppermute | solution.py:630
  109.5 3.4 %collective-permute-done.11.refs_2_ = f32[8,192]{1,0:T(8,128)S(1)} collective-permute-done((f32[8,192]{1,0:T(8,128)S(1)}, f32[8,192]{1,0:T(8,128)S(1)}, u32[]{:S(2)}, u32[]{:S(2)}) %collective-permute-start.11) | collective-permute-done | bytes 6176 | tf_op jit(solution)/shard_map/ppermute | solution.py:630
  112.9 0.7 fold_force.1
  113.6 5.5 %collective-permute-start.12 = (f32[8,128]{1,0:T(8,128)S(1)}, f32[8,128]{1,0:T(8,128)S(1)}, u32[]{:S(2)}, u32[]{:S(2)}) collective-permute-start(f32[8,128]{1,0:T(8,128)S(1)} %get-tuple-element.88), channel_id=1, source_target_pairs={{0,8},{8,0},{16,24},{24,16},{32,40},{40,32},{48,56},{56,48},{64,72... | collective-permute-start | bytes 12296 | tf_op jit(solution)/shard_map/ppermute | solution.py:629
  119.1 1.9 %collective-permute-start.13 = (f32[8,128]{1,0:T(8,128)S(1)}, f32[8,128]{1,0:T(8,128)S(1)}, u32[]{:S(2)}, u32[]{:S(2)}) collective-permute-start(f32[8,128]{1,0:T(8,128)S(1)} %get-tuple-element.89), channel_id=1, source_target_pairs={{0,504},{8,16},{16,8},{24,32},{32,24},{40,48},{48,40},{56,64},{64,... | collective-permute-start | bytes 12296 | tf_op jit(solution)/shard_map/ppermute | solution.py:630
  121.1 3.0 %collective-permute-done.13.refs_2_ = f32[8,128]{1,0:T(8,128)S(1)} collective-permute-done((f32[8,128]{1,0:T(8,128)S(1)}, f32[8,128]{1,0:T(8,128)S(1)}, u32[]{:S(2)}, u32[]{:S(2)}) %collective-permute-start.13) | collective-permute-done | bytes 4128 | tf_op jit(solution)/shard_map/ppermute | solution.py:630
  124.0 0.9 final.1
  (9 shorter events, 0.0 us)
Async XLA Ops:
  2.2 9.8 %collective-permute-start = (f32[8,128]{1,0:T(8,128)}, f32[8,128]{1,0:T(8,128)S(1)}, u32[]{:S(2)}, u32[]{:S(2)}) collective-permute-start(f32[8,128]{1,0:T(8,128)} %get-tuple-element.48), channel_id=1, source_target_pairs={{0,8},{8,0},{16,24},{24,16},{32,40},{40,32},{48,56},{56,48},{64,72... | collective-permute-start | bytes 12296 | tf_op jit(solution)/shard_map/ppermute | solution.py:659
  12.0 5.1 %collective-permute-start.1 = (f32[8,640]{1,0:T(8,128)S(1)}, f32[8,640]{1,0:T(8,128)S(1)}, u32[]{:S(2)}, u32[]{:S(2)}) collective-permute-start(f32[8,640]{1,0:T(8,128)S(1)} %constant_dynamic-update-slice_fusion.refs_0_), channel_id=1, source_target_pairs={{0,504},{8,16},{16,8},{24,32},{32,24},{40,48},{48,40},{56,64},{64,... | collective-permute-start | bytes 61448 | tf_op jit(solution)/shard_map/ppermute | solution.py:661
  18.2 18.2 %all-to-all-start = ((f32[16,8,512]{2,1,0:T(8,128)}), f32[16,8,512]{2,1,0:T(8,128)S(1)}, u32[]{:S(2)}, u32[]{:S(2)}) async-start(f32[16,8,512]{2,1,0:T(8,128)} %get-tuple-element.49), calls=%async_computation | async-start | bytes 524288 | tf_op jit(solution)/shard_map/all_to_all | solution.py:665
  29.0 0.8 copy-start
  29.8 0.8 copy-start.1
  30.6 0.7 copy-start.2
  31.3 0.7 copy-start.3
  32.0 0.7 copy-start.4
  40.9 6.9 %collective-permute-start.2 = (f32[32,128]{1,0:T(8,128)S(1)}, f32[32,128]{1,0:T(8,128)S(1)}, u32[]{:S(2)}, u32[]{:S(2)}) collective-permute-start(f32[32,128]{1,0:T(8,128)S(1)} %get-tuple-element.55), channel_id=1, source_target_pairs={{0,8},{8,0},{16,24},{24,16},{32,40},{40,32},{48,56},{56,48},{64,72... | collective-permute-start | bytes 49160 | tf_op jit(solution)/shard_map/ppermute | solution.py:629
  44.4 5.1 %collective-permute-start.3 = (f32[32,128]{1,0:T(8,128)S(1)}, f32[32,128]{1,0:T(8,128)S(1)}, u32[]{:S(2)}, u32[]{:S(2)}) collective-permute-start(f32[32,128]{1,0:T(8,128)S(1)} %get-tuple-element.56), channel_id=1, source_target_pairs={{0,504},{8,16},{16,8},{24,32},{32,24},{40,48},{48,40},{56,64},{64,... | collective-permute-start | bytes 49160 | tf_op jit(solution)/shard_map/ppermute | solution.py:630
  49.6 9.2 %collective-permute-start.4 = (f32[32,256]{1,0:T(8,128)S(1)}, f32[32,256]{1,0:T(8,128)S(1)}, u32[]{:S(2)}, u32[]{:S(2)}) collective-permute-start(f32[32,256]{1,0:T(8,128)S(1)} %get-tuple-element.62), channel_id=1, source_target_pairs={{0,1},{1,0},{2,3},{3,2},{4,5},{5,4},{6,7},{7,6},{8,9},{9,8},{10,11... | collective-permute-start | bytes 98312 | tf_op jit(solution)/shard_map/ppermute | solution.py:629
  52.0 8.3 %collective-permute-start.5 = (f32[32,256]{1,0:T(8,128)S(1)}, f32[32,256]{1,0:T(8,128)S(1)}, u32[]{:S(2)}, u32[]{:S(2)}) collective-permute-start(f32[32,256]{1,0:T(8,128)S(1)} %get-tuple-element.63), channel_id=1, source_target_pairs={{0,7},{1,2},{2,1},{3,4},{4,3},{5,6},{6,5},{7,0},{8,15},{9,10},{10,... | collective-permute-start | bytes 98312 | tf_op jit(solution)/shard_map/ppermute | solution.py:630
  73.2 7.9 %collective-permute-start.6 = (f32[32,192]{1,0:T(8,128)S(1)}, f32[32,192]{1,0:T(8,128)S(1)}, u32[]{:S(2)}, u32[]{:S(2)}) collective-permute-start(f32[32,192]{1,0:T(8,128)S(1)} %get-tuple-element.70), channel_id=1, source_target_pairs={{0,1},{1,0},{2,3},{3,2},{4,5},{5,4},{6,7},{7,6},{8,9},{9,8},{10,11... | collective-permute-start | bytes 73736 | tf_op jit(solution)/shard_map/ppermute | solution.py:629
  76.4 8.3 %collective-permute-start.7 = (f32[32,192]{1,0:T(8,128)S(1)}, f32[32,192]{1,0:T(8,128)S(1)}, u32[]{:S(2)}, u32[]{:S(2)}) collective-permute-start(f32[32,192]{1,0:T(8,128)S(1)} %get-tuple-element.71), channel_id=1, source_target_pairs={{0,7},{1,2},{2,1},{3,4},{4,3},{5,6},{6,5},{7,0},{8,15},{9,10},{10,... | collective-permute-start | bytes 73736 | tf_op jit(solution)/shard_map/ppermute | solution.py:630
  85.5 11.2 %collective-permute-start.8 = (f32[32,128]{1,0:T(8,128)S(1)}, f32[32,128]{1,0:T(8,128)S(1)}, u32[]{:S(2)}, u32[]{:S(2)}) collective-permute-start(f32[32,128]{1,0:T(8,128)S(1)} %get-tuple-element.75), channel_id=1, source_target_pairs={{0,8},{8,0},{16,24},{24,16},{32,40},{40,32},{48,56},{56,48},{64,72... | collective-permute-start | bytes 49160 | tf_op jit(solution)/shard_map/ppermute | solution.py:629
  92.4 5.1 %collective-permute-start.9 = (f32[32,128]{1,0:T(8,128)S(1)}, f32[32,128]{1,0:T(8,128)S(1)}, u32[]{:S(2)}, u32[]{:S(2)}) collective-permute-start(f32[32,128]{1,0:T(8,128)S(1)} %get-tuple-element.76), channel_id=1, source_target_pairs={{0,504},{8,16},{16,8},{24,32},{32,24},{40,48},{48,40},{56,64},{64,... | collective-permute-start | bytes 49160 | tf_op jit(solution)/shard_map/ppermute | solution.py:630
  102.3 7.2 %collective-permute-start.10 = (f32[8,192]{1,0:T(8,128)S(1)}, f32[8,192]{1,0:T(8,128)S(1)}, u32[]{:S(2)}, u32[]{:S(2)}) collective-permute-start(f32[8,192]{1,0:T(8,128)S(1)} %get-tuple-element.85), channel_id=1, source_target_pairs={{0,1},{1,0},{2,3},{3,2},{4,5},{5,4},{6,7},{7,6},{8,9},{9,8},{10,11... | collective-permute-start | bytes 18440 | tf_op jit(solution)/shard_map/ppermute | solution.py:629
  104.9 8.0 %collective-permute-start.11 = (f32[8,192]{1,0:T(8,128)S(1)}, f32[8,192]{1,0:T(8,128)S(1)}, u32[]{:S(2)}, u32[]{:S(2)}) collective-permute-start(f32[8,192]{1,0:T(8,128)S(1)} %get-tuple-element.86), channel_id=1, source_target_pairs={{0,7},{1,2},{2,1},{3,4},{4,3},{5,6},{6,5},{7,0},{8,15},{9,10},{10,... | collective-permute-start | bytes 18440 | tf_op jit(solution)/shard_map/ppermute | solution.py:630
  113.6 7.4 %collective-permute-start.12 = (f32[8,128]{1,0:T(8,128)S(1)}, f32[8,128]{1,0:T(8,128)S(1)}, u32[]{:S(2)}, u32[]{:S(2)}) collective-permute-start(f32[8,128]{1,0:T(8,128)S(1)} %get-tuple-element.88), channel_id=1, source_target_pairs={{0,8},{8,0},{16,24},{24,16},{32,40},{40,32},{48,56},{56,48},{64,72... | collective-permute-start | bytes 12296 | tf_op jit(solution)/shard_map/ppermute | solution.py:629
  119.1 4.9 %collective-permute-start.13 = (f32[8,128]{1,0:T(8,128)S(1)}, f32[8,128]{1,0:T(8,128)S(1)}, u32[]{:S(2)}, u32[]{:S(2)}) collective-permute-start(f32[8,128]{1,0:T(8,128)S(1)} %get-tuple-element.89), channel_id=1, source_target_pairs={{0,504},{8,16},{16,8},{24,32},{32,24},{40,48},{48,40},{56,64},{64,... | collective-permute-start | bytes 12296 | tf_op jit(solution)/shard_map/ppermute | solution.py:630

commit v5 on v4

--- a/solution.py
+++ b/solution.py
@@ -32,8 +32,12 @@
 BIG = 24 * 1024 * 1024
 WHOLE = 60 * 1024 * 1024
 GROUP = 4
-CHUNK = 512
+PAIR_GROUP = 16
+SPAN = 2
+FORCE_GROUP = 8
 UNROLL_ENV = 8
+ENV_WIDTH = 256
+ENV_TURNS = 16
 
 
 def half_split(value):
@@ -388,10 +392,10 @@
             geo[3, rows, lanes] = jnp.where(index >= 0, 1.0 / (1.0 + total), 0.0)
 
     centre = centres()
-    ones = jnp.ones((NB, HALF), F32)
+    ones = jnp.ones((NB, ENV_WIDTH), F32)
     left = basis[...]
-    for half in range(OWN // HALF):
-        lanes = slice(HALF * half, HALF * (half + 1))
+    for half in range(OWN // ENV_WIDTH):
+        lanes = slice(ENV_WIDTH * half, ENV_WIDTH * (half + 1))
 
         def turn(n, gathered):
             offset = square[pl.ds(n, 1), lanes] - centre
@@ -403,7 +407,7 @@
             latent_out[n, H : 2 * H, lanes] = low
             return gathered + latent
 
-        gathered = lax.fori_loop(0, NEI, turn, jnp.zeros((H, HALF), F32), unroll=UNROLL_ENV)
+        gathered = lax.fori_loop(0, NEI, turn, jnp.zeros((H, ENV_WIDTH), F32), unroll=ENV_TURNS)
         environ = gathered * (1.0 / math.sqrt(NEI))
         embed[:, lanes] = jnp.dot(w_embed[...], environ, precision=HIGHEST, preferred_element_type=F32)
     p = par[0]
@@ -437,54 +441,53 @@
     right_back = back[...]
     readout = columns[:, 1:2]
 
+    def rows_of(read, start, count):
+        return jnp.concatenate([read(start + j) for j in range(count)], axis=1)
+
     def scatter(g, joined):
-        index = jnp.concatenate([nbr[pl.ds(GROUP * g + j, 1), :] for j in range(GROUP)], axis=1)
+        index = rows_of(lambda n: nbr[pl.ds(n, 1), :], PAIR_GROUP * g, PAIR_GROUP)
         spread_sum[...] += lax.dot_general(
             level_rows(joined, index >> 8), hot_rows(index & (HALF - 1)),
             (((1,), (1,)), ((), ())), preferred_element_type=F32,
         )
 
-    def chunk(n, lanes, width):
-        index = nbr[pl.ds(n, 1), lanes]
-        weight = geo[3, pl.ds(n, 1), lanes]
+    def chunk(n):
+        index = rows_of(lambda m: nbr[pl.ds(m, 1), :], n, SPAN)
+        weight = rows_of(lambda m: geo[3, pl.ds(m, 1), :], n, SPAN)
         partner = jnp.concatenate(
             [
                 take_lanes(tile_reader(table), EMB, GROUPS, index[:, LANES * c : LANES * (c + 1)])
-                for c in range(width // LANES)
+                for c in range(SPAN * OWN // LANES)
             ],
             axis=1,
         )
-        embed_own = own[:, lanes]
+        embed_own = jnp.concatenate([own[...]] * SPAN, axis=1)
         product_high, product_low = half_split(partner * embed_own)
         sums = product(left, jnp.concatenate([product_high, product_low], axis=0))
-        value = first[n, :, lanes] + sums[:H] + sums[H:]
+        value = rows_of(lambda m: first[m], n, SPAN) + sums[:H] + sums[H:]
         gate = 0.5 * jnp.tanh(0.5 * value) + 0.5
         hidden = value * gate
         dvalue = (gate + hidden * (1.0 - gate)) * (readout * weight)
         dhigh, dlow = half_split(dvalue)
         dvalue = jnp.concatenate([dhigh, dlow], axis=0)
-        dvalue_out[n, :, lanes] = dvalue
         sums = product(right_back, dvalue)
         dproduct = sums[:EMB] + sums[EMB:]
-        part[pl.ds(n, 1), lanes] = -(weight * weight) * jnp.sum(hidden * readout, axis=0, keepdims=True)
+        partial = -(weight * weight) * jnp.sum(hidden * readout, axis=0, keepdims=True)
+        more = dproduct * partner
+        for j in range(SPAN):
+            lanes = slice(OWN * j, OWN * (j + 1))
+            dvalue_out[n + j] = dvalue[:, lanes]
+            part[pl.ds(n + j, 1), :] = partial[:, lanes]
+            own_sum[...] += more[:, lanes]
         high, low = half_split(dproduct * embed_own)
-        return dproduct * partner, jnp.concatenate([high, low], axis=0)
+        return jnp.concatenate([high, low], axis=0)
 
     def turn(g, joined):
         scatter(jnp.maximum(g - 1, 0), joined)
-        pieces = {}
-        for part in range(OWN // CHUNK):
-            lanes = slice(CHUNK * part, CHUNK * (part + 1))
-            grown = own_sum[:, lanes]
-            for j in range(GROUP):
-                more, piece = chunk(GROUP * g + j, lanes, CHUNK)
-                grown = grown + more
-                pieces[j, part] = piece
-            own_sum[:, lanes] = grown
-        return jnp.concatenate([pieces[j, part] for j in range(GROUP) for part in range(OWN // CHUNK)], axis=1)
-
-    joined = lax.fori_loop(0, NEI // GROUP, turn, jnp.zeros((2 * EMB, GROUP * OWN), BF16))
-    scatter(NEI // GROUP - 1, joined)
+        return jnp.concatenate([chunk(PAIR_GROUP * g + SPAN * j) for j in range(PAIR_GROUP // SPAN)], axis=1)
+
+    joined = lax.fori_loop(0, NEI // PAIR_GROUP, turn, jnp.zeros((2 * EMB, PAIR_GROUP * OWN), BF16))
+    scatter(NEI // PAIR_GROUP - 1, joined)
     for k in range(LEVELS):
         base = 2 * EMB * k
         width = min(HALF, EXT - HALF * k)
@@ -545,8 +548,8 @@
         lifted = []
         hot = []
         pushed = pushes[...]
-        for j in range(GROUP):
-            n = GROUP * g + j
+        for j in range(FORCE_GROUP):
+            n = FORCE_GROUP * g + j
             rate = jnp.concatenate(
                 [
                     jnp.sum(slope[n] * grown[:, HALF * h : HALF * (h + 1)], axis=0, keepdims=True)
@@ -572,7 +575,7 @@
         )
         return carry
 
-    lax.fori_loop(0, NEI // GROUP, turn, 0)
+    lax.fori_loop(0, NEI // FORCE_GROUP, turn, 0)
     table[...] = jnp.zeros(table.shape, F32)
     for k in range(LEVELS):
         width = min(HALF, EXT - HALF * k)

time: 126 us -> 122 us (0.968)
  Pallas kernels: 35.6 us -> 31.7 us
    pallas_call x14, Pallas kernels: 35.6 us -> 31.7 us  [call(): pl.pallas_call(placed, name=name, out_shape=[jax.ShapeDtypeStruct(shape,...]
  transfers between devices with their start and end apart: 15 -> 15, of which waited for: 9 -> 9; matrix products, arithmetic and copies ran while one was open for 1% -> 1% of each run, Pallas kernels for 6% -> 7%
where the time goes in v5:
time: 122 us; the launch traced here: 121 us
  starting transfers between devices  62.8 us (51%)
  Pallas kernels  31.7 us (26%)
  waiting for transfers between devices  20.6 us (17%)
  local copies, waits for them, and re-layouts  4.44 us (4%)
    pallas_call x14, Pallas kernels, call(): pl.pallas_call(placed, name=name, out_shape=[jax.ShapeDtypeStruct(shape,...  31.7 us
    ppermute x6, starting transfers between devices, exchange(): lax.ppermute(one, axis, swap(axis, True))  24 us
    ppermute x6, starting transfers between devices, exchange(): lax.ppermute(two, axis, swap(axis, False))  18 us
    ppermute x6, waiting for transfers between devices, exchange(): lax.ppermute(two, axis, swap(axis, False))  13.8 us
    all_to_all x1, starting transfers between devices, on_device(): lax.all_to_all(blocks, ('gx', 'gy'), 0, 0, axis_index_groups=members)  10.1 us
    ppermute x1, starting transfers between devices, on_device(): message = lax.ppermute(message, 'gx', swap('gx', True))  8.79 us
    unnamed x11, local copies, waits for them, and re-layouts  4.44 us
    all_to_all x1, waiting for transfers between devices, on_device(): lax.all_to_all(blocks, ('gx', 'gy'), 0, 0, axis_index_groups=members)  3.3 us
  transfers between devices with their start and end apart: 15, of which 9 were waited for; matrix products, arithmetic and copies ran while one was open for 1% of the time, Pallas kernels for 7%

profile of v5, /device:TPU:1, one launch (start us, length us, event | category | flops | bytes accessed | tf_op | source)
XLA Modules:
  0.0 121.0 jit_solution(837890778291042263)
XLA Ops:
  0.6 1.6 %start.1 = (f32[8,512]{1,0:T(8,128)}, f32[8,128]{1,0:T(8,128)}) custom-call(f32[3,512]{1,0:T(4,128)} %refs_0_.2, f32[3,512]{1,0:T(4,128)} %refs_1_.1, f32[3,512]{1,0:T(4,128)} %refs_2_.2, s32[1,2,128]{2,1,0:T(2,128)} %refs_3_.1, s32[1,2,192]{2,1,0:T(2,128)} %refs_4_.2, s32[1,2,8]{2,1,0:T(2,128)} %refs_5_.1, s32[1,2,8]{2,1,0:T(2,128)} %refs_6_.1), custom_call_target="tpu_custom_call" | custom-call | tf_op jit(solution)/shard_map/start/pallas_call | solution.py:604
  2.2 8.8 %collective-permute-start = (f32[8,128]{1,0:T(8,128)}, f32[8,128]{1,0:T(8,128)S(1)}, u32[]{:S(2)}, u32[]{:S(2)}) collective-permute-start(f32[8,128]{1,0:T(8,128)} %get-tuple-element.48), channel_id=1, source_target_pairs={{0,8},{8,0},{16,24},{24,16},{32,40},{40,32},{48,56},{56,48},{64,72... | collective-permute-start | bytes 12296 | tf_op jit(solution)/shard_map/ppermute | solution.py:662
  11.0 0.7 constant_dynamic-update-slice_fusion.1
  11.7 0.3 collective-permute-done
  12.0 1.9 %collective-permute-start.1 = (f32[8,640]{1,0:T(8,128)S(1)}, f32[8,640]{1,0:T(8,128)S(1)}, u32[]{:S(2)}, u32[]{:S(2)}) collective-permute-start(f32[8,640]{1,0:T(8,128)S(1)} %constant_dynamic-update-slice_fusion.refs_0_), channel_id=1, source_target_pairs={{0,504},{8,16},{16,8},{24,32},{32,24},{40,48},{48,40},{56,64},{64,... | collective-permute-start | bytes 61448 | tf_op jit(solution)/shard_map/ppermute | solution.py:664
  14.0 3.2 %collective-permute-done.1.refs_1_ = f32[8,640]{1,0:T(8,128)S(1)} collective-permute-done((f32[8,640]{1,0:T(8,128)S(1)}, f32[8,640]{1,0:T(8,128)S(1)}, u32[]{:S(2)}, u32[]{:S(2)}) %collective-permute-start.1) | collective-permute-done | bytes 20512 | tf_op jit(solution)/shard_map/ppermute | solution.py:664
  17.1 1.1 cross.1
  18.2 10.1 %all-to-all-start = ((f32[16,8,512]{2,1,0:T(8,128)}), f32[16,8,512]{2,1,0:T(8,128)S(1)}, u32[]{:S(2)}, u32[]{:S(2)}) async-start(f32[16,8,512]{2,1,0:T(8,128)} %get-tuple-element.49), calls=%async_computation | async-start | bytes 524288 | tf_op jit(solution)/shard_map/all_to_all | solution.py:668
  28.3 0.7 pad_maximum_fusion.refs_5_
  29.0 0.8 copy-done
  29.8 0.8 copy-done.1
  30.6 0.7 copy-done.2
  31.3 0.7 copy-done.3
  32.0 0.7 copy-done.4
  32.7 0.4 prepare.1
  33.1 3.3 %all-to-all-done.refs_0_ = f32[16,8,512]{2,1,0:T(8,128)S(1)} async-done(((f32[16,8,512]{2,1,0:T(8,128)}), f32[16,8,512]{2,1,0:T(8,128)S(1)}, u32[]{:S(2)}, u32[]{:S(2)}) %all-to-all-start) | async-done | bytes 262176 | tf_op jit(solution)/shard_map/all_to_all | solution.py:668
  36.4 4.0 %env.1 = (f32[8,512]{1,0:T(8,128)S(1)}, s32[2,128]{1,0:T(2,128)S(1)}, s32[2,256]{1,0:T(2,128)S(1)}, f32[32,512]{1,0:T(8,128)S(1)}, f32[32,128]{1,0:T(8,128)S(1)}...) custom-call(f32[16,8,512]{2,1,0:T(8,128)S(1)} %all-to-all-done.refs_, ...), custom_call_target="tpu_custom_call" | custom-call | tf_op jit(solution)/shard_map/env/pallas_call | solution.py:604
  40.3 3.4 %collective-permute-start.2 = (f32[32,128]{1,0:T(8,128)S(1)}, f32[32,128]{1,0:T(8,128)S(1)}, u32[]{:S(2)}, u32[]{:S(2)}) collective-permute-start(f32[32,128]{1,0:T(8,128)S(1)} %get-tuple-element.55), channel_id=1, source_target_pairs={{0,8},{8,0},{16,24},{24,16},{32,40},{40,32},{48,56},{56,48},{64,72... | collective-permute-start | bytes 49160 | tf_op jit(solution)/shard_map/ppermute | solution.py:632
  43.8 1.9 %collective-permute-start.3 = (f32[32,128]{1,0:T(8,128)S(1)}, f32[32,128]{1,0:T(8,128)S(1)}, u32[]{:S(2)}, u32[]{:S(2)}) collective-permute-start(f32[32,128]{1,0:T(8,128)S(1)} %get-tuple-element.56), channel_id=1, source_target_pairs={{0,504},{8,16},{16,8},{24,32},{32,24},{40,48},{48,40},{56,64},{64,... | collective-permute-start | bytes 49160 | tf_op jit(solution)/shard_map/ppermute | solution.py:633
  45.7 1.5 %slope0.1.refs_2_.refs_5_ = f32[32,64,256]{2,1,0:T(8,128)S(1)} custom-call(f32[32,512]{1,0:T(8,128)S(1)} %get-tuple-element.57.refs_0_, f32[4,32,512]{2,1,0:T(8,128)S(1)} %get-tuple-element.58.refs_1_.refs_7_.refs_8_, bf16[64,32]{1,0:T(8,128)(2,1)S(1)} %get-tuple-element.52.refs_3_.refs_2_), custom_call_target="tpu_custom_call" | custom-call | tf_op jit(solution)/shard_map/slope0/pallas_call | solution.py:604
  47.2 0.0 collective-permute-done.2.refs_1_
  47.2 1.6 %collective-permute-done.3.refs_2_ = f32[32,128]{1,0:T(8,128)S(1)} collective-permute-done((f32[32,128]{1,0:T(8,128)S(1)}, f32[32,128]{1,0:T(8,128)S(1)}, u32[]{:S(2)}, u32[]{:S(2)}) %collective-permute-start.3) | collective-permute-done | bytes 16416 | tf_op jit(solution)/shard_map/ppermute | solution.py:633
  48.8 0.2 ghost_embed.1
  49.0 2.4 %collective-permute-start.4 = (f32[32,256]{1,0:T(8,128)S(1)}, f32[32,256]{1,0:T(8,128)S(1)}, u32[]{:S(2)}, u32[]{:S(2)}) collective-permute-start(f32[32,256]{1,0:T(8,128)S(1)} %get-tuple-element.62), channel_id=1, source_target_pairs={{0,1},{1,0},{2,3},{3,2},{4,5},{5,4},{6,7},{7,6},{8,9},{9,8},{10,11... | collective-permute-start | bytes 98312 | tf_op jit(solution)/shard_map/ppermute | solution.py:632
  51.4 4.4 %collective-permute-start.5 = (f32[32,256]{1,0:T(8,128)S(1)}, f32[32,256]{1,0:T(8,128)S(1)}, u32[]{:S(2)}, u32[]{:S(2)}) collective-permute-start(f32[32,256]{1,0:T(8,128)S(1)} %get-tuple-element.63), channel_id=1, source_target_pairs={{0,7},{1,2},{2,1},{3,4},{4,3},{5,6},{6,5},{7,0},{8,15},{9,10},{10,... | collective-permute-start | bytes 98312 | tf_op jit(solution)/shard_map/ppermute | solution.py:633
  55.9 2.3 %first.1.refs_6_ = f32[32,64,512]{2,1,0:T(8,128)S(1)} custom-call(bf16[32,128,512]{2,1,0:T(8,128)(2,1)S(1)} %get-tuple-element.64.refs_0_, bf16[128,128]{1,0:T(8,128)(2,1)S(1)} %get-tuple-element.65.refs_1_, f32[64,8]{1,0:T(8,128)S(1)} %get-tuple-element.66.refs_2_.refs_10_), custom_call_target="tpu_custom_call" | custom-call | tf_op jit(solution)/shard_map/first/pallas_call | solution.py:604
  58.2 0.0 collective-permute-done.4.refs_3_
  58.2 1.5 %collective-permute-done.5.refs_4_ = f32[32,256]{1,0:T(8,128)S(1)} collective-permute-done((f32[32,256]{1,0:T(8,128)S(1)}, f32[32,256]{1,0:T(8,128)S(1)}, u32[]{:S(2)}, u32[]{:S(2)}) %collective-permute-start.5) | collective-permute-done | bytes 32800 | tf_op jit(solution)/shard_map/ppermute | solution.py:633
  59.7 9.9 %pair.1 = (bf16[32,128,512]{2,1,0:T(8,128)(2,1)S(1)}, f32[32,512]{1,0:T(8,128)S(1)}, f32[32,768]{1,0:T(8,128)S(1)}, f32[32,192]{1,0:T(8,128)S(1)}, f32[32,192]{1,0:T(8,128)S(1)}) custom-call(f32[32,512]{1,0:T(8,128)S(1)} %get-tuple-element.54.refs_0_, f32[32,128]{1,0:T(8,128)S(1)} %collective-permute-done.2.refs_1_, ...), custom_call_target="tpu_custom_call" | custom-call | tf_op jit(solution)/shard_map/pair/pallas_call | solution.py:604
  69.6 3.2 %collective-permute-start.6 = (f32[32,192]{1,0:T(8,128)S(1)}, f32[32,192]{1,0:T(8,128)S(1)}, u32[]{:S(2)}, u32[]{:S(2)}) collective-permute-start(f32[32,192]{1,0:T(8,128)S(1)} %get-tuple-element.70), channel_id=1, source_target_pairs={{0,1},{1,0},{2,3},{3,2},{4,5},{5,4},{6,7},{7,6},{8,9},{9,8},{10,11... | collective-permute-start | bytes 73736 | tf_op jit(solution)/shard_map/ppermute | solution.py:632
  72.8 3.2 %collective-permute-start.7 = (f32[32,192]{1,0:T(8,128)S(1)}, f32[32,192]{1,0:T(8,128)S(1)}, u32[]{:S(2)}, u32[]{:S(2)}) collective-permute-start(f32[32,192]{1,0:T(8,128)S(1)} %get-tuple-element.71), channel_id=1, source_target_pairs={{0,7},{1,2},{2,1},{3,4},{4,3},{5,6},{6,5},{7,0},{8,15},{9,10},{10,... | collective-permute-start | bytes 73736 | tf_op jit(solution)/shard_map/ppermute | solution.py:633
  76.0 1.5 %slope1.1.refs_3_.refs_6_ = f32[32,64,256]{2,1,0:T(8,128)S(1)} custom-call(f32[32,512]{1,0:T(8,128)S(1)} %get-tuple-element.57.refs_0_, f32[4,32,512]{2,1,0:T(8,128)S(1)} %get-tuple-element.58.refs_1_.refs_7_.refs_8_, bf16[64,32]{1,0:T(8,128)(2,1)S(1)} %get-tuple-element.52.refs_3_.refs_2_), custom_call_target="tpu_custom_call" | custom-call | tf_op jit(solution)/shard_map/slope1/pallas_call | solution.py:604
  77.5 0.0 collective-permute-done.6.refs_1_
  77.5 3.5 %collective-permute-done.7.refs_2_ = f32[32,192]{1,0:T(8,128)S(1)} collective-permute-done((f32[32,192]{1,0:T(8,128)S(1)}, f32[32,192]{1,0:T(8,128)S(1)}, u32[]{:S(2)}, u32[]{:S(2)}) %collective-permute-start.7) | collective-permute-done | bytes 24608 | tf_op jit(solution)/shard_map/ppermute | solution.py:633
  81.1 0.8 fold_embed.1
  81.9 6.9 %collective-permute-start.8 = (f32[32,128]{1,0:T(8,128)S(1)}, f32[32,128]{1,0:T(8,128)S(1)}, u32[]{:S(2)}, u32[]{:S(2)}) collective-permute-start(f32[32,128]{1,0:T(8,128)S(1)} %get-tuple-element.75), channel_id=1, source_target_pairs={{0,8},{8,0},{16,24},{24,16},{32,40},{40,32},{48,56},{56,48},{64,72... | collective-permute-start | bytes 49160 | tf_op jit(solution)/shard_map/ppermute | solution.py:632
  88.8 1.9 %collective-permute-start.9 = (f32[32,128]{1,0:T(8,128)S(1)}, f32[32,128]{1,0:T(8,128)S(1)}, u32[]{:S(2)}, u32[]{:S(2)}) collective-permute-start(f32[32,128]{1,0:T(8,128)S(1)} %get-tuple-element.76), channel_id=1, source_target_pairs={{0,504},{8,16},{16,8},{24,32},{32,24},{40,48},{48,40},{56,64},{64,... | collective-permute-start | bytes 49160 | tf_op jit(solution)/shard_map/ppermute | solution.py:633
  90.7 2.4 %rise.1.refs_7_ = f32[32,512]{1,0:T(8,128)S(1)} custom-call(bf16[32,128,512]{2,1,0:T(8,128)(2,1)S(1)} %get-tuple-element.81.refs_0_, f32[32,512]{1,0:T(8,128)S(1)} %get-tuple-element.82.refs_1_, f32[32,64,256]{2,1,0:T(8,128)S(1)} %slope0.1.refs_2_.refs_5_, f32[32,64,256]{2,1,0:T(8,128)S(1)} %slope1.1.refs_3_.refs_6_, ...), custom_call_target="tpu_custom_call" | custom-call | tf_op jit(solution)/shard_map/rise/pallas_call | solution.py:604
  93.1 0.7 collective-permute-done.9.refs_2_
  93.8 4.5 %force.1 = (f32[8,768]{1,0:T(8,128)S(1)}, f32[8,192]{1,0:T(8,128)S(1)}, f32[8,192]{1,0:T(8,128)S(1)}) custom-call(f32[32,512]{1,0:T(8,128)S(1)} %get-tuple-element.74.refs_0_, f32[32,128]{1,0:T(8,128)S(1)} %collective-permute-done.8.refs_1_, f32[32,128]{1,0:T(8,128)S(1)} %collective-permute-done.9.refs_2_, s32[2,128]{1,0:T(2,128)S(1)} %get-tuple-element.77.refs_3_, ...), custom_call_target="tpu_custom_call" | custom-call | tf_op jit(solution)/shard_map/force/pallas_call | solution.py:604
  98.4 2.6 %collective-permute-start.10 = (f32[8,192]{1,0:T(8,128)S(1)}, f32[8,192]{1,0:T(8,128)S(1)}, u32[]{:S(2)}, u32[]{:S(2)}) collective-permute-start(f32[8,192]{1,0:T(8,128)S(1)} %get-tuple-element.85), channel_id=1, source_target_pairs={{0,1},{1,0},{2,3},{3,2},{4,5},{5,4},{6,7},{7,6},{8,9},{9,8},{10,11... | collective-permute-start | bytes 18440 | tf_op jit(solution)/shard_map/ppermute | solution.py:632
  101.0 4.6 %collective-permute-start.11 = (f32[8,192]{1,0:T(8,128)S(1)}, f32[8,192]{1,0:T(8,128)S(1)}, u32[]{:S(2)}, u32[]{:S(2)}) collective-permute-start(f32[8,192]{1,0:T(8,128)S(1)} %get-tuple-element.86), channel_id=1, source_target_pairs={{0,7},{1,2},{2,1},{3,4},{4,3},{5,6},{6,5},{7,0},{8,15},{9,10},{10,... | collective-permute-start | bytes 18440 | tf_op jit(solution)/shard_map/ppermute | solution.py:633
  105.6 3.4 %collective-permute-done.11.refs_2_ = f32[8,192]{1,0:T(8,128)S(1)} collective-permute-done((f32[8,192]{1,0:T(8,128)S(1)}, f32[8,192]{1,0:T(8,128)S(1)}, u32[]{:S(2)}, u32[]{:S(2)}) %collective-permute-start.11) | collective-permute-done | bytes 6176 | tf_op jit(solution)/shard_map/ppermute | solution.py:633
  109.0 0.7 fold_force.1
  109.7 5.5 %collective-permute-start.12 = (f32[8,128]{1,0:T(8,128)S(1)}, f32[8,128]{1,0:T(8,128)S(1)}, u32[]{:S(2)}, u32[]{:S(2)}) collective-permute-start(f32[8,128]{1,0:T(8,128)S(1)} %get-tuple-element.88), channel_id=1, source_target_pairs={{0,8},{8,0},{16,24},{24,16},{32,40},{40,32},{48,56},{56,48},{64,72... | collective-permute-start | bytes 12296 | tf_op jit(solution)/shard_map/ppermute | solution.py:632
  115.2 1.9 %collective-permute-start.13 = (f32[8,128]{1,0:T(8,128)S(1)}, f32[8,128]{1,0:T(8,128)S(1)}, u32[]{:S(2)}, u32[]{:S(2)}) collective-permute-start(f32[8,128]{1,0:T(8,128)S(1)} %get-tuple-element.89), channel_id=1, source_target_pairs={{0,504},{8,16},{16,8},{24,32},{32,24},{40,48},{48,40},{56,64},{64,... | collective-permute-start | bytes 12296 | tf_op jit(solution)/shard_map/ppermute | solution.py:633
  117.1 3.0 %collective-permute-done.13.refs_2_ = f32[8,128]{1,0:T(8,128)S(1)} collective-permute-done((f32[8,128]{1,0:T(8,128)S(1)}, f32[8,128]{1,0:T(8,128)S(1)}, u32[]{:S(2)}, u32[]{:S(2)}) %collective-permute-start.13) | collective-permute-done | bytes 4128 | tf_op jit(solution)/shard_map/ppermute | solution.py:633
  120.1 0.9 final.1
  (9 shorter events, 0.0 us)
Async XLA Ops:
  2.2 9.8 %collective-permute-start = (f32[8,128]{1,0:T(8,128)}, f32[8,128]{1,0:T(8,128)S(1)}, u32[]{:S(2)}, u32[]{:S(2)}) collective-permute-start(f32[8,128]{1,0:T(8,128)} %get-tuple-element.48), channel_id=1, source_target_pairs={{0,8},{8,0},{16,24},{24,16},{32,40},{40,32},{48,56},{56,48},{64,72... | collective-permute-start | bytes 12296 | tf_op jit(solution)/shard_map/ppermute | solution.py:662
  12.0 5.1 %collective-permute-start.1 = (f32[8,640]{1,0:T(8,128)S(1)}, f32[8,640]{1,0:T(8,128)S(1)}, u32[]{:S(2)}, u32[]{:S(2)}) collective-permute-start(f32[8,640]{1,0:T(8,128)S(1)} %constant_dynamic-update-slice_fusion.refs_0_), channel_id=1, source_target_pairs={{0,504},{8,16},{16,8},{24,32},{32,24},{40,48},{48,40},{56,64},{64,... | collective-permute-start | bytes 61448 | tf_op jit(solution)/shard_map/ppermute | solution.py:664
  18.2 18.2 %all-to-all-start = ((f32[16,8,512]{2,1,0:T(8,128)}), f32[16,8,512]{2,1,0:T(8,128)S(1)}, u32[]{:S(2)}, u32[]{:S(2)}) async-start(f32[16,8,512]{2,1,0:T(8,128)} %get-tuple-element.49), calls=%async_computation | async-start | bytes 524288 | tf_op jit(solution)/shard_map/all_to_all | solution.py:668
  29.0 0.8 copy-start
  29.8 0.8 copy-start.1
  30.6 0.7 copy-start.2
  31.3 0.7 copy-start.3
  32.0 0.7 copy-start.4
  40.3 6.8 %collective-permute-start.2 = (f32[32,128]{1,0:T(8,128)S(1)}, f32[32,128]{1,0:T(8,128)S(1)}, u32[]{:S(2)}, u32[]{:S(2)}) collective-permute-start(f32[32,128]{1,0:T(8,128)S(1)} %get-tuple-element.55), channel_id=1, source_target_pairs={{0,8},{8,0},{16,24},{24,16},{32,40},{40,32},{48,56},{56,48},{64,72... | collective-permute-start | bytes 49160 | tf_op jit(solution)/shard_map/ppermute | solution.py:632
  43.8 5.1 %collective-permute-start.3 = (f32[32,128]{1,0:T(8,128)S(1)}, f32[32,128]{1,0:T(8,128)S(1)}, u32[]{:S(2)}, u32[]{:S(2)}) collective-permute-start(f32[32,128]{1,0:T(8,128)S(1)} %get-tuple-element.56), channel_id=1, source_target_pairs={{0,504},{8,16},{16,8},{24,32},{32,24},{40,48},{48,40},{56,64},{64,... | collective-permute-start | bytes 49160 | tf_op jit(solution)/shard_map/ppermute | solution.py:633
  49.0 9.2 %collective-permute-start.4 = (f32[32,256]{1,0:T(8,128)S(1)}, f32[32,256]{1,0:T(8,128)S(1)}, u32[]{:S(2)}, u32[]{:S(2)}) collective-permute-start(f32[32,256]{1,0:T(8,128)S(1)} %get-tuple-element.62), channel_id=1, source_target_pairs={{0,1},{1,0},{2,3},{3,2},{4,5},{5,4},{6,7},{7,6},{8,9},{9,8},{10,11... | collective-permute-start | bytes 98312 | tf_op jit(solution)/shard_map/ppermute | solution.py:632
  51.4 8.3 %collective-permute-start.5 = (f32[32,256]{1,0:T(8,128)S(1)}, f32[32,256]{1,0:T(8,128)S(1)}, u32[]{:S(2)}, u32[]{:S(2)}) collective-permute-start(f32[32,256]{1,0:T(8,128)S(1)} %get-tuple-element.63), channel_id=1, source_target_pairs={{0,7},{1,2},{2,1},{3,4},{4,3},{5,6},{6,5},{7,0},{8,15},{9,10},{10,... | collective-permute-start | bytes 98312 | tf_op jit(solution)/shard_map/ppermute | solution.py:633
  69.6 7.9 %collective-permute-start.6 = (f32[32,192]{1,0:T(8,128)S(1)}, f32[32,192]{1,0:T(8,128)S(1)}, u32[]{:S(2)}, u32[]{:S(2)}) collective-permute-start(f32[32,192]{1,0:T(8,128)S(1)} %get-tuple-element.70), channel_id=1, source_target_pairs={{0,1},{1,0},{2,3},{3,2},{4,5},{5,4},{6,7},{7,6},{8,9},{9,8},{10,11... | collective-permute-start | bytes 73736 | tf_op jit(solution)/shard_map/ppermute | solution.py:632
  72.8 8.3 %collective-permute-start.7 = (f32[32,192]{1,0:T(8,128)S(1)}, f32[32,192]{1,0:T(8,128)S(1)}, u32[]{:S(2)}, u32[]{:S(2)}) collective-permute-start(f32[32,192]{1,0:T(8,128)S(1)} %get-tuple-element.71), channel_id=1, source_target_pairs={{0,7},{1,2},{2,1},{3,4},{4,3},{5,6},{6,5},{7,0},{8,15},{9,10},{10,... | collective-permute-start | bytes 73736 | tf_op jit(solution)/shard_map/ppermute | solution.py:633
  81.9 11.2 %collective-permute-start.8 = (f32[32,128]{1,0:T(8,128)S(1)}, f32[32,128]{1,0:T(8,128)S(1)}, u32[]{:S(2)}, u32[]{:S(2)}) collective-permute-start(f32[32,128]{1,0:T(8,128)S(1)} %get-tuple-element.75), channel_id=1, source_target_pairs={{0,8},{8,0},{16,24},{24,16},{32,40},{40,32},{48,56},{56,48},{64,72... | collective-permute-start | bytes 49160 | tf_op jit(solution)/shard_map/ppermute | solution.py:632
  88.8 5.1 %collective-permute-start.9 = (f32[32,128]{1,0:T(8,128)S(1)}, f32[32,128]{1,0:T(8,128)S(1)}, u32[]{:S(2)}, u32[]{:S(2)}) collective-permute-start(f32[32,128]{1,0:T(8,128)S(1)} %get-tuple-element.76), channel_id=1, source_target_pairs={{0,504},{8,16},{16,8},{24,32},{32,24},{40,48},{48,40},{56,64},{64,... | collective-permute-start | bytes 49160 | tf_op jit(solution)/shard_map/ppermute | solution.py:633
  98.4 7.2 %collective-permute-start.10 = (f32[8,192]{1,0:T(8,128)S(1)}, f32[8,192]{1,0:T(8,128)S(1)}, u32[]{:S(2)}, u32[]{:S(2)}) collective-permute-start(f32[8,192]{1,0:T(8,128)S(1)} %get-tuple-element.85), channel_id=1, source_target_pairs={{0,1},{1,0},{2,3},{3,2},{4,5},{5,4},{6,7},{7,6},{8,9},{9,8},{10,11... | collective-permute-start | bytes 18440 | tf_op jit(solution)/shard_map/ppermute | solution.py:632
  101.0 8.0 %collective-permute-start.11 = (f32[8,192]{1,0:T(8,128)S(1)}, f32[8,192]{1,0:T(8,128)S(1)}, u32[]{:S(2)}, u32[]{:S(2)}) collective-permute-start(f32[8,192]{1,0:T(8,128)S(1)} %get-tuple-element.86), channel_id=1, source_target_pairs={{0,7},{1,2},{2,1},{3,4},{4,3},{5,6},{6,5},{7,0},{8,15},{9,10},{10,... | collective-permute-start | bytes 18440 | tf_op jit(solution)/shard_map/ppermute | solution.py:633
  109.7 7.4 %collective-permute-start.12 = (f32[8,128]{1,0:T(8,128)S(1)}, f32[8,128]{1,0:T(8,128)S(1)}, u32[]{:S(2)}, u32[]{:S(2)}) collective-permute-start(f32[8,128]{1,0:T(8,128)S(1)} %get-tuple-element.88), channel_id=1, source_target_pairs={{0,8},{8,0},{16,24},{24,16},{32,40},{40,32},{48,56},{56,48},{64,72... | collective-permute-start | bytes 12296 | tf_op jit(solution)/shard_map/ppermute | solution.py:632
  115.2 4.9 %collective-permute-start.13 = (f32[8,128]{1,0:T(8,128)S(1)}, f32[8,128]{1,0:T(8,128)S(1)}, u32[]{:S(2)}, u32[]{:S(2)}) collective-permute-start(f32[8,128]{1,0:T(8,128)S(1)} %get-tuple-element.89), channel_id=1, source_target_pairs={{0,504},{8,16},{16,8},{24,32},{32,24},{40,48},{48,40},{56,64},{64,... | collective-permute-start | bytes 12296 | tf_op jit(solution)/shard_map/ppermute | solution.py:633

commit v6 on v5

--- a/solution.py
+++ b/solution.py
@@ -34,7 +34,7 @@
 GROUP = 4
 PAIR_GROUP = 16
 SPAN = 2
-FORCE_GROUP = 8
+FORCE_GROUP = 16
 UNROLL_ENV = 8
 ENV_WIDTH = 256
 ENV_TURNS = 16
@@ -628,10 +628,10 @@
 
 
 def exchange(axis, one, two):
-    return (
-        lax.ppermute(one, axis, swap(axis, True)),
-        lax.ppermute(two, axis, swap(axis, False)),
-    )
+    two = lax.ppermute(two, axis, swap(axis, False))
+    one = lax.ppermute(one, axis, swap(axis, True))
+    two, one = lax.optimization_barrier((two, one))
+    return one, two
 
 
 def on_device(

time: 122 us -> 116 us (0.951)
  waiting for transfers between devices: 20.6 us -> 15.4 us
    ppermute x12, waiting for transfers between devices: 13.8 us -> 8.61 us  [the longest x6 6.96 us: exchange(): one = lax.ppermute(one, axis, swap(axis, True))]
  transfers between devices with their start and end apart: 15 -> 15, of which waited for: 9 -> 8; matrix products, arithmetic and copies ran while one was open for 1% -> 1% of each run, Pallas kernels for 7% -> 7%
where the time goes in v6:
time: 116 us; the launch traced here: 115 us
  starting transfers between devices  61.8 us (53%)
  Pallas kernels  31.5 us (27%)
  waiting for transfers between devices  15.4 us (13%)
  local copies, waits for them, and re-layouts  4.44 us (4%)
    pallas_call x14, Pallas kernels, call(): pl.pallas_call(placed, name=name, out_shape=[jax.ShapeDtypeStruct(shape,...  31.5 us
    ppermute x6, starting transfers between devices, exchange(): one = lax.ppermute(one, axis, swap(axis, True))  20.7 us
    ppermute x6, starting transfers between devices, exchange(): two = lax.ppermute(two, axis, swap(axis, False))  20.4 us
    all_to_all x1, starting transfers between devices, on_device(): lax.all_to_all(blocks, ('gx', 'gy'), 0, 0, axis_index_groups=members)  10.1 us
    ppermute x1, starting transfers between devices, on_device(): message = lax.ppermute(message, 'gx', swap('gx', True))  8.79 us
    ppermute x6, waiting for transfers between devices, exchange(): one = lax.ppermute(one, axis, swap(axis, True))  6.96 us
    unnamed x11, local copies, waits for them, and re-layouts  4.44 us
    all_to_all x1, waiting for transfers between devices, on_device(): lax.all_to_all(blocks, ('gx', 'gy'), 0, 0, axis_index_groups=members)  3.3 us
  transfers between devices with their start and end apart: 15, of which 8 were waited for; matrix products, arithmetic and copies ran while one was open for 1% of the time, Pallas kernels for 7%

profile of v6, /device:TPU:1, one launch (start us, length us, event | category | flops | bytes accessed | tf_op | source)
XLA Modules:
  0.0 114.7 jit_solution(10168946225722397883)
XLA Ops:
  0.6 1.6 %start.1 = (f32[8,512]{1,0:T(8,128)}, f32[8,128]{1,0:T(8,128)}) custom-call(f32[3,512]{1,0:T(4,128)} %refs_0_.2, f32[3,512]{1,0:T(4,128)} %refs_1_.1, f32[3,512]{1,0:T(4,128)} %refs_2_.2, s32[1,2,128]{2,1,0:T(2,128)} %refs_3_.1, s32[1,2,192]{2,1,0:T(2,128)} %refs_4_.2, s32[1,2,8]{2,1,0:T(2,128)} %refs_5_.1, s32[1,2,8]{2,1,0:T(2,128)} %refs_6_.1), custom_call_target="tpu_custom_call" | custom-call | tf_op jit(solution)/shard_map/start/pallas_call | solution.py:604
  2.2 8.8 %collective-permute-start = (f32[8,128]{1,0:T(8,128)}, f32[8,128]{1,0:T(8,128)S(1)}, u32[]{:S(2)}, u32[]{:S(2)}) collective-permute-start(f32[8,128]{1,0:T(8,128)} %get-tuple-element.60), channel_id=1, source_target_pairs={{0,8},{8,0},{16,24},{24,16},{32,40},{40,32},{48,56},{56,48},{64,72... | collective-permute-start | bytes 12296 | tf_op jit(solution)/shard_map/ppermute | solution.py:662
  11.0 0.7 constant_dynamic-update-slice_fusion.1
  11.7 0.3 collective-permute-done
  12.0 1.9 %collective-permute-start.1 = (f32[8,640]{1,0:T(8,128)S(1)}, f32[8,640]{1,0:T(8,128)S(1)}, u32[]{:S(2)}, u32[]{:S(2)}) collective-permute-start(f32[8,640]{1,0:T(8,128)S(1)} %constant_dynamic-update-slice_fusion.refs_0_), channel_id=1, source_target_pairs={{0,504},{8,16},{16,8},{24,32},{32,24},{40,48},{48,40},{56,64},{64,... | collective-permute-start | bytes 61448 | tf_op jit(solution)/shard_map/ppermute | solution.py:664
  14.0 3.2 %collective-permute-done.1.refs_1_ = f32[8,640]{1,0:T(8,128)S(1)} collective-permute-done((f32[8,640]{1,0:T(8,128)S(1)}, f32[8,640]{1,0:T(8,128)S(1)}, u32[]{:S(2)}, u32[]{:S(2)}) %collective-permute-start.1) | collective-permute-done | bytes 20512 | tf_op jit(solution)/shard_map/ppermute | solution.py:664
  17.1 1.1 cross.1
  18.2 10.1 %all-to-all-start = ((f32[16,8,512]{2,1,0:T(8,128)}), f32[16,8,512]{2,1,0:T(8,128)S(1)}, u32[]{:S(2)}, u32[]{:S(2)}) async-start(f32[16,8,512]{2,1,0:T(8,128)} %get-tuple-element.61), calls=%async_computation | async-start | bytes 524288 | tf_op jit(solution)/shard_map/all_to_all | solution.py:668
  28.3 0.7 pad_maximum_fusion.refs_5_
  29.0 0.8 copy-done
  29.8 0.8 copy-done.1
  30.6 0.7 copy-done.2
  31.3 0.7 copy-done.3
  32.0 0.7 copy-done.4
  32.7 0.4 prepare.1
  33.1 3.3 %all-to-all-done.refs_0_ = f32[16,8,512]{2,1,0:T(8,128)S(1)} async-done(((f32[16,8,512]{2,1,0:T(8,128)}), f32[16,8,512]{2,1,0:T(8,128)S(1)}, u32[]{:S(2)}, u32[]{:S(2)}) %all-to-all-start) | async-done | bytes 262176 | tf_op jit(solution)/shard_map/all_to_all | solution.py:668
  36.4 4.0 %env.1 = (f32[8,512]{1,0:T(8,128)S(1)}, s32[2,128]{1,0:T(2,128)S(1)}, s32[2,256]{1,0:T(2,128)S(1)}, f32[32,512]{1,0:T(8,128)S(1)}, f32[32,128]{1,0:T(8,128)S(1)}...) custom-call(f32[16,8,512]{2,1,0:T(8,128)S(1)} %all-to-all-done.refs_, ...), custom_call_target="tpu_custom_call" | custom-call | tf_op jit(solution)/shard_map/env/pallas_call | solution.py:604
  40.3 1.9 %collective-permute-start.2 = (f32[32,128]{1,0:T(8,128)S(1)}, f32[32,128]{1,0:T(8,128)S(1)}, u32[]{:S(2)}, u32[]{:S(2)}) collective-permute-start(f32[32,128]{1,0:T(8,128)S(1)} %get-tuple-element.67), channel_id=1, source_target_pairs={{0,504},{8,16},{16,8},{24,32},{32,24},{40,48},{48,40},{56,64},{64,... | collective-permute-start | bytes 49160 | tf_op jit(solution)/shard_map/ppermute | solution.py:631
  42.3 5.2 %collective-permute-start.3 = (f32[32,128]{1,0:T(8,128)S(1)}, f32[32,128]{1,0:T(8,128)S(1)}, u32[]{:S(2)}, u32[]{:S(2)}) collective-permute-start(f32[32,128]{1,0:T(8,128)S(1)} %get-tuple-element.68), channel_id=1, source_target_pairs={{0,8},{8,0},{16,24},{24,16},{32,40},{40,32},{48,56},{56,48},{64,72... | collective-permute-start | bytes 49160 | tf_op jit(solution)/shard_map/ppermute | solution.py:632
  47.5 1.5 %slope0.1.refs_2_.refs_5_ = f32[32,64,256]{2,1,0:T(8,128)S(1)} custom-call(f32[32,512]{1,0:T(8,128)S(1)} %get-tuple-element.71.refs_0_, f32[4,32,512]{2,1,0:T(8,128)S(1)} %get-tuple-element.72.refs_1_.refs_7_.refs_8_, bf16[64,32]{1,0:T(8,128)(2,1)S(1)} %get-tuple-element.64.refs_3_.refs_2_), custom_call_target="tpu_custom_call" | custom-call | tf_op jit(solution)/shard_map/slope0/pallas_call | solution.py:604
  49.0 0.0 collective-permute-done.2.refs_2_
  49.0 0.0 collective-permute-done.3.refs_1_
  49.0 0.2 ghost_embed.1
  49.2 4.4 %collective-permute-start.4 = (f32[32,256]{1,0:T(8,128)S(1)}, f32[32,256]{1,0:T(8,128)S(1)}, u32[]{:S(2)}, u32[]{:S(2)}) collective-permute-start(f32[32,256]{1,0:T(8,128)S(1)} %get-tuple-element.76), channel_id=1, source_target_pairs={{0,7},{1,2},{2,1},{3,4},{4,3},{5,6},{6,5},{7,0},{8,15},{9,10},{10,... | collective-permute-start | bytes 98312 | tf_op jit(solution)/shard_map/ppermute | solution.py:631
  53.7 2.4 %collective-permute-start.5 = (f32[32,256]{1,0:T(8,128)S(1)}, f32[32,256]{1,0:T(8,128)S(1)}, u32[]{:S(2)}, u32[]{:S(2)}) collective-permute-start(f32[32,256]{1,0:T(8,128)S(1)} %get-tuple-element.77), channel_id=1, source_target_pairs={{0,1},{1,0},{2,3},{3,2},{4,5},{5,4},{6,7},{7,6},{8,9},{9,8},{10,11... | collective-permute-start | bytes 98312 | tf_op jit(solution)/shard_map/ppermute | solution.py:632
  56.0 2.3 %first.1.refs_6_ = f32[32,64,512]{2,1,0:T(8,128)S(1)} custom-call(bf16[32,128,512]{2,1,0:T(8,128)(2,1)S(1)} %get-tuple-element.80.refs_0_, bf16[128,128]{1,0:T(8,128)(2,1)S(1)} %get-tuple-element.81.refs_1_, f32[64,8]{1,0:T(8,128)S(1)} %get-tuple-element.82.refs_2_.refs_10_), custom_call_target="tpu_custom_call" | custom-call | tf_op jit(solution)/shard_map/first/pallas_call | solution.py:604
  58.3 0.0 collective-permute-done.4.refs_4_
  58.3 1.5 %collective-permute-done.5.refs_3_ = f32[32,256]{1,0:T(8,128)S(1)} collective-permute-done((f32[32,256]{1,0:T(8,128)S(1)}, f32[32,256]{1,0:T(8,128)S(1)}, u32[]{:S(2)}, u32[]{:S(2)}) %collective-permute-start.5) | collective-permute-done | bytes 32800 | tf_op jit(solution)/shard_map/ppermute | solution.py:632
  59.8 9.9 %pair.1 = (bf16[32,128,512]{2,1,0:T(8,128)(2,1)S(1)}, f32[32,512]{1,0:T(8,128)S(1)}, f32[32,768]{1,0:T(8,128)S(1)}, f32[32,192]{1,0:T(8,128)S(1)}, f32[32,192]{1,0:T(8,128)S(1)}) custom-call(f32[32,512]{1,0:T(8,128)S(1)} %get-tuple-element.66.refs_0_, f32[32,128]{1,0:T(8,128)S(1)} %collective-permute-done.3.refs_1_, ...), custom_call_target="tpu_custom_call" | custom-call | tf_op jit(solution)/shard_map/pair/pallas_call | solution.py:604
  69.8 4.5 %collective-permute-start.6 = (f32[32,192]{1,0:T(8,128)S(1)}, f32[32,192]{1,0:T(8,128)S(1)}, u32[]{:S(2)}, u32[]{:S(2)}) collective-permute-start(f32[32,192]{1,0:T(8,128)S(1)} %get-tuple-element.86), channel_id=1, source_target_pairs={{0,7},{1,2},{2,1},{3,4},{4,3},{5,6},{6,5},{7,0},{8,15},{9,10},{10,... | collective-permute-start | bytes 73736 | tf_op jit(solution)/shard_map/ppermute | solution.py:631
  74.2 2.3 %collective-permute-start.7 = (f32[32,192]{1,0:T(8,128)S(1)}, f32[32,192]{1,0:T(8,128)S(1)}, u32[]{:S(2)}, u32[]{:S(2)}) collective-permute-start(f32[32,192]{1,0:T(8,128)S(1)} %get-tuple-element.87), channel_id=1, source_target_pairs={{0,1},{1,0},{2,3},{3,2},{4,5},{5,4},{6,7},{7,6},{8,9},{9,8},{10,11... | collective-permute-start | bytes 73736 | tf_op jit(solution)/shard_map/ppermute | solution.py:632
  76.5 1.5 %slope1.1.refs_3_.refs_6_ = f32[32,64,256]{2,1,0:T(8,128)S(1)} custom-call(f32[32,512]{1,0:T(8,128)S(1)} %get-tuple-element.71.refs_0_, f32[4,32,512]{2,1,0:T(8,128)S(1)} %get-tuple-element.72.refs_1_.refs_7_.refs_8_, bf16[64,32]{1,0:T(8,128)(2,1)S(1)} %get-tuple-element.64.refs_3_.refs_2_), custom_call_target="tpu_custom_call" | custom-call | tf_op jit(solution)/shard_map/slope1/pallas_call | solution.py:604
  78.0 0.0 collective-permute-done.6.refs_2_
  78.0 2.4 %collective-permute-done.7.refs_1_ = f32[32,192]{1,0:T(8,128)S(1)} collective-permute-done((f32[32,192]{1,0:T(8,128)S(1)}, f32[32,192]{1,0:T(8,128)S(1)}, u32[]{:S(2)}, u32[]{:S(2)}) %collective-permute-start.7) | collective-permute-done | bytes 24608 | tf_op jit(solution)/shard_map/ppermute | solution.py:632
  80.4 0.8 fold_embed.1
  81.2 3.2 %collective-permute-start.8 = (f32[32,128]{1,0:T(8,128)S(1)}, f32[32,128]{1,0:T(8,128)S(1)}, u32[]{:S(2)}, u32[]{:S(2)}) collective-permute-start(f32[32,128]{1,0:T(8,128)S(1)} %get-tuple-element.93), channel_id=1, source_target_pairs={{0,504},{8,16},{16,8},{24,32},{32,24},{40,48},{48,40},{56,64},{64,... | collective-permute-start | bytes 49160 | tf_op jit(solution)/shard_map/ppermute | solution.py:631
  84.4 3.7 %collective-permute-start.9 = (f32[32,128]{1,0:T(8,128)S(1)}, f32[32,128]{1,0:T(8,128)S(1)}, u32[]{:S(2)}, u32[]{:S(2)}) collective-permute-start(f32[32,128]{1,0:T(8,128)S(1)} %get-tuple-element.94), channel_id=1, source_target_pairs={{0,8},{8,0},{16,24},{24,16},{32,40},{40,32},{48,56},{56,48},{64,72... | collective-permute-start | bytes 49160 | tf_op jit(solution)/shard_map/ppermute | solution.py:632
  88.1 2.4 %rise.1.refs_7_ = f32[32,512]{1,0:T(8,128)S(1)} custom-call(bf16[32,128,512]{2,1,0:T(8,128)(2,1)S(1)} %get-tuple-element.101.refs_0_, f32[32,512]{1,0:T(8,128)S(1)} %get-tuple-element.102.refs_1_, f32[32,64,256]{2,1,0:T(8,128)S(1)} %slope0.1.refs_2_.refs_5_, f32[32,64,256]{2,1,0:T(8,128)S(1)} %slope1.1.refs_3_.refs_6_, ...), custom_call_target="tpu_custom_call" | custom-call | tf_op jit(solution)/shard_map/rise/pallas_call | solution.py:604
  90.5 4.3 %force.1 = (f32[8,768]{1,0:T(8,128)S(1)}, f32[8,192]{1,0:T(8,128)S(1)}, f32[8,192]{1,0:T(8,128)S(1)}) custom-call(f32[32,512]{1,0:T(8,128)S(1)} %get-tuple-element.92.refs_0_, f32[32,128]{1,0:T(8,128)S(1)} %collective-permute-done.9.refs_1_, f32[32,128]{1,0:T(8,128)S(1)} %collective-permute-done.8.refs_2_, s32[2,128]{1,0:T(2,128)S(1)} %get-tuple-element.97.refs_3_, ...), custom_call_target="tpu_custom_call" | custom-call | tf_op jit(solution)/shard_map/force/pallas_call | solution.py:604
  94.8 4.4 %collective-permute-start.10 = (f32[8,192]{1,0:T(8,128)S(1)}, f32[8,192]{1,0:T(8,128)S(1)}, u32[]{:S(2)}, u32[]{:S(2)}) collective-permute-start(f32[8,192]{1,0:T(8,128)S(1)} %get-tuple-element.105), channel_id=1, source_target_pairs={{0,7},{1,2},{2,1},{3,4},{4,3},{5,6},{6,5},{7,0},{8,15},{9,10},{10,... | collective-permute-start | bytes 18440 | tf_op jit(solution)/shard_map/ppermute | solution.py:631
  99.3 1.9 %collective-permute-start.11 = (f32[8,192]{1,0:T(8,128)S(1)}, f32[8,192]{1,0:T(8,128)S(1)}, u32[]{:S(2)}, u32[]{:S(2)}) collective-permute-start(f32[8,192]{1,0:T(8,128)S(1)} %get-tuple-element.106), channel_id=1, source_target_pairs={{0,1},{1,0},{2,3},{3,2},{4,5},{5,4},{6,7},{7,6},{8,9},{9,8},{10,11... | collective-permute-start | bytes 18440 | tf_op jit(solution)/shard_map/ppermute | solution.py:632
  101.2 1.6 %collective-permute-done.10.refs_2_ = f32[8,192]{1,0:T(8,128)S(1)} collective-permute-done((f32[8,192]{1,0:T(8,128)S(1)}, f32[8,192]{1,0:T(8,128)S(1)}, u32[]{:S(2)}, u32[]{:S(2)}) %collective-permute-start.10) | collective-permute-done | bytes 6176 | tf_op jit(solution)/shard_map/ppermute | solution.py:631
  102.8 2.3 %collective-permute-done.11.refs_1_ = f32[8,192]{1,0:T(8,128)S(1)} collective-permute-done((f32[8,192]{1,0:T(8,128)S(1)}, f32[8,192]{1,0:T(8,128)S(1)}, u32[]{:S(2)}, u32[]{:S(2)}) %collective-permute-start.11) | collective-permute-done | bytes 6176 | tf_op jit(solution)/shard_map/ppermute | solution.py:632
  105.2 0.7 fold_force.1
  105.9 1.9 %collective-permute-start.12 = (f32[8,128]{1,0:T(8,128)S(1)}, f32[8,128]{1,0:T(8,128)S(1)}, u32[]{:S(2)}, u32[]{:S(2)}) collective-permute-start(f32[8,128]{1,0:T(8,128)S(1)} %get-tuple-element.110), channel_id=1, source_target_pairs={{0,504},{8,16},{16,8},{24,32},{32,24},{40,48},{48,40},{56,64},{64,... | collective-permute-start | bytes 12296 | tf_op jit(solution)/shard_map/ppermute | solution.py:631
  107.8 5.1 %collective-permute-start.13 = (f32[8,128]{1,0:T(8,128)S(1)}, f32[8,128]{1,0:T(8,128)S(1)}, u32[]{:S(2)}, u32[]{:S(2)}) collective-permute-start(f32[8,128]{1,0:T(8,128)S(1)} %get-tuple-element.111), channel_id=1, source_target_pairs={{0,8},{8,0},{16,24},{24,16},{32,40},{40,32},{48,56},{56,48},{64,72... | collective-permute-start | bytes 12296 | tf_op jit(solution)/shard_map/ppermute | solution.py:632
  113.0 0.8 collective-permute-done.13.refs_1_
  113.8 0.9 final.1
  (9 shorter events, 0.0 us)
Async XLA Ops:
  2.2 9.8 %collective-permute-start = (f32[8,128]{1,0:T(8,128)}, f32[8,128]{1,0:T(8,128)S(1)}, u32[]{:S(2)}, u32[]{:S(2)}) collective-permute-start(f32[8,128]{1,0:T(8,128)} %get-tuple-element.60), channel_id=1, source_target_pairs={{0,8},{8,0},{16,24},{24,16},{32,40},{40,32},{48,56},{56,48},{64,72... | collective-permute-start | bytes 12296 | tf_op jit(solution)/shard_map/ppermute | solution.py:662
  12.0 5.1 %collective-permute-start.1 = (f32[8,640]{1,0:T(8,128)S(1)}, f32[8,640]{1,0:T(8,128)S(1)}, u32[]{:S(2)}, u32[]{:S(2)}) collective-permute-start(f32[8,640]{1,0:T(8,128)S(1)} %constant_dynamic-update-slice_fusion.refs_0_), channel_id=1, source_target_pairs={{0,504},{8,16},{16,8},{24,32},{32,24},{40,48},{48,40},{56,64},{64,... | collective-permute-start | bytes 61448 | tf_op jit(solution)/shard_map/ppermute | solution.py:664
  18.2 18.2 %all-to-all-start = ((f32[16,8,512]{2,1,0:T(8,128)}), f32[16,8,512]{2,1,0:T(8,128)S(1)}, u32[]{:S(2)}, u32[]{:S(2)}) async-start(f32[16,8,512]{2,1,0:T(8,128)} %get-tuple-element.61), calls=%async_computation | async-start | bytes 524288 | tf_op jit(solution)/shard_map/all_to_all | solution.py:668
  29.0 0.8 copy-start
  29.8 0.8 copy-start.1
  30.6 0.7 copy-start.2
  31.3 0.7 copy-start.3
  32.0 0.7 copy-start.4
  40.3 8.7 %collective-permute-start.2 = (f32[32,128]{1,0:T(8,128)S(1)}, f32[32,128]{1,0:T(8,128)S(1)}, u32[]{:S(2)}, u32[]{:S(2)}) collective-permute-start(f32[32,128]{1,0:T(8,128)S(1)} %get-tuple-element.67), channel_id=1, source_target_pairs={{0,504},{8,16},{16,8},{24,32},{32,24},{40,48},{48,40},{56,64},{64,... | collective-permute-start | bytes 49160 | tf_op jit(solution)/shard_map/ppermute | solution.py:631
  42.3 6.7 %collective-permute-start.3 = (f32[32,128]{1,0:T(8,128)S(1)}, f32[32,128]{1,0:T(8,128)S(1)}, u32[]{:S(2)}, u32[]{:S(2)}) collective-permute-start(f32[32,128]{1,0:T(8,128)S(1)} %get-tuple-element.68), channel_id=1, source_target_pairs={{0,8},{8,0},{16,24},{24,16},{32,40},{40,32},{48,56},{56,48},{64,72... | collective-permute-start | bytes 49160 | tf_op jit(solution)/shard_map/ppermute | solution.py:632
  49.2 9.1 %collective-permute-start.4 = (f32[32,256]{1,0:T(8,128)S(1)}, f32[32,256]{1,0:T(8,128)S(1)}, u32[]{:S(2)}, u32[]{:S(2)}) collective-permute-start(f32[32,256]{1,0:T(8,128)S(1)} %get-tuple-element.76), channel_id=1, source_target_pairs={{0,7},{1,2},{2,1},{3,4},{4,3},{5,6},{6,5},{7,0},{8,15},{9,10},{10,... | collective-permute-start | bytes 98312 | tf_op jit(solution)/shard_map/ppermute | solution.py:631
  53.7 6.2 %collective-permute-start.5 = (f32[32,256]{1,0:T(8,128)S(1)}, f32[32,256]{1,0:T(8,128)S(1)}, u32[]{:S(2)}, u32[]{:S(2)}) collective-permute-start(f32[32,256]{1,0:T(8,128)S(1)} %get-tuple-element.77), channel_id=1, source_target_pairs={{0,1},{1,0},{2,3},{3,2},{4,5},{5,4},{6,7},{7,6},{8,9},{9,8},{10,11... | collective-permute-start | bytes 98312 | tf_op jit(solution)/shard_map/ppermute | solution.py:632
  69.8 8.3 %collective-permute-start.6 = (f32[32,192]{1,0:T(8,128)S(1)}, f32[32,192]{1,0:T(8,128)S(1)}, u32[]{:S(2)}, u32[]{:S(2)}) collective-permute-start(f32[32,192]{1,0:T(8,128)S(1)} %get-tuple-element.86), channel_id=1, source_target_pairs={{0,7},{1,2},{2,1},{3,4},{4,3},{5,6},{6,5},{7,0},{8,15},{9,10},{10,... | collective-permute-start | bytes 73736 | tf_op jit(solution)/shard_map/ppermute | solution.py:631
  74.2 6.2 %collective-permute-start.7 = (f32[32,192]{1,0:T(8,128)S(1)}, f32[32,192]{1,0:T(8,128)S(1)}, u32[]{:S(2)}, u32[]{:S(2)}) collective-permute-start(f32[32,192]{1,0:T(8,128)S(1)} %get-tuple-element.87), channel_id=1, source_target_pairs={{0,1},{1,0},{2,3},{3,2},{4,5},{5,4},{6,7},{7,6},{8,9},{9,8},{10,11... | collective-permute-start | bytes 73736 | tf_op jit(solution)/shard_map/ppermute | solution.py:632
  81.2 9.3 %collective-permute-start.8 = (f32[32,128]{1,0:T(8,128)S(1)}, f32[32,128]{1,0:T(8,128)S(1)}, u32[]{:S(2)}, u32[]{:S(2)}) collective-permute-start(f32[32,128]{1,0:T(8,128)S(1)} %get-tuple-element.93), channel_id=1, source_target_pairs={{0,504},{8,16},{16,8},{24,32},{32,24},{40,48},{48,40},{56,64},{64,... | collective-permute-start | bytes 49160 | tf_op jit(solution)/shard_map/ppermute | solution.py:631
  84.4 6.1 %collective-permute-start.9 = (f32[32,128]{1,0:T(8,128)S(1)}, f32[32,128]{1,0:T(8,128)S(1)}, u32[]{:S(2)}, u32[]{:S(2)}) collective-permute-start(f32[32,128]{1,0:T(8,128)S(1)} %get-tuple-element.94), channel_id=1, source_target_pairs={{0,8},{8,0},{16,24},{24,16},{32,40},{40,32},{48,56},{56,48},{64,72... | collective-permute-start | bytes 49160 | tf_op jit(solution)/shard_map/ppermute | solution.py:632
  94.8 8.0 %collective-permute-start.10 = (f32[8,192]{1,0:T(8,128)S(1)}, f32[8,192]{1,0:T(8,128)S(1)}, u32[]{:S(2)}, u32[]{:S(2)}) collective-permute-start(f32[8,192]{1,0:T(8,128)S(1)} %get-tuple-element.105), channel_id=1, source_target_pairs={{0,7},{1,2},{2,1},{3,4},{4,3},{5,6},{6,5},{7,0},{8,15},{9,10},{10,... | collective-permute-start | bytes 18440 | tf_op jit(solution)/shard_map/ppermute | solution.py:631
  99.3 5.9 %collective-permute-start.11 = (f32[8,192]{1,0:T(8,128)S(1)}, f32[8,192]{1,0:T(8,128)S(1)}, u32[]{:S(2)}, u32[]{:S(2)}) collective-permute-start(f32[8,192]{1,0:T(8,128)S(1)} %get-tuple-element.106), channel_id=1, source_target_pairs={{0,1},{1,0},{2,3},{3,2},{4,5},{5,4},{6,7},{7,6},{8,9},{9,8},{10,11... | collective-permute-start | bytes 18440 | tf_op jit(solution)/shard_map/ppermute | solution.py:632
  105.9 7.1 %collective-permute-start.12 = (f32[8,128]{1,0:T(8,128)S(1)}, f32[8,128]{1,0:T(8,128)S(1)}, u32[]{:S(2)}, u32[]{:S(2)}) collective-permute-start(f32[8,128]{1,0:T(8,128)S(1)} %get-tuple-element.110), channel_id=1, source_target_pairs={{0,504},{8,16},{16,8},{24,32},{32,24},{40,48},{48,40},{56,64},{64,... | collective-permute-start | bytes 12296 | tf_op jit(solution)/shard_map/ppermute | solution.py:631
  107.8 6.0 %collective-permute-start.13 = (f32[8,128]{1,0:T(8,128)S(1)}, f32[8,128]{1,0:T(8,128)S(1)}, u32[]{:S(2)}, u32[]{:S(2)}) collective-permute-start(f32[8,128]{1,0:T(8,128)S(1)} %get-tuple-element.111), channel_id=1, source_target_pairs={{0,8},{8,0},{16,24},{24,16},{32,40},{40,32},{48,56},{56,48},{64,72... | collective-permute-start | bytes 12296 | tf_op jit(solution)/shard_map/ppermute | solution.py:632

commit v7 on v6

--- a/solution.py
+++ b/solution.py
@@ -31,7 +31,7 @@
 LEVELS = -(-EXT // HALF)
 BIG = 24 * 1024 * 1024
 WHOLE = 60 * 1024 * 1024
-GROUP = 4
+GROUP = 8
 PAIR_GROUP = 16
 SPAN = 2
 FORCE_GROUP = 16

time: 116 us -> 115 us (level)
  Pallas kernels: 31.5 us -> 30.3 us
    pallas_call x14, Pallas kernels: 31.5 us -> 30.3 us  [call(): pl.pallas_call(placed, name=name, out_shape=[jax.ShapeDtypeStruct(shape,...]
  transfers between devices with their start and end apart: 15 -> 15, of which waited for: 8 -> 8; matrix products, arithmetic and copies ran while one was open for 1% -> 1% of each run, Pallas kernels for 7% -> 6%
where the time goes in v7:
time: 115 us; the launch traced here: 114 us
  starting transfers between devices  61.8 us (54%)
  Pallas kernels  30.3 us (26%)
  waiting for transfers between devices  16 us (14%)
  local copies, waits for them, and re-layouts  4.44 us (4%)
    pallas_call x14, Pallas kernels, call(): pl.pallas_call(placed, name=name, out_shape=[jax.ShapeDtypeStruct(shape,...  30.3 us
    ppermute x6, starting transfers between devices, exchange(): one = lax.ppermute(one, axis, swap(axis, True))  20.7 us
    ppermute x6, starting transfers between devices, exchange(): two = lax.ppermute(two, axis, swap(axis, False))  20.4 us
    all_to_all x1, starting transfers between devices, on_device(): lax.all_to_all(blocks, ('gx', 'gy'), 0, 0, axis_index_groups=members)  10.1 us
    ppermute x1, starting transfers between devices, on_device(): message = lax.ppermute(message, 'gx', swap('gx', True))  8.79 us
    ppermute x6, waiting for transfers between devices, exchange(): one = lax.ppermute(one, axis, swap(axis, True))  7.54 us
    unnamed x11, local copies, waits for them, and re-layouts  4.44 us
    all_to_all x1, waiting for transfers between devices, on_device(): lax.all_to_all(blocks, ('gx', 'gy'), 0, 0, axis_index_groups=members)  3.3 us
  transfers between devices with their start and end apart: 15, of which 8 were waited for; matrix products, arithmetic and copies ran while one was open for 1% of the time, Pallas kernels for 6%

profile of v7, /device:TPU:1, one launch (start us, length us, event | category | flops | bytes accessed | tf_op | source)
XLA Modules:
  0.0 114.1 jit_solution(17165970346824671550)
XLA Ops:
  0.6 1.6 %start.1 = (f32[8,512]{1,0:T(8,128)}, f32[8,128]{1,0:T(8,128)}) custom-call(f32[3,512]{1,0:T(4,128)} %refs_0_.2, f32[3,512]{1,0:T(4,128)} %refs_1_.1, f32[3,512]{1,0:T(4,128)} %refs_2_.2, s32[1,2,128]{2,1,0:T(2,128)} %refs_3_.1, s32[1,2,192]{2,1,0:T(2,128)} %refs_4_.2, s32[1,2,8]{2,1,0:T(2,128)} %refs_5_.1, s32[1,2,8]{2,1,0:T(2,128)} %refs_6_.1), custom_call_target="tpu_custom_call" | custom-call | tf_op jit(solution)/shard_map/start/pallas_call | solution.py:604
  2.2 8.8 %collective-permute-start = (f32[8,128]{1,0:T(8,128)}, f32[8,128]{1,0:T(8,128)S(1)}, u32[]{:S(2)}, u32[]{:S(2)}) collective-permute-start(f32[8,128]{1,0:T(8,128)} %get-tuple-element.60), channel_id=1, source_target_pairs={{0,8},{8,0},{16,24},{24,16},{32,40},{40,32},{48,56},{56,48},{64,72... | collective-permute-start | bytes 12296 | tf_op jit(solution)/shard_map/ppermute | solution.py:662
  11.0 0.7 constant_dynamic-update-slice_fusion.1
  11.7 0.3 collective-permute-done
  12.0 1.9 %collective-permute-start.1 = (f32[8,640]{1,0:T(8,128)S(1)}, f32[8,640]{1,0:T(8,128)S(1)}, u32[]{:S(2)}, u32[]{:S(2)}) collective-permute-start(f32[8,640]{1,0:T(8,128)S(1)} %constant_dynamic-update-slice_fusion.refs_0_), channel_id=1, source_target_pairs={{0,504},{8,16},{16,8},{24,32},{32,24},{40,48},{48,40},{56,64},{64,... | collective-permute-start | bytes 61448 | tf_op jit(solution)/shard_map/ppermute | solution.py:664
  14.0 3.2 %collective-permute-done.1.refs_1_ = f32[8,640]{1,0:T(8,128)S(1)} collective-permute-done((f32[8,640]{1,0:T(8,128)S(1)}, f32[8,640]{1,0:T(8,128)S(1)}, u32[]{:S(2)}, u32[]{:S(2)}) %collective-permute-start.1) | collective-permute-done | bytes 20512 | tf_op jit(solution)/shard_map/ppermute | solution.py:664
  17.1 1.1 cross.1
  18.2 10.1 %all-to-all-start = ((f32[16,8,512]{2,1,0:T(8,128)}), f32[16,8,512]{2,1,0:T(8,128)S(1)}, u32[]{:S(2)}, u32[]{:S(2)}) async-start(f32[16,8,512]{2,1,0:T(8,128)} %get-tuple-element.61), calls=%async_computation | async-start | bytes 524288 | tf_op jit(solution)/shard_map/all_to_all | solution.py:668
  28.3 0.7 pad_maximum_fusion.refs_5_
  29.0 0.8 copy-done
  29.8 0.8 copy-done.1
  30.6 0.7 copy-done.2
  31.3 0.7 copy-done.3
  32.0 0.7 copy-done.4
  32.7 0.4 prepare.1
  33.1 3.3 %all-to-all-done.refs_0_ = f32[16,8,512]{2,1,0:T(8,128)S(1)} async-done(((f32[16,8,512]{2,1,0:T(8,128)}), f32[16,8,512]{2,1,0:T(8,128)S(1)}, u32[]{:S(2)}, u32[]{:S(2)}) %all-to-all-start) | async-done | bytes 262176 | tf_op jit(solution)/shard_map/all_to_all | solution.py:668
  36.4 4.0 %env.1 = (f32[8,512]{1,0:T(8,128)S(1)}, s32[2,128]{1,0:T(2,128)S(1)}, s32[2,256]{1,0:T(2,128)S(1)}, f32[32,512]{1,0:T(8,128)S(1)}, f32[32,128]{1,0:T(8,128)S(1)}...) custom-call(f32[16,8,512]{2,1,0:T(8,128)S(1)} %all-to-all-done.refs_, ...), custom_call_target="tpu_custom_call" | custom-call | tf_op jit(solution)/shard_map/env/pallas_call | solution.py:604
  40.3 1.9 %collective-permute-start.2 = (f32[32,128]{1,0:T(8,128)S(1)}, f32[32,128]{1,0:T(8,128)S(1)}, u32[]{:S(2)}, u32[]{:S(2)}) collective-permute-start(f32[32,128]{1,0:T(8,128)S(1)} %get-tuple-element.67), channel_id=1, source_target_pairs={{0,504},{8,16},{16,8},{24,32},{32,24},{40,48},{48,40},{56,64},{64,... | collective-permute-start | bytes 49160 | tf_op jit(solution)/shard_map/ppermute | solution.py:631
  42.3 5.2 %collective-permute-start.3 = (f32[32,128]{1,0:T(8,128)S(1)}, f32[32,128]{1,0:T(8,128)S(1)}, u32[]{:S(2)}, u32[]{:S(2)}) collective-permute-start(f32[32,128]{1,0:T(8,128)S(1)} %get-tuple-element.68), channel_id=1, source_target_pairs={{0,8},{8,0},{16,24},{24,16},{32,40},{40,32},{48,56},{56,48},{64,72... | collective-permute-start | bytes 49160 | tf_op jit(solution)/shard_map/ppermute | solution.py:632
  47.5 1.5 %slope0.1.refs_2_.refs_5_ = f32[32,64,256]{2,1,0:T(8,128)S(1)} custom-call(f32[32,512]{1,0:T(8,128)S(1)} %get-tuple-element.71.refs_0_, f32[4,32,512]{2,1,0:T(8,128)S(1)} %get-tuple-element.72.refs_1_.refs_7_.refs_8_, bf16[64,32]{1,0:T(8,128)(2,1)S(1)} %get-tuple-element.64.refs_3_.refs_2_), custom_call_target="tpu_custom_call" | custom-call | tf_op jit(solution)/shard_map/slope0/pallas_call | solution.py:604
  49.0 0.0 collective-permute-done.2.refs_2_
  49.0 0.0 collective-permute-done.3.refs_1_
  49.0 0.2 ghost_embed.1
  49.2 4.4 %collective-permute-start.4 = (f32[32,256]{1,0:T(8,128)S(1)}, f32[32,256]{1,0:T(8,128)S(1)}, u32[]{:S(2)}, u32[]{:S(2)}) collective-permute-start(f32[32,256]{1,0:T(8,128)S(1)} %get-tuple-element.76), channel_id=1, source_target_pairs={{0,7},{1,2},{2,1},{3,4},{4,3},{5,6},{6,5},{7,0},{8,15},{9,10},{10,... | collective-permute-start | bytes 98312 | tf_op jit(solution)/shard_map/ppermute | solution.py:631
  53.7 2.4 %collective-permute-start.5 = (f32[32,256]{1,0:T(8,128)S(1)}, f32[32,256]{1,0:T(8,128)S(1)}, u32[]{:S(2)}, u32[]{:S(2)}) collective-permute-start(f32[32,256]{1,0:T(8,128)S(1)} %get-tuple-element.77), channel_id=1, source_target_pairs={{0,1},{1,0},{2,3},{3,2},{4,5},{5,4},{6,7},{7,6},{8,9},{9,8},{10,11... | collective-permute-start | bytes 98312 | tf_op jit(solution)/shard_map/ppermute | solution.py:632
  56.0 1.7 %first.1.refs_6_ = f32[32,64,512]{2,1,0:T(8,128)S(1)} custom-call(bf16[32,128,512]{2,1,0:T(8,128)(2,1)S(1)} %get-tuple-element.80.refs_0_, bf16[128,128]{1,0:T(8,128)(2,1)S(1)} %get-tuple-element.81.refs_1_, f32[64,8]{1,0:T(8,128)S(1)} %get-tuple-element.82.refs_2_.refs_10_), custom_call_target="tpu_custom_call" | custom-call | tf_op jit(solution)/shard_map/first/pallas_call | solution.py:604
  57.7 0.0 collective-permute-done.4.refs_4_
  57.7 2.1 %collective-permute-done.5.refs_3_ = f32[32,256]{1,0:T(8,128)S(1)} collective-permute-done((f32[32,256]{1,0:T(8,128)S(1)}, f32[32,256]{1,0:T(8,128)S(1)}, u32[]{:S(2)}, u32[]{:S(2)}) %collective-permute-start.5) | collective-permute-done | bytes 32800 | tf_op jit(solution)/shard_map/ppermute | solution.py:632
  59.8 9.9 %pair.1 = (bf16[32,128,512]{2,1,0:T(8,128)(2,1)S(1)}, f32[32,512]{1,0:T(8,128)S(1)}, f32[32,768]{1,0:T(8,128)S(1)}, f32[32,192]{1,0:T(8,128)S(1)}, f32[32,192]{1,0:T(8,128)S(1)}) custom-call(f32[32,512]{1,0:T(8,128)S(1)} %get-tuple-element.66.refs_0_, f32[32,128]{1,0:T(8,128)S(1)} %collective-permute-done.3.refs_1_, ...), custom_call_target="tpu_custom_call" | custom-call | tf_op jit(solution)/shard_map/pair/pallas_call | solution.py:604
  69.8 4.5 %collective-permute-start.6 = (f32[32,192]{1,0:T(8,128)S(1)}, f32[32,192]{1,0:T(8,128)S(1)}, u32[]{:S(2)}, u32[]{:S(2)}) collective-permute-start(f32[32,192]{1,0:T(8,128)S(1)} %get-tuple-element.86), channel_id=1, source_target_pairs={{0,7},{1,2},{2,1},{3,4},{4,3},{5,6},{6,5},{7,0},{8,15},{9,10},{10,... | collective-permute-start | bytes 73736 | tf_op jit(solution)/shard_map/ppermute | solution.py:631
  74.2 2.3 %collective-permute-start.7 = (f32[32,192]{1,0:T(8,128)S(1)}, f32[32,192]{1,0:T(8,128)S(1)}, u32[]{:S(2)}, u32[]{:S(2)}) collective-permute-start(f32[32,192]{1,0:T(8,128)S(1)} %get-tuple-element.87), channel_id=1, source_target_pairs={{0,1},{1,0},{2,3},{3,2},{4,5},{5,4},{6,7},{7,6},{8,9},{9,8},{10,11... | collective-permute-start | bytes 73736 | tf_op jit(solution)/shard_map/ppermute | solution.py:632
  76.5 1.5 %slope1.1.refs_3_.refs_6_ = f32[32,64,256]{2,1,0:T(8,128)S(1)} custom-call(f32[32,512]{1,0:T(8,128)S(1)} %get-tuple-element.71.refs_0_, f32[4,32,512]{2,1,0:T(8,128)S(1)} %get-tuple-element.72.refs_1_.refs_7_.refs_8_, bf16[64,32]{1,0:T(8,128)(2,1)S(1)} %get-tuple-element.64.refs_3_.refs_2_), custom_call_target="tpu_custom_call" | custom-call | tf_op jit(solution)/shard_map/slope1/pallas_call | solution.py:604
  78.0 2.4 %collective-permute-done.7.refs_1_ = f32[32,192]{1,0:T(8,128)S(1)} collective-permute-done((f32[32,192]{1,0:T(8,128)S(1)}, f32[32,192]{1,0:T(8,128)S(1)}, u32[]{:S(2)}, u32[]{:S(2)}) %collective-permute-start.7) | collective-permute-done | bytes 24608 | tf_op jit(solution)/shard_map/ppermute | solution.py:632
  80.4 0.8 fold_embed.1
  81.2 3.2 %collective-permute-start.8 = (f32[32,128]{1,0:T(8,128)S(1)}, f32[32,128]{1,0:T(8,128)S(1)}, u32[]{:S(2)}, u32[]{:S(2)}) collective-permute-start(f32[32,128]{1,0:T(8,128)S(1)} %get-tuple-element.93), channel_id=1, source_target_pairs={{0,504},{8,16},{16,8},{24,32},{32,24},{40,48},{48,40},{56,64},{64,... | collective-permute-start | bytes 49160 | tf_op jit(solution)/shard_map/ppermute | solution.py:631
  84.4 3.7 %collective-permute-start.9 = (f32[32,128]{1,0:T(8,128)S(1)}, f32[32,128]{1,0:T(8,128)S(1)}, u32[]{:S(2)}, u32[]{:S(2)}) collective-permute-start(f32[32,128]{1,0:T(8,128)S(1)} %get-tuple-element.94), channel_id=1, source_target_pairs={{0,8},{8,0},{16,24},{24,16},{32,40},{40,32},{48,56},{56,48},{64,72... | collective-permute-start | bytes 49160 | tf_op jit(solution)/shard_map/ppermute | solution.py:632
  88.1 1.7 %rise.1.refs_7_ = f32[32,512]{1,0:T(8,128)S(1)} custom-call(bf16[32,128,512]{2,1,0:T(8,128)(2,1)S(1)} %get-tuple-element.101.refs_0_, f32[32,512]{1,0:T(8,128)S(1)} %get-tuple-element.102.refs_1_, f32[32,64,256]{2,1,0:T(8,128)S(1)} %slope0.1.refs_2_.refs_5_, f32[32,64,256]{2,1,0:T(8,128)S(1)} %slope1.1.refs_3_.refs_6_, ...), custom_call_target="tpu_custom_call" | custom-call | tf_op jit(solution)/shard_map/rise/pallas_call | solution.py:604
  89.8 0.0 collective-permute-done.8.refs_2_
  89.9 4.3 %force.1 = (f32[8,768]{1,0:T(8,128)S(1)}, f32[8,192]{1,0:T(8,128)S(1)}, f32[8,192]{1,0:T(8,128)S(1)}) custom-call(f32[32,512]{1,0:T(8,128)S(1)} %get-tuple-element.92.refs_0_, f32[32,128]{1,0:T(8,128)S(1)} %collective-permute-done.9.refs_1_, f32[32,128]{1,0:T(8,128)S(1)} %collective-permute-done.8.refs_2_, s32[2,128]{1,0:T(2,128)S(1)} %get-tuple-element.97.refs_3_, ...), custom_call_target="tpu_custom_call" | custom-call | tf_op jit(solution)/shard_map/force/pallas_call | solution.py:604
  94.2 4.4 %collective-permute-start.10 = (f32[8,192]{1,0:T(8,128)S(1)}, f32[8,192]{1,0:T(8,128)S(1)}, u32[]{:S(2)}, u32[]{:S(2)}) collective-permute-start(f32[8,192]{1,0:T(8,128)S(1)} %get-tuple-element.105), channel_id=1, source_target_pairs={{0,7},{1,2},{2,1},{3,4},{4,3},{5,6},{6,5},{7,0},{8,15},{9,10},{10,... | collective-permute-start | bytes 18440 | tf_op jit(solution)/shard_map/ppermute | solution.py:631
  98.6 1.9 %collective-permute-start.11 = (f32[8,192]{1,0:T(8,128)S(1)}, f32[8,192]{1,0:T(8,128)S(1)}, u32[]{:S(2)}, u32[]{:S(2)}) collective-permute-start(f32[8,192]{1,0:T(8,128)S(1)} %get-tuple-element.106), channel_id=1, source_target_pairs={{0,1},{1,0},{2,3},{3,2},{4,5},{5,4},{6,7},{7,6},{8,9},{9,8},{10,11... | collective-permute-start | bytes 18440 | tf_op jit(solution)/shard_map/ppermute | solution.py:632
  100.5 1.7 %collective-permute-done.10.refs_2_ = f32[8,192]{1,0:T(8,128)S(1)} collective-permute-done((f32[8,192]{1,0:T(8,128)S(1)}, f32[8,192]{1,0:T(8,128)S(1)}, u32[]{:S(2)}, u32[]{:S(2)}) %collective-permute-start.10) | collective-permute-done | bytes 6176 | tf_op jit(solution)/shard_map/ppermute | solution.py:631
  102.2 2.3 %collective-permute-done.11.refs_1_ = f32[8,192]{1,0:T(8,128)S(1)} collective-permute-done((f32[8,192]{1,0:T(8,128)S(1)}, f32[8,192]{1,0:T(8,128)S(1)}, u32[]{:S(2)}, u32[]{:S(2)}) %collective-permute-start.11) | collective-permute-done | bytes 6176 | tf_op jit(solution)/shard_map/ppermute | solution.py:632
  104.5 0.7 fold_force.1
  105.2 1.9 %collective-permute-start.12 = (f32[8,128]{1,0:T(8,128)S(1)}, f32[8,128]{1,0:T(8,128)S(1)}, u32[]{:S(2)}, u32[]{:S(2)}) collective-permute-start(f32[8,128]{1,0:T(8,128)S(1)} %get-tuple-element.110), channel_id=1, source_target_pairs={{0,504},{8,16},{16,8},{24,32},{32,24},{40,48},{48,40},{56,64},{64,... | collective-permute-start | bytes 12296 | tf_op jit(solution)/shard_map/ppermute | solution.py:631
  107.2 5.1 %collective-permute-start.13 = (f32[8,128]{1,0:T(8,128)S(1)}, f32[8,128]{1,0:T(8,128)S(1)}, u32[]{:S(2)}, u32[]{:S(2)}) collective-permute-start(f32[8,128]{1,0:T(8,128)S(1)} %get-tuple-element.111), channel_id=1, source_target_pairs={{0,8},{8,0},{16,24},{24,16},{32,40},{40,32},{48,56},{56,48},{64,72... | collective-permute-start | bytes 12296 | tf_op jit(solution)/shard_map/ppermute | solution.py:632
  112.3 0.8 collective-permute-done.13.refs_1_
  113.1 0.9 final.1
  (9 shorter events, 0.0 us)
Async XLA Ops:
  2.2 9.8 %collective-permute-start = (f32[8,128]{1,0:T(8,128)}, f32[8,128]{1,0:T(8,128)S(1)}, u32[]{:S(2)}, u32[]{:S(2)}) collective-permute-start(f32[8,128]{1,0:T(8,128)} %get-tuple-element.60), channel_id=1, source_target_pairs={{0,8},{8,0},{16,24},{24,16},{32,40},{40,32},{48,56},{56,48},{64,72... | collective-permute-start | bytes 12296 | tf_op jit(solution)/shard_map/ppermute | solution.py:662
  12.0 5.1 %collective-permute-start.1 = (f32[8,640]{1,0:T(8,128)S(1)}, f32[8,640]{1,0:T(8,128)S(1)}, u32[]{:S(2)}, u32[]{:S(2)}) collective-permute-start(f32[8,640]{1,0:T(8,128)S(1)} %constant_dynamic-update-slice_fusion.refs_0_), channel_id=1, source_target_pairs={{0,504},{8,16},{16,8},{24,32},{32,24},{40,48},{48,40},{56,64},{64,... | collective-permute-start | bytes 61448 | tf_op jit(solution)/shard_map/ppermute | solution.py:664
  18.2 18.2 %all-to-all-start = ((f32[16,8,512]{2,1,0:T(8,128)}), f32[16,8,512]{2,1,0:T(8,128)S(1)}, u32[]{:S(2)}, u32[]{:S(2)}) async-start(f32[16,8,512]{2,1,0:T(8,128)} %get-tuple-element.61), calls=%async_computation | async-start | bytes 524288 | tf_op jit(solution)/shard_map/all_to_all | solution.py:668
  29.0 0.8 copy-start
  29.8 0.8 copy-start.1
  30.6 0.7 copy-start.2
  31.3 0.7 copy-start.3
  32.0 0.7 copy-start.4
  40.3 8.7 %collective-permute-start.2 = (f32[32,128]{1,0:T(8,128)S(1)}, f32[32,128]{1,0:T(8,128)S(1)}, u32[]{:S(2)}, u32[]{:S(2)}) collective-permute-start(f32[32,128]{1,0:T(8,128)S(1)} %get-tuple-element.67), channel_id=1, source_target_pairs={{0,504},{8,16},{16,8},{24,32},{32,24},{40,48},{48,40},{56,64},{64,... | collective-permute-start | bytes 49160 | tf_op jit(solution)/shard_map/ppermute | solution.py:631
  42.3 6.7 %collective-permute-start.3 = (f32[32,128]{1,0:T(8,128)S(1)}, f32[32,128]{1,0:T(8,128)S(1)}, u32[]{:S(2)}, u32[]{:S(2)}) collective-permute-start(f32[32,128]{1,0:T(8,128)S(1)} %get-tuple-element.68), channel_id=1, source_target_pairs={{0,8},{8,0},{16,24},{24,16},{32,40},{40,32},{48,56},{56,48},{64,72... | collective-permute-start | bytes 49160 | tf_op jit(solution)/shard_map/ppermute | solution.py:632
  49.2 8.5 %collective-permute-start.4 = (f32[32,256]{1,0:T(8,128)S(1)}, f32[32,256]{1,0:T(8,128)S(1)}, u32[]{:S(2)}, u32[]{:S(2)}) collective-permute-start(f32[32,256]{1,0:T(8,128)S(1)} %get-tuple-element.76), channel_id=1, source_target_pairs={{0,7},{1,2},{2,1},{3,4},{4,3},{5,6},{6,5},{7,0},{8,15},{9,10},{10,... | collective-permute-start | bytes 98312 | tf_op jit(solution)/shard_map/ppermute | solution.py:631
  53.7 6.2 %collective-permute-start.5 = (f32[32,256]{1,0:T(8,128)S(1)}, f32[32,256]{1,0:T(8,128)S(1)}, u32[]{:S(2)}, u32[]{:S(2)}) collective-permute-start(f32[32,256]{1,0:T(8,128)S(1)} %get-tuple-element.77), channel_id=1, source_target_pairs={{0,1},{1,0},{2,3},{3,2},{4,5},{5,4},{6,7},{7,6},{8,9},{9,8},{10,11... | collective-permute-start | bytes 98312 | tf_op jit(solution)/shard_map/ppermute | solution.py:632
  69.8 8.3 %collective-permute-start.6 = (f32[32,192]{1,0:T(8,128)S(1)}, f32[32,192]{1,0:T(8,128)S(1)}, u32[]{:S(2)}, u32[]{:S(2)}) collective-permute-start(f32[32,192]{1,0:T(8,128)S(1)} %get-tuple-element.86), channel_id=1, source_target_pairs={{0,7},{1,2},{2,1},{3,4},{4,3},{5,6},{6,5},{7,0},{8,15},{9,10},{10,... | collective-permute-start | bytes 73736 | tf_op jit(solution)/shard_map/ppermute | solution.py:631
  74.2 6.2 %collective-permute-start.7 = (f32[32,192]{1,0:T(8,128)S(1)}, f32[32,192]{1,0:T(8,128)S(1)}, u32[]{:S(2)}, u32[]{:S(2)}) collective-permute-start(f32[32,192]{1,0:T(8,128)S(1)} %get-tuple-element.87), channel_id=1, source_target_pairs={{0,1},{1,0},{2,3},{3,2},{4,5},{5,4},{6,7},{7,6},{8,9},{9,8},{10,11... | collective-permute-start | bytes 73736 | tf_op jit(solution)/shard_map/ppermute | solution.py:632
  81.2 8.7 %collective-permute-start.8 = (f32[32,128]{1,0:T(8,128)S(1)}, f32[32,128]{1,0:T(8,128)S(1)}, u32[]{:S(2)}, u32[]{:S(2)}) collective-permute-start(f32[32,128]{1,0:T(8,128)S(1)} %get-tuple-element.93), channel_id=1, source_target_pairs={{0,504},{8,16},{16,8},{24,32},{32,24},{40,48},{48,40},{56,64},{64,... | collective-permute-start | bytes 49160 | tf_op jit(solution)/shard_map/ppermute | solution.py:631
  84.4 5.5 %collective-permute-start.9 = (f32[32,128]{1,0:T(8,128)S(1)}, f32[32,128]{1,0:T(8,128)S(1)}, u32[]{:S(2)}, u32[]{:S(2)}) collective-permute-start(f32[32,128]{1,0:T(8,128)S(1)} %get-tuple-element.94), channel_id=1, source_target_pairs={{0,8},{8,0},{16,24},{24,16},{32,40},{40,32},{48,56},{56,48},{64,72... | collective-permute-start | bytes 49160 | tf_op jit(solution)/shard_map/ppermute | solution.py:632
  94.2 8.0 %collective-permute-start.10 = (f32[8,192]{1,0:T(8,128)S(1)}, f32[8,192]{1,0:T(8,128)S(1)}, u32[]{:S(2)}, u32[]{:S(2)}) collective-permute-start(f32[8,192]{1,0:T(8,128)S(1)} %get-tuple-element.105), channel_id=1, source_target_pairs={{0,7},{1,2},{2,1},{3,4},{4,3},{5,6},{6,5},{7,0},{8,15},{9,10},{10,... | collective-permute-start | bytes 18440 | tf_op jit(solution)/shard_map/ppermute | solution.py:631
  98.6 5.9 %collective-permute-start.11 = (f32[8,192]{1,0:T(8,128)S(1)}, f32[8,192]{1,0:T(8,128)S(1)}, u32[]{:S(2)}, u32[]{:S(2)}) collective-permute-start(f32[8,192]{1,0:T(8,128)S(1)} %get-tuple-element.106), channel_id=1, source_target_pairs={{0,1},{1,0},{2,3},{3,2},{4,5},{5,4},{6,7},{7,6},{8,9},{9,8},{10,11... | collective-permute-start | bytes 18440 | tf_op jit(solution)/shard_map/ppermute | solution.py:632
  105.2 7.1 %collective-permute-start.12 = (f32[8,128]{1,0:T(8,128)S(1)}, f32[8,128]{1,0:T(8,128)S(1)}, u32[]{:S(2)}, u32[]{:S(2)}) collective-permute-start(f32[8,128]{1,0:T(8,128)S(1)} %get-tuple-element.110), channel_id=1, source_target_pairs={{0,504},{8,16},{16,8},{24,32},{32,24},{40,48},{48,40},{56,64},{64,... | collective-permute-start | bytes 12296 | tf_op jit(solution)/shard_map/ppermute | solution.py:631
  107.2 6.0 %collective-permute-start.13 = (f32[8,128]{1,0:T(8,128)S(1)}, f32[8,128]{1,0:T(8,128)S(1)}, u32[]{:S(2)}, u32[]{:S(2)}) collective-permute-start(f32[8,128]{1,0:T(8,128)S(1)} %get-tuple-element.111), channel_id=1, source_target_pairs={{0,8},{8,0},{16,24},{24,16},{32,40},{40,32},{48,56},{56,48},{64,72... | collective-permute-start | bytes 12296 | tf_op jit(solution)/shard_map/ppermute | solution.py:632
